TPU v7x, 256 devices: a whole 4x4x8 slice. The times are simulated.
256 devices in a mesh: row: 16 (over y_lo, x, core), col: 16 (over z, y_hi).
Axes of the slice: x: 4, y: 4 (y_hi: 2, y_lo: 2; y = y_hi * 2 + y_lo), z: 8, core: 2. Of those that a mesh axis runs over, the one named last changes fastest.
Arguments:
- vector: float32 [8192, 8192], P('row', 'col'), may hold values from -6 to 6
- one_electron: float32 [16, 16], replicated, may hold values from -0.18 to 0.18
- links: int32 [64, 8], replicated, may hold values from 0 to 63, as said below
- counts: int32 [64], replicated, may hold values from 4 to 8, as said below
- pairs: int32 [64, 8], P('row'), may hold values from 0 to 255
- signs: int32 [64, 8, 128, 128], P('row'), may hold values from -1 to 1
Outputs:
- sigma_vector: float32 [8192, 8192], P('row', 'col')
Inputs may be any that keep to these rules, and one draw needn't show every extreme that they name: `links`: entries name string blocks; only the first counts[I] entries of block I are used. Counting used entries only, the blocks I with I // 4 = d name blocks K with K // 4 = s at most 2 times for any d and s, and some pair d, s reaches 2. Block I has counts[I] used links; every block I with I % 4 = 0 has 8.
All inputs are finite; a program needn't handle non-finite values.
Results may differ from a plain program's by a relative error of at most 0.000051.
Values sent between devices are 32-bit elements; how exact they have to be, the bound alone decides.
No kernel may reach another device: no remote copies, remote signals or barrier semaphores. Data moves between devices by JAX's collectives and lax.ppermute only.
A program may use at most 128 MiB of HBM per device.

v0:
```python
import jax
import jax.numpy as jnp
from jax import lax
from jax.sharding import PartitionSpec as P


def broadcast(value, axis, source):
    kept = jnp.where(lax.axis_index(axis) == source, value, 0).astype(value.dtype)
    return lax.psum(kept, axis)


def pair_values(pair_ids, used, integrals):
    flat_table = integrals.reshape(-1)
    onehot = pair_ids[:, :, None] == jnp.arange(flat_table.shape[0], dtype=jnp.int32)[None, None, :]
    values = jnp.sum(jnp.where(onehot, flat_table[None, None, :], 0.0), axis=2)
    in_use = jnp.arange(pair_ids.shape[1], dtype=jnp.int32)[None, :] < used[:, None]
    return jnp.where(in_use, values, 0.0)


def local(vector, one_electron, links, counts, pairs, signs):
    block_size = signs.shape[2]
    blocks_a = pairs.shape[0]
    link_max = links.shape[1]
    rows_here, cols_here = vector.shape
    row_count = lax.axis_size("row")
    col_count = lax.axis_size("col")
    row_index = lax.axis_index("row")
    col_index = lax.axis_index("col")
    spread = row_count // col_count
    blocks_b = blocks_a * spread
    local_counts_a = lax.dynamic_slice_in_dim(counts, row_index * blocks_a, blocks_a)
    replace_alpha = pair_values(pairs, local_counts_a, one_electron)[
        :, :, None, None
    ] * signs.astype(jnp.float32)
    whole_column = lax.all_gather(vector, "row", axis=0, tiled=True).reshape(
        -1, block_size, cols_here
    )
    local_links_a = lax.dynamic_slice_in_dim(links, row_index * blocks_a, blocks_a)
    fetched_alpha = whole_column[local_links_a.reshape(-1)]
    fetched_alpha = fetched_alpha.reshape(blocks_a, link_max, block_size, cols_here)
    sigma_alpha = jnp.einsum(
        "ilmk,ilkw->imw", replace_alpha, fetched_alpha, precision=lax.Precision.HIGHEST
    )
    sigma_alpha = sigma_alpha.reshape(rows_here, cols_here)
    owner = col_index * spread + 0
    table_pieces = broadcast(replace_alpha, "row", owner)
    whole_row = lax.all_gather(vector, "col", axis=1, tiled=True).reshape(rows_here, -1, block_size)
    local_links_b = lax.dynamic_slice_in_dim(links, col_index * blocks_b, blocks_b)
    fetched_beta = jnp.take(whole_row, local_links_b.reshape(-1), axis=1)
    fetched_beta = fetched_beta.reshape(rows_here, blocks_b, link_max, block_size)
    sigma_beta = jnp.einsum(
        "rjlk,jlmk->rjm", fetched_beta, table_pieces, precision=lax.Precision.HIGHEST
    )
    sigma_beta = sigma_beta.reshape(rows_here, cols_here)
    return sigma_alpha + sigma_beta


def solution(mesh):
    in_specs = (P("row", "col"), P(), P(), P(), P("row", None), P("row", None, None, None))
    out_specs = P("row", "col")
    return jax.shard_map(local, mesh=mesh, in_specs=in_specs, out_specs=out_specs, check_vma=False)
```

profile of v0, /device:TPU:1, one launch (start us, length us, event | category | flops | bytes accessed | tf_op | source)
XLA Modules:
  0.0 482.7 jit_solution(17171341943436736919)
XLA Ops:
  6.5 0.0 copy-start.1
  6.5 0.0 all-gather.5.cloned.1.call-start
  6.5 2.5 copy.24
  9.1 0.0 all-gather.5.cloned.1.call-update
  9.1 0.0 all-gather.3.cloned.1.call-start
  9.2 0.7 all-gather.3.cloned.1.call-update
  9.9 0.0 all-reduce.2.cloned.1.call-start
  9.9 0.8 broadcast_in_dim.38
  10.7 0.7 dynamic_slice.9
  11.4 0.8 select_reduce_fusion
  12.3 0.1 fusion.7
  12.3 3.2 fusion.4
  15.6 0.0 all-reduce.2.cloned.1.call-update
  15.6 0.0 copy-done.1
  15.6 0.1 constant_dynamic-slice_fusion.1
  15.7 0.1 copy.22
  15.8 0.1 reshape.113
  15.8 0.1 compare_and_fusion
  15.9 0.1 copy.23
  16.0 0.1 copy.25
  16.1 0.1 reshape.117
  16.2 222.2 %all-gather.5.cloned.1.call-done = f32[512,8192]{0,1:T(8,128)} async-done(((f32[512,512]{0,1:T(8,128)}), f32[512,8192]{0,1:T(8,128)}) %all-gather.5.cloned.1.call-update) | async-done | bytes 16777232 | tf_op jit(solution)/shard_map/all_gather | solution.py:47
  238.4 17.4 %copy.26 = f32[512,64,128]{2,0,1:T(8,128)} copy(f32[512,64,128]{0,2,1:T(8,128)} %bitcast.25) | data formatting | bytes 33554432 | tf_op jit(solution)/shard_map/reshape | solution.py:47
  255.8 76.3 %all-gather.3.cloned.1.call-done = f32[8192,512]{1,0:T(8,128)} async-done(((f32[512,512]{1,0:T(8,128)}), f32[8192,512]{1,0:T(8,128)}) %all-gather.3.cloned.1.call-update) | async-done | bytes 16777232 | tf_op jit(solution)/shard_map/all_gather | solution.py:35
  332.1 10.1 %gather_fusion = f32[32,128,512]{2,1,0:T(8,128)} fusion(f32[64,128,512]{2,1,0:T(8,128)} %bitcast.26, s32[1024]{0:T(1024)S(1)} %pad_clamp_fusion.1), kind=kCustom, calls=%fused_computation | custom fusion | bytes 16777344 | tf_op jit(solution)/shard_map/gather | solution.py:39
  342.2 0.0 copy-start
  342.2 10.3 %gather_fusion.1 = f32[32,512,128]{2,1,0:T(8,128)} fusion(f32[512,64,128]{2,0,1:T(8,128)} %copy.26, s32[1024]{0:T(1024)S(1)} %pad_clamp_fusion), kind=kCustom, calls=%fused_computation.1 | custom fusion | bytes 16777344 | tf_op jit(solution)/shard_map/jit(_take)/gather | solution.py:49
  352.5 0.0 copy-done
  352.5 7.3 %fusion.5 = f32[4,128,512,1]{2,1,3,0:T(8,128)S(1)} fusion(f32[4,8,128,512]{3,2,1,0:T(8,128)} %bitcast.23, s32[4,8,128,128]{3,2,1,0:T(8,128)S(1)} %copy-done, f32[4,8]{1,0:T(4,128)S(1)} %fusion.7), kind=kOutput, calls=%fused_computation.8 | convolution fusion | flops 3222274048 | bytes 11534464 | tf_op jit(solution)/shard_map/ilmk,ilkw->imw/dot_general | solution.py:41
  359.8 103.1 %all-reduce.2.cloned.1.call-done = f32[4,8,128,128]{3,2,1,0:T(8,128)} async-done(((f32[4,8,128,128]{3,2,1,0:T(8,128)}), f32[4,8,128,128]{3,2,1,0:T(8,128)}) %all-reduce.2.cloned.1.call-update) | async-done | bytes 2097168 | tf_op jit(solution)/shard_map/psum | solution.py:9
  462.9 11.7 %fusion = f32[4,128,512,1]{2,1,3,0:T(8,128)S(1)} fusion(f32[4,8,128,128]{3,2,1,0:T(8,128)} %all-reduce.2.cloned.1.call-done, f32[512,4,8,128]{3,0,2,1:T(8,128)} %bitcast.24, pred[4,8]{1,0:T(4,128)(4,1)S(1)} %copy.23), kind=kOutput, calls=%fused_computation.2 | convolution fusion | flops 3223322624 | bytes 11534368 | tf_op jit(solution)/shard_map/rjlk,jlmk->rjm/dot_general | solution.py:51
  474.6 0.3 copy.27
  474.9 1.2 bitcast_add_fusion
  (4 shorter events, 0.0 us)
Async XLA Ops:
  6.5 9.1 %copy-start.1 = (s32[64,8]{0,1:T(8,128)S(1)}, s32[64,8]{0,1:T(8,128)}, u32[]{:S(2)}) copy-start(s32[64,8]{0,1:T(8,128)} %param.8) | copy-start | bytes 6148
  6.5 231.9 %all-gather.5.cloned.1.call-start = ((), (), s32[]{:S(2)}) async-start(), calls=%async_computation.2 | async-start | bytes 17825792 | tf_op jit(solution)/shard_map/all_gather | solution.py:47
  9.1 323.0 %all-gather.3.cloned.1.call-start = ((), (), s32[]{:S(2)}) async-start(), calls=%async_computation | async-start | bytes 17825792 | tf_op jit(solution)/shard_map/all_gather | solution.py:35
  9.9 453.0 %all-reduce.2.cloned.1.call-start = ((), (), s32[]{:S(2)}) async-start(), calls=%async_computation.1 | async-start | bytes 4194304 | tf_op jit(solution)/shard_map/psum | solution.py:9
  342.2 10.3 %copy-start = (s32[4,8,128,128]{3,2,1,0:T(8,128)S(1)}, s32[4,8,128,128]{3,2,1,0:T(8,128)}, u32[]{:S(2)}) copy-start(s32[4,8,128,128]{3,2,1,0:T(8,128)} %param.11) | copy-start | bytes 6291460
Sparse Core Ops, SparseCore 0:
  9.9 228.4 all-gather.4
  240.3 91.7 all-gather.2
  334.7 128.0 all-reduce.1
where the time goes:
time: 483 us
  waiting for transfers between devices  402 us (83%)
  local copies, waits for them, and re-layouts  42.7 us (9%)
  matrix products  19 us (4%)
  between operations  13.2 us (3%)
  other arithmetic  5.42 us (1%)
    all_gather x1, waiting for transfers between devices, local(): lax.all_gather(vector, 'col', axis=1, tiled=True)  222 us
    psum x1, waiting for transfers between devices, broadcast(): return lax.psum(kept, axis)  103 us
    all_gather x1, waiting for transfers between devices, local(): lax.all_gather(vector, 'row', axis=0, tiled=True)  76.3 us
    reshape x1, local copies, waits for them, and re-layouts, local(): lax.all_gather(vector, 'col', axis=1, tiled=True)  17.4 us
    dot_general x1, matrix products, local(): jnp.einsum('rjlk,jlmk->rjm', fetched_beta, table_pieces, precision=lax.Pr...  11.7 us
    gather x1, local copies, waits for them, and re-layouts, local(): fetched_beta = jnp.take(whole_row, local_links_b.reshape(-1), axis=1)  10.3 us
    gather x1, local copies, waits for them, and re-layouts, local(): fetched_alpha = whole_column[local_links_a.reshape(-1)]  10.1 us
  transfers between devices with their start and end apart: 3, of which 3 were waited for; matrix products, arithmetic and copies ran while one was open for 11% of the time, Pallas kernels for 0%

commit v1 on v0

v1 whole, which is shorter than its diff:
```python
import functools

import jax
import jax.numpy as jnp
from jax import lax
from jax.experimental import pallas as pl
from jax.experimental.pallas import tpu as pltpu
from jax.sharding import Mesh, PartitionSpec as P

AXES = ("yl", "x", "c", "z", "yh")
SIZES = (2, 4, 2, 8, 2)
ROW = ("yl", "x", "c")
COL = ("z", "yh")
B = 128
VMEM_LIMIT = 56 * 1024 * 1024


def flat(yl, x, c, z, yh):
    return (((yl * 4 + x) * 2 + c) * 8 + z) * 2 + yh


def shift(value, axis, by):
    n = SIZES[AXES.index(axis)]
    return lax.ppermute(value, axis, [(i, (i + by) % n) for i in range(n)])


def scatter_pairs(dy, dx):
    pairs = []
    for z in range(8):
        ys, xs = z >> 2, z & 3
        for yh in range(2):
            for c in range(2):
                pairs.append((flat(ys, xs, c, z, yh), flat(ys ^ dy, (xs + dx) % 4, c, z, yh)))
    return pairs


def pair_values(pair_ids, used, integrals):
    flat_table = integrals.reshape(-1)
    onehot = pair_ids[:, :, None] == jnp.arange(flat_table.shape[0], dtype=jnp.int32)[None, None, :]
    values = jnp.sum(jnp.where(onehot, flat_table[None, None, :], 0.0), axis=2)
    in_use = jnp.arange(pair_ids.shape[1], dtype=jnp.int32)[None, :] < used[:, None]
    return jnp.where(in_use, values, 0.0)


def halves(value):
    high = value.astype(jnp.bfloat16)
    low = (value - high.astype(jnp.float32)).astype(jnp.bfloat16)
    return high, low


def phase_and_size(table):
    size = jnp.max(jnp.max(jnp.abs(table), axis=0, keepdims=True), axis=1, keepdims=True)
    phase = jnp.where(table > 0, 1.0, jnp.where(table < 0, -1.0, 0.0)).astype(jnp.bfloat16)
    return phase, size


def beta_kernel(place, links, columns, tables, out, left, right):
    step = pl.program_id(0)
    yh, which = place[1], place[2]
    block = (place[0] * 2 + which) * 4 + step
    rows = out.shape[0]
    for l in range(8):
        source = links[block, l]
        owner = source >> 2
        slot = step * 8 + l
        part = slot >> 2
        at = (((part >> 2) ^ place[3]) * 8 + (((part & 3) + place[4]) & 3) * 2 + which) * 4 + (slot & 3)
        phase, size = phase_and_size(tables[at])
        size = size * jnp.where((owner & 1) == yh, 1.0, 0.0)
        lanes = pl.ds(pl.multiple_of((source & 3) * B, B), B)
        high, low = halves(columns[owner >> 1, :, lanes] * size)
        left[:, 2 * l * B:(2 * l + 1) * B] = high
        left[:, (2 * l + 1) * B:(2 * l + 2) * B] = low
        right[:, 2 * l * B:(2 * l + 1) * B] = phase
        right[:, (2 * l + 1) * B:(2 * l + 2) * B] = phase
    out[...] = lax.dot_general(left[...], right[...], (((1,), (1,)), ((), ())), preferred_element_type=jnp.float32)


def beta_part(place, links, columns, tables):
    rows = columns.shape[1]
    return pl.pallas_call(
        beta_kernel,
        out_shape=jax.ShapeDtypeStruct((rows, 4 * B), jnp.float32),
        grid_spec=pltpu.PrefetchScalarGridSpec(
            num_scalar_prefetch=2,
            grid=(4,),
            in_specs=[
                pl.BlockSpec(columns.shape, lambda i, *_: (0, 0, 0), pipeline_mode=pl.Buffered(1)),
                pl.BlockSpec(tables.shape, lambda i, *_: (0, 0, 0), pipeline_mode=pl.Buffered(1)),
            ],
            out_specs=pl.BlockSpec((rows, B), lambda i, *_: (0, i)),
            scratch_shapes=[pltpu.VMEM((rows, 16 * B), jnp.bfloat16), pltpu.VMEM((B, 16 * B), jnp.bfloat16)],
        ),
        compiler_params=pltpu.CompilerParams(dimension_semantics=("arbitrary",), vmem_limit_bytes=VMEM_LIMIT),
        cost_estimate=pl.CostEstimate(flops=4 * rows * B * 16 * B * 2, bytes_accessed=columns.size * 4 + tables.size * 4, transcendentals=0),
        name="beta",
    )(place, links, columns, tables)


def alpha_kernel(place, links, mine, other, *rest):
    pieces, (out_other, out_mine, held, left, right, sems) = rest[:10], rest[10:]
    step = pl.program_id(0)
    spots = [(0, 0, 512), (3, 0, 512), (1, 0, 512), (2, 0, 256), (2, 256, 256), (4, 0, 512), (7, 0, 512), (5, 0, 512), (6, 0, 256), (6, 256, 256)]
    copies = [
        pltpu.make_async_copy(piece, held.at[slot, pl.ds(start, size), :], sems.at[i])
        for i, (piece, (slot, start, size)) in enumerate(zip(pieces, spots))
    ]

    @pl.when(step == 0)
    def _():
        for copy in copies:
            copy.start()
        for copy in copies:
            copy.wait()

    yl, x, c = place[0], place[1], place[2]

    def product(table, core, number, out):
        block = (yl * 8 + x * 2 + core) * 4 + number
        for l in range(8):
            source = links[block, l]
            chip = source >> 3
            slot = ((chip >> 2) ^ yl) * 4 + (((chip & 3) - x) & 3)
            phase, size = phase_and_size(table[number * 8 + l])
            size = size * jnp.where(((source >> 2) & 1) == c, 1.0, 0.0)
            rows = pl.ds(pl.multiple_of((source & 3) * B, B), B)
            high, low = halves(held[slot, rows, :] * size)
            right[2 * l * B:(2 * l + 1) * B, :] = high
            right[(2 * l + 1) * B:(2 * l + 2) * B, :] = low
            left[:, 2 * l * B:(2 * l + 1) * B] = phase
            left[:, (2 * l + 1) * B:(2 * l + 2) * B] = phase
        out[pl.ds(pl.multiple_of(number * B, B), B), :] = jnp.dot(left[...], right[...], preferred_element_type=jnp.float32)

    @pl.when(step < 4)
    def _():
        product(other, 1 - c, step, out_other)

    @pl.when(step >= 4)
    def _():
        product(mine, c, step - 4, out_mine)


def alpha_part(place, links, mine, other, pieces):
    whole = pl.BlockSpec((32, B, B), lambda i, *_: (0, 0, 0), pipeline_mode=pl.Buffered(1))
    result = pl.BlockSpec((4 * B, 4 * B), lambda i, *_: (0, 0))
    return pl.pallas_call(
        alpha_kernel,
        out_shape=[jax.ShapeDtypeStruct((4 * B, 4 * B), jnp.float32)] * 2,
        grid_spec=pltpu.PrefetchScalarGridSpec(
            num_scalar_prefetch=2,
            grid=(8,),
            in_specs=[whole, whole] + [pl.BlockSpec(memory_space=pl.ANY)] * 10,
            out_specs=[result, result],
            scratch_shapes=[
                pltpu.VMEM((8, 4 * B, 4 * B), jnp.float32),
                pltpu.VMEM((B, 16 * B), jnp.bfloat16),
                pltpu.VMEM((16 * B, 4 * B), jnp.bfloat16),
                pltpu.SemaphoreType.DMA((10,)),
            ],
        ),
        compiler_params=pltpu.CompilerParams(dimension_semantics=("arbitrary",), vmem_limit_bytes=VMEM_LIMIT),
        cost_estimate=pl.CostEstimate(flops=8 * 4 * B * B * 16 * B * 2, bytes_accessed=14 << 20, transcendentals=0),
        name="alpha",
    )(place, links, mine, other, *pieces)


CHUNKS = ((0, 256), (256, 256))


def local(vector, one_electron, links, counts, pairs, signs):
    yl, x, c, z, yh = (lax.axis_index(a) for a in AXES)
    row_index = (yl * 4 + x) * 2 + c

    from_left = shift(vector, "x", 1)
    from_right = shift(vector, "x", -1)
    from_y = shift(vector, "yl", 1)

    local_counts = lax.dynamic_slice_in_dim(counts, row_index * 4, 4)
    replace = (pair_values(pairs, local_counts, one_electron)[:, :, None, None] * signs.astype(jnp.float32)).reshape(32, B, B)
    replace_other = shift(replace, "c", 1)

    ys, xs = z >> 2, z & 3
    is_source = (yl == ys) & (x == xs)
    part = jnp.where(is_source, replace[:4], 0.0)
    for j in range(1, 8):
        part = part + lax.ppermute(replace[4 * j:4 * j + 4], AXES, scatter_pairs(j >> 2, j & 3))

    gathered = []
    tables = None
    for n, (start, size) in enumerate(CHUNKS):
        gathered.append(lax.all_gather(vector[start:start + size], "z", axis=0))
        if n == 0:
            tables = lax.all_gather(part, ROW, axis=0, tiled=True)

    across_top = shift(from_left[:256], "x", 1)
    across_low = shift(from_right[256:], "x", -1)
    y_left = shift(from_y, "x", 1)
    y_right = shift(from_y, "x", -1)
    y_across_top = shift(across_top, "yl", 1)
    y_across_low = shift(across_low, "yl", 1)

    alpha_place = jnp.stack([yl, x, c]).astype(jnp.int32)
    pieces = (vector, from_left, from_right, across_top, across_low, from_y, y_left, y_right, y_across_top, y_across_low)
    alpha_other, alpha_mine = alpha_part(alpha_place, links, replace, replace_other, pieces)
    alpha = alpha_mine + shift(alpha_other, "c", 1)

    theirs, ours = [], []
    for columns in gathered:
        place = jnp.stack([z, yh, 1 - yh, ys, xs]).astype(jnp.int32)
        theirs.append(shift(beta_part(place, links, columns, tables), "yh", 1))
        place = jnp.stack([z, yh, yh, ys, xs]).astype(jnp.int32)
        ours.append(beta_part(place, links, columns, tables))
    return jnp.concatenate([alpha[s:s + n] + o + t for (s, n), o, t in zip(CHUNKS, ours, theirs)], axis=0)


def solution(mesh):
    fine = Mesh(mesh.devices.reshape(SIZES), AXES)
    in_specs = (P(ROW, COL), P(), P(), P(), P(ROW, None), P(ROW, None, None, None))
    return jax.shard_map(local, mesh=fine, in_specs=in_specs, out_specs=P(ROW, COL), check_vma=False)
```

time: 483 us -> 218 us (0.45)
  waiting for transfers between devices: 402 us -> 105 us
  Pallas kernels: 0 us -> 46.5 us
  starting transfers between devices: 0.08 us -> 37.4 us
  local copies, waits for them, and re-layouts: 42.7 us -> 8.42 us
  matrix products: 19 us -> 0 us
    all_gather x2 -> x3, waiting for transfers between devices: 298 us -> 29.8 us  [the longest x2 29.8 us: local(): gathered.append(lax.all_gather(vector[start:start + size], 'z', axis=0))]
    psum x1 -> x0, waiting for transfers between devices: 103 us -> none  [broadcast(): return lax.psum(kept, axis)]
    ppermute x0 -> x20, waiting for transfers between devices: none -> 74.7 us  [the longest x13 65.8 us: shift(): return lax.ppermute(value, axis, [(i, (i + by) % n) for i in range(n)])]
    pallas_call x0 -> x5, Pallas kernels: none -> 46.5 us  [the longest x4 32.4 us: beta_part(): pl.pallas_call(beta_kernel, out_shape=jax.ShapeDtypeStruct((rows, 4 * B),...]
    ppermute x0 -> x20, starting transfers between devices: none -> 37.3 us  [the longest x13 21 us: shift(): return lax.ppermute(value, axis, [(i, (i + by) % n) for i in range(n)])]
    gather x2 -> x0, local copies, waits for them, and re-layouts: 20.4 us -> none  [the longest x1 10.3 us: local(): fetched_beta = jnp.take(whole_row, local_links_b.reshape(-1), axis=1)]
    dot_general x2 -> x0, matrix products: 19 us -> none  [the longest x1 11.7 us: local(): jnp.einsum('rjlk,jlmk->rjm', fetched_beta, table_pieces, precision=lax.Pr...]
    reshape x4 -> x0, local copies, waits for them, and re-layouts: 17.9 us -> none  [the longest x1 17.4 us: local(): lax.all_gather(vector, 'col', axis=1, tiled=True)]
  transfers between devices with their start and end apart: 3 -> 23, of which waited for: 3 -> 9; matrix products, arithmetic and copies ran while one was open for 11% -> 4% of each run, Pallas kernels for 0% -> 21%
where the time goes in v1:
time: 218 us; the launch traced here: 217 us
  waiting for transfers between devices  105 us (48%)
  Pallas kernels  46.5 us (21%)
  starting transfers between devices  37.4 us (17%)
  between operations  13.3 us (6%)
  local copies, waits for them, and re-layouts  8.42 us (4%)
  other arithmetic  6.56 us (3%)
    ppermute x13, waiting for transfers between devices, shift(): return lax.ppermute(value, axis, [(i, (i + by) % n) for i in range(n)])  65.8 us
    pallas_call x4, Pallas kernels, beta_part(): pl.pallas_call(beta_kernel, out_shape=jax.ShapeDtypeStruct((rows, 4 * B),...  32.4 us
    all_gather x2, waiting for transfers between devices, local(): gathered.append(lax.all_gather(vector[start:start + size], 'z', axis=0))  29.8 us
    ppermute x13, starting transfers between devices, shift(): return lax.ppermute(value, axis, [(i, (i + by) % n) for i in range(n)])  21 us
    ppermute x7, starting transfers between devices, local(): lax.ppermute(replace[4 * j:4 * j + 4], AXES, scatter_pairs(j >> 2, j & 3))  16.3 us
    pallas_call x1, Pallas kernels, alpha_part(): pl.pallas_call(alpha_kernel, out_shape=[jax.ShapeDtypeStruct((4 * B, 4 *...  14.1 us
    ppermute x7, waiting for transfers between devices, local(): lax.ppermute(replace[4 * j:4 * j + 4], AXES, scatter_pairs(j >> 2, j & 3))  8.96 us
  transfers between devices with their start and end apart: 23, of which 9 were waited for; matrix products, arithmetic and copies ran while one was open for 4% of the time, Pallas kernels for 21%

profile of v1, /device:TPU:1, one launch (start us, length us, event | category | flops | bytes accessed | tf_op | source)
XLA Modules:
  0.0 217.4 jit_solution(8054741464276750074)
XLA Ops:
  6.5 2.3 %fusion.11 = (f32[256,512]{1,0:T(8,128)}, f32[256,512]{1,0:T(8,128)}) fusion(f32[512,512]{1,0:T(8,128)} %rest_0_.1), kind=kLoop, calls=%fused_computation.20 | loop fusion | bytes 2097152 | tf_op jit(solution)/shard_map/slice | solution.py:191
  9.1 0.2 select_reduce_fusion
  9.3 1.8 convert_multiply_fusion
  11.2 1.2 fusion.10
  12.3 4.1 %collective-permute-start.11 = (f32[4,128,128]{2,1,0:T(8,128)S(1)}, f32[4,128,128]{2,1,0:T(8,128)S(1)}, u32[]{:S(2)}, u32[]{:S(2)}) collective-permute-start(f32[4,128,128]{2,1,0:T(8,128)S(1)} %get-tuple-element.9), channel_id=1, source_target_pairs={{0,32},{16,48},{1,33},{17,49},{34,66},{50,82},{35,67},{51,83},{68,... | collective-permute-start | bytes 786440 | tf_op jit(solution)/shard_map/ppermute | solution.py:186
  16.4 2.2 %collective-permute-start.12 = (f32[4,128,128]{2,1,0:T(8,128)S(1)}, f32[4,128,128]{2,1,0:T(8,128)S(1)}, u32[]{:S(2)}, u32[]{:S(2)}) collective-permute-start(f32[4,128,128]{2,1,0:T(8,128)S(1)} %get-tuple-element.15), channel_id=1, source_target_pairs={{0,64},{16,80},{1,65},{17,81},{34,98},{50,114},{35,99},{51,115},{6... | collective-permute-start | bytes 786440 | tf_op jit(solution)/shard_map/ppermute | solution.py:186
  18.7 2.0 collective-permute-start.13
  20.7 2.0 collective-permute-start.14
  22.7 2.0 collective-permute-start.15
  24.7 2.0 collective-permute-start.16
  26.7 0.3 collective-permute-done.12
  27.0 0.7 copy-done.8
  27.7 2.0 collective-permute-start.17
  29.7 3.0 %collective-permute-done.15 = f32[4,128,128]{2,1,0:T(8,128)} collective-permute-done((f32[4,128,128]{2,1,0:T(8,128)}, f32[4,128,128]{2,1,0:T(8,128)}, u32[]{:S(2)}, u32[]{:S(2)}) %collective-permute-start.15) | collective-permute-done | bytes 262176 | tf_op jit(solution)/shard_map/ppermute | solution.py:186
  32.7 5.7 %collective-permute-done.16 = f32[4,128,128]{2,1,0:T(8,128)} collective-permute-done((f32[4,128,128]{2,1,0:T(8,128)}, f32[4,128,128]{2,1,0:T(8,128)}, u32[]{:S(2)}, u32[]{:S(2)}) %collective-permute-start.16) | collective-permute-done | bytes 262176 | tf_op jit(solution)/shard_map/ppermute | solution.py:186
  38.4 2.3 %fusion.8 = f32[4,128,128]{2,1,0:T(8,128)} fusion(f32[4,128,128]{2,1,0:T(8,128)} %collective-permute-done.17, f32[4,128,128]{2,1,0:T(8,128)} %collective-permute-done.16, f32[4,128,128]{2,1,0:T(8,128)} %collective-permute-done.15, f32[4,128,128]{2,1,0:T(8,128)} %collective-permute-done.14, f32[4,128,128]{2,1,0:T(8,128)} %collective-permute-done.13, ...), kind=kLoop, calls=%fused_computation.13 | loop fusion | flops 524288 | bytes 2359297 | tf_op jit(solution)/shard_map/add | solution.py:186
  40.7 0.7 all-gather.8.cloned.1.call-update
  41.4 0.1 collective-permute-start.1
  41.5 2.7 %collective-permute-start.2 = (f32[512,512]{1,0:T(8,128)S(1)}, f32[512,512]{1,0:T(8,128)S(1)}, u32[]{:S(2)}, u32[]{:S(2)}) collective-permute-start(f32[512,512]{1,0:T(8,128)S(1)} %copy-done.1), channel_id=1, source_target_pairs={{0,96},{32,0},{64,32},{96,64},{1,97},{33,1},{65,33},{97,65},{2,98}... | collective-permute-start | bytes 3145736 | tf_op jit(solution)/shard_map/ppermute | solution.py:24
  44.2 2.1 collective-permute-start
  46.2 19.7 %collective-permute-done.1.rest_1_ = f32[512,512]{1,0:T(8,128)S(1)} collective-permute-done((f32[512,512]{1,0:T(8,128)S(1)}, f32[512,512]{1,0:T(8,128)S(1)}, u32[]{:S(2)}, u32[]{:S(2)}) %collective-permute-start.1) | collective-permute-done | bytes 1048608 | tf_op jit(solution)/shard_map/ppermute | solution.py:24
  66.0 0.1 collective-permute-start.3
  66.1 2.7 %collective-permute-start.4 = (f32[256,512]{1,0:T(8,128)S(1)}, f32[256,512]{1,0:T(8,128)}, u32[]{:S(2)}, u32[]{:S(2)}) collective-permute-start(f32[256,512]{1,0:T(8,128)S(1)} %slice.57), channel_id=1, source_target_pairs={{0,96},{32,0},{64,32},{96,64},{1,97},{33,1},{65,33},{97,65},{2,98}... | collective-permute-start | bytes 1572872 | tf_op jit(solution)/shard_map/ppermute | solution.py:24
  68.9 2.3 %collective-permute-done.5.rest_5_ = f32[512,512]{1,0:T(8,128)} collective-permute-done((f32[512,512]{1,0:T(8,128)S(1)}, f32[512,512]{1,0:T(8,128)}, u32[]{:S(2)}, u32[]{:S(2)}) %collective-permute-start.5) | collective-permute-done | bytes 1048608 | tf_op jit(solution)/shard_map/ppermute | solution.py:24
  71.1 0.3 collective-permute-start.6
  71.5 2.3 %collective-permute-start.7 = (f32[512,512]{1,0:T(8,128)}, f32[512,512]{1,0:T(8,128)}, u32[]{:S(2)}, u32[]{:S(2)}) collective-permute-start(f32[512,512]{1,0:T(8,128)} %collective-permute-done.5.rest_5_), channel_id=1, source_target_pairs={{0,96},{32,0},{64,32},{96,64},{1,97},{33,1},{65,33},{97,65},{2,98}... | collective-permute-start | bytes 3145736 | tf_op jit(solution)/shard_map/ppermute | solution.py:24
  73.8 4.6 %collective-permute-done.3.rest_3_ = f32[256,512]{1,0:T(8,128)} collective-permute-done((f32[256,512]{1,0:T(8,128)S(1)}, f32[256,512]{1,0:T(8,128)}, u32[]{:S(2)}, u32[]{:S(2)}) %collective-permute-start.3) | collective-permute-done | bytes 524320 | tf_op jit(solution)/shard_map/ppermute | solution.py:24
  78.4 0.5 collective-permute-start.8
  79.0 1.0 collective-permute-start.9
  79.9 0.7 copy.17.links
  80.6 0.6 pad_add_fusion.place
  81.3 16.9 %collective-permute-done.8.rest_8_ = f32[256,512]{1,0:T(8,128)} collective-permute-done((f32[256,512]{1,0:T(8,128)}, f32[256,512]{1,0:T(8,128)}, u32[]{:S(2)}, u32[]{:S(2)}) %collective-permute-start.8) | collective-permute-done | bytes 524320 | tf_op jit(solution)/shard_map/ppermute | solution.py:24
  98.2 22.2 %collective-permute-done.9.rest_9_ = f32[256,512]{1,0:T(8,128)} collective-permute-done((f32[256,512]{1,0:T(8,128)}, f32[256,512]{1,0:T(8,128)}, u32[]{:S(2)}, u32[]{:S(2)}) %collective-permute-start.9) | collective-permute-done | bytes 524320 | tf_op jit(solution)/shard_map/ppermute | solution.py:24
  120.4 1.0 copy-done.6
  121.4 14.1 %alpha.1 = (f32[512,512]{1,0:T(8,128)}, f32[512,512]{1,0:T(8,128)}) custom-call(s32[3]{0:T(128)} %pad_add_fusion.place, s32[64,8]{1,0:T(8,128)} %copy.17.links, f32[32,128,128]{2,1,0:T(8,128)} %bitcast.14, f32[32,128,128]{2,1,0:T(8,128)} %collective-permute-done.other, f32[512,512]{1,0:T(8,128)} %rest_0_.1, f32[512,512]{1,0:T(8,128)} %copy-done.2, ...), custom_call_target="tpu_custom_call" | custom-call | flops 2147483648 | bytes 14680064 | tf_op jit(solution)/shard_map/alpha/pallas_call | solution.py:146
  135.5 3.7 %collective-permute-start.10 = (f32[512,512]{1,0:T(8,128)}, f32[512,512]{1,0:T(8,128)S(1)}, u32[]{:S(2)}, u32[]{:S(2)}) collective-permute-start(f32[512,512]{1,0:T(8,128)} %get-tuple-element.8), channel_id=1, source_target_pairs={{0,16},{16,0},{1,17},{17,1},{2,18},{18,2},{3,19},{19,3},{4,20},{20... | collective-permute-start | bytes 3145736 | tf_op jit(solution)/shard_map/ppermute | solution.py:24
  139.2 0.7 stack.60.place
  139.9 8.1 %beta.7 = f32[256,512]{1,0:T(8,128)} custom-call(s32[5]{0:T(128)} %stack.60.place, s32[64,8]{1,0:T(8,128)} %copy.17.links, f32[8,256,512]{2,1,0:T(8,128)} %bitcast.15, f32[64,128,128]{2,1,0:T(8,128)} %all-gather.6.cloned.1.call-done.tables), custom_call_target="tpu_custom_call" | custom-call | flops 536870912 | bytes 8388608 | tf_op jit(solution)/shard_map/beta/pallas_call | solution.py:81
  148.0 2.8 %collective-permute-start.19 = (f32[256,512]{1,0:T(8,128)}, f32[256,512]{1,0:T(8,128)S(1)}, u32[]{:S(2)}, u32[]{:S(2)}) collective-permute-start(f32[256,512]{1,0:T(8,128)} %beta.7), channel_id=1, source_target_pairs={{0,1},{1,0},{2,3},{3,2},{4,5},{5,4},{6,7},{7,6},{8,9},{9,8},{10,11... | collective-permute-start | bytes 1572872 | tf_op jit(solution)/shard_map/ppermute | solution.py:24
  150.8 29.8 %all-gather.8.cloned.1.call-done = f32[2048,512]{1,0:T(8,128)} async-done(((f32[256,512]{1,0:T(8,128)}), f32[2048,512]{1,0:T(8,128)}) %all-gather.8.cloned.1.call-update) | async-done | bytes 4194320 | tf_op jit(solution)/shard_map/all_gather | solution.py:191
  180.6 8.2 %beta.5 = f32[256,512]{1,0:T(8,128)} custom-call(s32[5]{0:T(128)} %stack.60.place, s32[64,8]{1,0:T(8,128)} %copy.17.links, f32[8,256,512]{2,1,0:T(8,128)} %bitcast.17, f32[64,128,128]{2,1,0:T(8,128)} %all-gather.6.cloned.1.call-done.tables), custom_call_target="tpu_custom_call" | custom-call | flops 536870912 | bytes 8388608 | tf_op jit(solution)/shard_map/beta/pallas_call | solution.py:81
  188.7 2.7 %collective-permute-start.18 = (f32[256,512]{1,0:T(8,128)}, f32[256,512]{1,0:T(8,128)S(1)}, u32[]{:S(2)}, u32[]{:S(2)}) collective-permute-start(f32[256,512]{1,0:T(8,128)} %beta.5), channel_id=1, source_target_pairs={{0,1},{1,0},{2,3},{3,2},{4,5},{5,4},{6,7},{7,6},{8,9},{9,8},{10,11... | collective-permute-start | bytes 1572872 | tf_op jit(solution)/shard_map/ppermute | solution.py:24
  191.4 0.7 stack.58.place
  192.1 0.2 add.48
  192.3 8.0 %beta.6 = f32[256,512]{1,0:T(8,128)} custom-call(s32[5]{0:T(128)} %stack.58.place, s32[64,8]{1,0:T(8,128)} %copy.17.links, f32[8,256,512]{2,1,0:T(8,128)} %bitcast.16, f32[64,128,128]{2,1,0:T(8,128)} %all-gather.6.cloned.1.call-done.tables), custom_call_target="tpu_custom_call" | custom-call | flops 536870912 | bytes 8388608 | tf_op jit(solution)/shard_map/beta/pallas_call | solution.py:81
  200.3 8.2 %beta.4 = f32[256,512]{1,0:T(8,128)} custom-call(s32[5]{0:T(128)} %stack.58.place, s32[64,8]{1,0:T(8,128)} %copy.17.links, f32[8,256,512]{2,1,0:T(8,128)} %bitcast.18, f32[64,128,128]{2,1,0:T(8,128)} %all-gather.6.cloned.1.call-done.tables), custom_call_target="tpu_custom_call" | custom-call | flops 536870912 | bytes 8388608 | tf_op jit(solution)/shard_map/beta/pallas_call | solution.py:81
  208.5 1.4 fusion.1
  209.9 1.0 copy-done.13
  (53 shorter events, 0.5 us)
Async XLA Ops:
  6.5 2.4 %copy-start.9 = (f32[16,16]{1,0:T(8,128)S(1)}, f32[16,16]{1,0:T(8,128)}, u32[]{:S(2)}) copy-start(f32[16,16]{1,0:T(8,128)} %param.7) | copy-start | bytes 3076
  6.5 2.5 %copy-start.14 = (s32[64]{0:T(128)S(1)}, s32[64]{0:T(128)}, u32[]{:S(2)}) copy-start(s32[64]{0:T(128)} %param.9) | copy-start | bytes 772
  6.5 2.5 %copy-start.11 = (s32[4,8]{1,0:T(4,128)S(1)}, s32[4,8]{1,0:T(4,128)}, u32[]{:S(2)}) copy-start(s32[4,8]{1,0:T(4,128)} %param.10) | copy-start | bytes 388
  6.5 133.4 %all-gather.10.cloned.1.call-start = ((), (), s32[]{:S(2)}) async-start(), calls=%async_computation.2 | async-start | bytes 4718592 | tf_op jit(solution)/shard_map/all_gather | solution.py:191
  8.9 131.1 %all-gather.6.cloned.1.call-start = ((), (), s32[]{:S(2)}) async-start(), calls=%async_computation | async-start | bytes 4456448 | tf_op jit(solution)/shard_map/all_gather | solution.py:193
  11.1 33.0 %copy-start = (f32[4,8,128,128]{3,2,1,0:T(8,128)}, f32[4,8,128,128]{3,2,1,0:T(8,128)S(1)}, u32[]{:S(2)}) copy-start(f32[4,8,128,128]{3,2,1,0:T(8,128)S(1)} %convert_multiply_fusion) | copy-start | bytes 6291460
  12.3 29.1 %copy-start.1 = (f32[512,512]{1,0:T(8,128)S(1)}, f32[512,512]{1,0:T(8,128)}, u32[]{:S(2)}) copy-start(f32[512,512]{1,0:T(8,128)} %rest_0_.1) | copy-start | bytes 3145732
  12.3 12.4 %collective-permute-start.11 = (f32[4,128,128]{2,1,0:T(8,128)S(1)}, f32[4,128,128]{2,1,0:T(8,128)S(1)}, u32[]{:S(2)}, u32[]{:S(2)}) collective-permute-start(f32[4,128,128]{2,1,0:T(8,128)S(1)} %get-tuple-element.9), channel_id=1, source_target_pairs={{0,32},{16,48},{1,33},{17,49},{34,66},{50,82},{35,67},{51,83},{68,... | collective-permute-start | bytes 786440 | tf_op jit(solution)/shard_map/ppermute | solution.py:186
  16.4 10.6 %collective-permute-start.12 = (f32[4,128,128]{2,1,0:T(8,128)S(1)}, f32[4,128,128]{2,1,0:T(8,128)S(1)}, u32[]{:S(2)}, u32[]{:S(2)}) collective-permute-start(f32[4,128,128]{2,1,0:T(8,128)S(1)} %get-tuple-element.15), channel_id=1, source_target_pairs={{0,64},{16,80},{1,65},{17,81},{34,98},{50,114},{35,99},{51,115},{6... | collective-permute-start | bytes 786440 | tf_op jit(solution)/shard_map/ppermute | solution.py:186
  18.7 11.1 %collective-permute-start.13 = (f32[4,128,128]{2,1,0:T(8,128)}, f32[4,128,128]{2,1,0:T(8,128)}, u32[]{:S(2)}, u32[]{:S(2)}) collective-permute-start(f32[4,128,128]{2,1,0:T(8,128)} %get-tuple-element.14), channel_id=1, source_target_pairs={{0,96},{16,112},{1,97},{17,113},{34,2},{50,18},{35,3},{51,19},{68,... | collective-permute-start | bytes 786440 | tf_op jit(solution)/shard_map/ppermute | solution.py:186
  20.7 9.0 %collective-permute-start.14 = (f32[4,128,128]{2,1,0:T(8,128)}, f32[4,128,128]{2,1,0:T(8,128)}, u32[]{:S(2)}, u32[]{:S(2)}) collective-permute-start(f32[4,128,128]{2,1,0:T(8,128)} %get-tuple-element.13), channel_id=1, source_target_pairs={{0,128},{16,144},{1,129},{17,145},{34,162},{50,178},{35,163},{51,1... | collective-permute-start | bytes 786440 | tf_op jit(solution)/shard_map/ppermute | solution.py:186
  22.7 10.0 %collective-permute-start.15 = (f32[4,128,128]{2,1,0:T(8,128)}, f32[4,128,128]{2,1,0:T(8,128)}, u32[]{:S(2)}, u32[]{:S(2)}) collective-permute-start(f32[4,128,128]{2,1,0:T(8,128)} %get-tuple-element.12), channel_id=1, source_target_pairs={{0,160},{16,176},{1,161},{17,177},{34,194},{50,210},{35,195},{51,2... | collective-permute-start | bytes 786440 | tf_op jit(solution)/shard_map/ppermute | solution.py:186
  24.7 2.3 %copy-start.7 = (f32[4,128,128]{2,1,0:T(8,128)}, f32[4,128,128]{2,1,0:T(8,128)S(1)}, u32[]{:S(2)}) copy-start(f32[4,128,128]{2,1,0:T(8,128)S(1)} %collective-permute-done.11) | copy-start | bytes 786436
  24.7 13.7 %collective-permute-start.16 = (f32[4,128,128]{2,1,0:T(8,128)}, f32[4,128,128]{2,1,0:T(8,128)}, u32[]{:S(2)}, u32[]{:S(2)}) collective-permute-start(f32[4,128,128]{2,1,0:T(8,128)} %get-tuple-element.11), channel_id=1, source_target_pairs={{0,192},{16,208},{1,193},{17,209},{34,226},{50,242},{35,227},{51,2... | collective-permute-start | bytes 786440 | tf_op jit(solution)/shard_map/ppermute | solution.py:186
  27.0 0.7 copy-start.8
  27.7 10.7 %collective-permute-start.17 = (f32[4,128,128]{2,1,0:T(8,128)S(1)}, f32[4,128,128]{2,1,0:T(8,128)}, u32[]{:S(2)}, u32[]{:S(2)}) collective-permute-start(f32[4,128,128]{2,1,0:T(8,128)S(1)} %get-tuple-element.10), channel_id=1, source_target_pairs={{0,224},{16,240},{1,225},{17,241},{34,130},{50,146},{35,131},{51,1... | collective-permute-start | bytes 786440 | tf_op jit(solution)/shard_map/ppermute | solution.py:186
  29.7 50.2 %copy-start.10 = (s32[64,8]{0,1:T(8,128)S(1)}, s32[64,8]{0,1:T(8,128)}, u32[]{:S(2)}) copy-start(s32[64,8]{0,1:T(8,128)} %param.8) | copy-start | bytes 6148
  40.7 139.9 %all-gather.8.cloned.1.call-start = ((), (), s32[]{:S(2)}) async-start(), calls=%async_computation.1 | async-start | bytes 4718592 | tf_op jit(solution)/shard_map/all_gather | solution.py:191
  41.4 24.5 %collective-permute-start.1 = (f32[512,512]{1,0:T(8,128)S(1)}, f32[512,512]{1,0:T(8,128)S(1)}, u32[]{:S(2)}, u32[]{:S(2)}) collective-permute-start(f32[512,512]{1,0:T(8,128)S(1)} %copy-done.1), channel_id=1, source_target_pairs={{0,32},{32,64},{64,96},{96,0},{1,33},{33,65},{65,97},{97,1},{2,34}... | collective-permute-start | bytes 3145736 | tf_op jit(solution)/shard_map/ppermute | solution.py:24
  41.5 24.6 %collective-permute-start.2 = (f32[512,512]{1,0:T(8,128)S(1)}, f32[512,512]{1,0:T(8,128)S(1)}, u32[]{:S(2)}, u32[]{:S(2)}) collective-permute-start(f32[512,512]{1,0:T(8,128)S(1)} %copy-done.1), channel_id=1, source_target_pairs={{0,96},{32,0},{64,32},{96,64},{1,97},{33,1},{65,33},{97,65},{2,98}... | collective-permute-start | bytes 3145736 | tf_op jit(solution)/shard_map/ppermute | solution.py:24
  44.2 37.1 %collective-permute-start = (f32[32,128,128]{2,1,0:T(8,128)S(1)}, f32[32,128,128]{2,1,0:T(8,128)}, u32[]{:S(2)}, u32[]{:S(2)}) collective-permute-start(f32[32,128,128]{2,1,0:T(8,128)S(1)} %bitcast.13), channel_id=1, source_target_pairs={{0,16},{16,0},{1,17},{17,1},{2,18},{18,2},{3,19},{19,3},{4,20},{20... | collective-permute-start | bytes 6291464 | tf_op jit(solution)/shard_map/ppermute | solution.py:24
  46.2 24.9 %collective-permute-start.5 = (f32[512,512]{1,0:T(8,128)S(1)}, f32[512,512]{1,0:T(8,128)}, u32[]{:S(2)}, u32[]{:S(2)}) collective-permute-start(f32[512,512]{1,0:T(8,128)S(1)} %copy-done.1), channel_id=1, source_target_pairs={{0,128},{128,0},{1,129},{129,1},{2,130},{130,2},{3,131},{131,3},{4... | collective-permute-start | bytes 3145736 | tf_op jit(solution)/shard_map/ppermute | solution.py:24
  65.9 5.2 %copy-start.2 = (f32[512,512]{1,0:T(8,128)}, f32[512,512]{1,0:T(8,128)S(1)}, u32[]{:S(2)}) copy-start(f32[512,512]{1,0:T(8,128)S(1)} %collective-permute-done.1.rest_1_) | copy-start | bytes 3145732
  66.0 12.5 %collective-permute-start.3 = (f32[256,512]{1,0:T(8,128)S(1)}, f32[256,512]{1,0:T(8,128)}, u32[]{:S(2)}, u32[]{:S(2)}) collective-permute-start(f32[256,512]{1,0:T(8,128)S(1)} %slice.56), channel_id=1, source_target_pairs={{0,32},{32,64},{64,96},{96,0},{1,33},{33,65},{65,97},{97,1},{2,34}... | collective-permute-start | bytes 1572872 | tf_op jit(solution)/shard_map/ppermute | solution.py:24
  66.1 5.4 %copy-start.3 = (f32[512,512]{1,0:T(8,128)}, f32[512,512]{1,0:T(8,128)S(1)}, u32[]{:S(2)}) copy-start(f32[512,512]{1,0:T(8,128)S(1)} %collective-permute-done.2.rest_2_) | copy-start | bytes 3145732
  66.1 12.8 %collective-permute-start.4 = (f32[256,512]{1,0:T(8,128)S(1)}, f32[256,512]{1,0:T(8,128)}, u32[]{:S(2)}, u32[]{:S(2)}) collective-permute-start(f32[256,512]{1,0:T(8,128)S(1)} %slice.57), channel_id=1, source_target_pairs={{0,96},{32,0},{64,32},{96,64},{1,97},{33,1},{65,33},{97,65},{2,98}... | collective-permute-start | bytes 1572872 | tf_op jit(solution)/shard_map/ppermute | solution.py:24
  71.1 49.3 %collective-permute-start.6 = (f32[512,512]{1,0:T(8,128)}, f32[512,512]{1,0:T(8,128)S(1)}, u32[]{:S(2)}, u32[]{:S(2)}) collective-permute-start(f32[512,512]{1,0:T(8,128)} %collective-permute-done.5.rest_5_), channel_id=1, source_target_pairs={{0,32},{32,64},{64,96},{96,0},{1,33},{33,65},{65,97},{97,1},{2,34}... | collective-permute-start | bytes 3145736 | tf_op jit(solution)/shard_map/ppermute | solution.py:24
  71.5 48.9 %collective-permute-start.7 = (f32[512,512]{1,0:T(8,128)}, f32[512,512]{1,0:T(8,128)}, u32[]{:S(2)}, u32[]{:S(2)}) collective-permute-start(f32[512,512]{1,0:T(8,128)} %collective-permute-done.5.rest_5_), channel_id=1, source_target_pairs={{0,96},{32,0},{64,32},{96,64},{1,97},{33,1},{65,33},{97,65},{2,98}... | collective-permute-start | bytes 3145736 | tf_op jit(solution)/shard_map/ppermute | solution.py:24
  78.4 19.7 %collective-permute-start.8 = (f32[256,512]{1,0:T(8,128)}, f32[256,512]{1,0:T(8,128)}, u32[]{:S(2)}, u32[]{:S(2)}) collective-permute-start(f32[256,512]{1,0:T(8,128)} %collective-permute-done.3.rest_3_), channel_id=1, source_target_pairs={{0,128},{128,0},{1,129},{129,1},{2,130},{130,2},{3,131},{131,3},{4... | collective-permute-start | bytes 1572872 | tf_op jit(solution)/shard_map/ppermute | solution.py:24
  79.0 41.4 %collective-permute-start.9 = (f32[256,512]{1,0:T(8,128)}, f32[256,512]{1,0:T(8,128)}, u32[]{:S(2)}, u32[]{:S(2)}) collective-permute-start(f32[256,512]{1,0:T(8,128)} %collective-permute-done.4.rest_4_), channel_id=1, source_target_pairs={{0,128},{128,0},{1,129},{129,1},{2,130},{130,2},{3,131},{131,3},{4... | collective-permute-start | bytes 1572872 | tf_op jit(solution)/shard_map/ppermute | solution.py:24
  120.4 1.0 copy-start.6
  135.5 56.6 %collective-permute-start.10 = (f32[512,512]{1,0:T(8,128)}, f32[512,512]{1,0:T(8,128)S(1)}, u32[]{:S(2)}, u32[]{:S(2)}) collective-permute-start(f32[512,512]{1,0:T(8,128)} %get-tuple-element.8), channel_id=1, source_target_pairs={{0,16},{16,0},{1,17},{17,1},{2,18},{18,2},{3,19},{19,3},{4,20},{20... | collective-permute-start | bytes 3145736 | tf_op jit(solution)/shard_map/ppermute | solution.py:24
  148.0 60.5 %collective-permute-start.19 = (f32[256,512]{1,0:T(8,128)}, f32[256,512]{1,0:T(8,128)S(1)}, u32[]{:S(2)}, u32[]{:S(2)}) collective-permute-start(f32[256,512]{1,0:T(8,128)} %beta.7), channel_id=1, source_target_pairs={{0,1},{1,0},{2,3},{3,2},{4,5},{5,4},{6,7},{7,6},{8,9},{9,8},{10,11... | collective-permute-start | bytes 1572872 | tf_op jit(solution)/shard_map/ppermute | solution.py:24
  180.6 11.5 %copy-start.5 = (f32[512,512]{1,0:T(8,128)S(1)}, f32[512,512]{1,0:T(8,128)}, u32[]{:S(2)}) copy-start(f32[512,512]{1,0:T(8,128)} %get-tuple-element.7) | copy-start | bytes 3145732
  188.7 19.8 %collective-permute-start.18 = (f32[256,512]{1,0:T(8,128)}, f32[256,512]{1,0:T(8,128)S(1)}, u32[]{:S(2)}, u32[]{:S(2)}) collective-permute-start(f32[256,512]{1,0:T(8,128)} %beta.5), channel_id=1, source_target_pairs={{0,1},{1,0},{2,3},{3,2},{4,5},{5,4},{6,7},{7,6},{8,9},{9,8},{10,11... | collective-permute-start | bytes 1572872 | tf_op jit(solution)/shard_map/ppermute | solution.py:24
  200.3 8.2 %copy-start.4 = (f32[256,512]{1,0:T(8,128)S(1)}, f32[256,512]{1,0:T(8,128)}, u32[]{:S(2)}) copy-start(f32[256,512]{1,0:T(8,128)} %beta.6) | copy-start | bytes 1572868
  200.3 8.2 %copy-start.12 = (f32[512,512]{1,0:T(8,128)S(1)}, f32[512,512]{1,0:T(8,128)}, u32[]{:S(2)}) copy-start(f32[512,512]{1,0:T(8,128)} %custom-call) | copy-start | bytes 3145732
  209.9 1.0 copy-start.13
Sparse Core Ops, SparseCore 0:
  9.2 58.6 all-gather.9
  69.7 52.5 all-gather.5
  124.1 56.4 all-gather.7

commit v2 on v0

v2 whole, which is shorter than its diff:
```python
import functools

import jax
import jax.numpy as jnp
from jax import lax
from jax.experimental import pallas as pl
from jax.experimental.pallas import tpu as pltpu
from jax.sharding import Mesh, PartitionSpec as P

AXES = ("yl", "x", "c", "z", "yh")
SIZES = (2, 4, 2, 8, 2)
ROW = ("yl", "x", "c")
COL = ("z", "yh")
B = 128
VMEM_LIMIT = 56 * 1024 * 1024


def flat(yl, x, c, z, yh):
    return (((yl * 4 + x) * 2 + c) * 8 + z) * 2 + yh


def spread(value, moves):
    pairs = []
    for z in range(8):
        ys, xs = z >> 2, z & 3
        for yh in range(2):
            for c in range(2):
                for (ay, ax), (by, bx) in moves:
                    pairs.append((flat(ys ^ ay, (xs + ax) % 4, c, z, yh), flat(ys ^ by, (xs + bx) % 4, c, z, yh)))
    return lax.ppermute(value, AXES, pairs)


def shift(value, axis, by):
    n = SIZES[AXES.index(axis)]
    return lax.ppermute(value, axis, [(i, (i + by) % n) for i in range(n)])


def halves(value):
    high = value.astype(jnp.bfloat16)
    low = (value - high.astype(jnp.float32)).astype(jnp.bfloat16)
    return high, low


def phase_and_size(table):
    size = jnp.max(jnp.max(jnp.abs(table), axis=0, keepdims=True), axis=1, keepdims=True)
    return jnp.where(table > 0, 1.0, jnp.where(table < 0, -1.0, 0.0)), size


def prepare_beta_kernel(*refs):
    tables, (phases, sizes) = refs[:-2], refs[-2:]
    for side in range(2):
        for rank in range(2 * FEW):
            phase, size = phase_and_size(tables[2 * side + rank // FEW][rank % FEW])
            phase = phase.T.astype(jnp.bfloat16)
            phases[side, rank, :B, :] = phase
            phases[side, rank, B:, :] = phase
            sizes[side, rank:rank + 1, :] = jnp.broadcast_to(size, (1, B))


def prepare_beta(*tables):
    count = 2 * FEW
    return pl.pallas_call(
        prepare_beta_kernel,
        out_shape=[jax.ShapeDtypeStruct((2, count, 2 * B, B), jnp.bfloat16), jax.ShapeDtypeStruct((2, count, B), jnp.float32)],
        compiler_params=pltpu.CompilerParams(vmem_limit_bytes=16 << 20),
        cost_estimate=pl.CostEstimate(flops=32 * B * B * 4, bytes_accessed=32 * B * B * 8, transcendentals=0),
        name="prepare_beta",
    )(*tables)


FEW = 8


def pack_kernel(place, links, counts, pairs, integrals, signs, out):
    first, is_source, yh = place[0] * 4, place[1] == 1, place[2]

    @pl.when(jnp.logical_not(is_source))
    def _():
        out[...] = jnp.zeros_like(out)

    @pl.when(is_source)
    def _():
        rank = jnp.int32(0)
        for i in range(4):
            for l in range(8):
                used = (l < counts[first + i]) & (((links[first + i, l] >> 2) & 1) == yh)

                @pl.when(used)
                def _(i=i, l=l, rank=rank):
                    pair = pairs[i, l]
                    out[jnp.minimum(rank, 2 * FEW - 1)] = signs[i, l].astype(jnp.float32) * integrals[pair >> 4, pair & 15]

                rank = rank + used.astype(jnp.int32)

        def clear(i, carry):
            out[i] = jnp.zeros((B, B), jnp.float32)
            return carry

        lax.fori_loop(rank, 2 * FEW, clear, 0)


def pack(place, links, counts, pairs, integrals, signs):
    scalar = pl.BlockSpec(memory_space=pltpu.SMEM)
    return pl.pallas_call(
        pack_kernel,
        out_shape=jax.ShapeDtypeStruct((2 * FEW, B, B), jnp.float32),
        in_specs=[scalar] * 5 + [pl.BlockSpec(memory_space=pltpu.VMEM)],
        out_specs=pl.BlockSpec(memory_space=pltpu.VMEM),
        compiler_params=pltpu.CompilerParams(vmem_limit_bytes=16 << 20),
        cost_estimate=pl.CostEstimate(flops=32 * B * B, bytes_accessed=48 * B * B * 4, transcendentals=0),
        name="pack",
    )(place, links, counts, pairs, integrals, signs)


def beta_kernel(place, links, counts, phases, sizes, *rest, spots):
    count = len(spots)
    pieces, (out, held, names, left, sems) = rest[:count], rest[count:]
    rows = out.shape[0]
    copies = [
        pltpu.make_async_copy(piece.at[pl.ds(start, size), :], held.at[slot, pl.ds(to, size), :], sems.at[i])
        for i, (piece, (slot, start, to, size)) in enumerate(zip(pieces, spots))
    ]
    for copy in copies:
        copy.start()
    z, yh, which = place[0], place[1], place[2]
    first = (z * 2 + which) * 4
    rank = jnp.int32(0)
    for r in range(2 * FEW):
        names[r] = 0
    for i in range(4):
        for l in range(8):
            source = links[first + i, l]
            used = (l < counts[first + i]) & (((source >> 2) & 1) == yh)

            @pl.when(used)
            def _(i=i, source=source, rank=rank):
                names[jnp.minimum(rank, 2 * FEW - 1)] = source * 4 + i

            rank = rank + used.astype(jnp.int32)
    out[...] = jnp.zeros_like(out)
    for copy in copies:
        copy.wait()
    for r in range(2 * FEW):
        name = names[r]
        slot = ((name >> 5) - z) & 7
        lanes = pl.ds(pl.multiple_of(((name >> 2) & 3) * B, B), B)
        target = pl.ds(pl.multiple_of((name & 3) * B, B), B)
        left[r % 2, :, :B], left[r % 2, :, B:] = halves(held[slot, :, lanes] * sizes[0, r:r + 1, :])
        out[:, target] += jnp.dot(left[r % 2], phases[0, r], preferred_element_type=jnp.float32)


def beta_part(place, links, counts, phases, sizes, rows, pieces, spots):
    return pl.pallas_call(
        functools.partial(beta_kernel, spots=spots),
        out_shape=jax.ShapeDtypeStruct((rows, 4 * B), jnp.float32),
        grid_spec=pltpu.PrefetchScalarGridSpec(
            num_scalar_prefetch=3,
            grid=(1,),
            in_specs=[
                pl.BlockSpec((1, 2 * FEW, 2 * B, B), lambda i, place, *_: (place[3], 0, 0, 0), pipeline_mode=pl.Buffered(1)),
                pl.BlockSpec((1, 2 * FEW, B), lambda i, place, *_: (place[3], 0, 0), pipeline_mode=pl.Buffered(1)),
            ] + [pl.BlockSpec(memory_space=pl.ANY)] * len(spots),
            out_specs=pl.BlockSpec((rows, 4 * B), lambda i, *_: (0, 0), pipeline_mode=pl.Buffered(1)),
            scratch_shapes=[
                pltpu.VMEM((8, rows, 4 * B), jnp.float32),
                pltpu.SMEM((2 * FEW,), jnp.int32),
                pltpu.VMEM((2, rows, 2 * B), jnp.bfloat16),
                pltpu.SemaphoreType.DMA((len(spots),)),
            ],
        ),
        compiler_params=pltpu.CompilerParams(dimension_semantics=("arbitrary",), vmem_limit_bytes=24 << 20),
        cost_estimate=pl.CostEstimate(flops=16 * rows * B * 2 * B * 2, bytes_accessed=rows * 512 * 36 + (1 << 20), transcendentals=0),
        name="beta",
    )(place, links, counts, phases, sizes, *pieces)


def alpha_kernel(place, links, counts, pairs, integrals, signs, *rest):
    tiles, (out, left, high, low) = rest[:8], rest[8:]
    step = pl.program_id(0)
    block = place[0] * 4 + step
    for l in range(8):
        pair = pairs[step, l]
        coef = jnp.where(l < counts[block], integrals[pair >> 4, pair & 15], 0.0)
        left[:, l * B:(l + 1) * B] = signs[0, l].astype(jnp.float32).astype(jnp.bfloat16)
        high[l * B:(l + 1) * B, :], low[l * B:(l + 1) * B, :] = halves(tiles[l][0] * coef)
    out[...] = jnp.dot(left[...], high[...], preferred_element_type=jnp.float32) + jnp.dot(
        left[...], low[...], preferred_element_type=jnp.float32
    )


def alpha_part(place, links, counts, pairs, integrals, signs, column):
    def tile(l):
        return pl.BlockSpec((1, B, 4 * B), lambda i, place, links, *_: (links[place[0] * 4 + i, l], 0, 0))

    return pl.pallas_call(
        alpha_kernel,
        out_shape=jax.ShapeDtypeStruct((4 * B, 4 * B), jnp.float32),
        grid_spec=pltpu.PrefetchScalarGridSpec(
            num_scalar_prefetch=5,
            grid=(4,),
            in_specs=[pl.BlockSpec((1, 8, B, B), lambda i, *_: (i, 0, 0, 0))] + [tile(l) for l in range(8)],
            out_specs=pl.BlockSpec((B, 4 * B), lambda i, *_: (i, 0)),
            scratch_shapes=[
                pltpu.VMEM((B, 8 * B), jnp.bfloat16),
                pltpu.VMEM((8 * B, 4 * B), jnp.bfloat16),
                pltpu.VMEM((8 * B, 4 * B), jnp.bfloat16),
            ],
        ),
        compiler_params=pltpu.CompilerParams(dimension_semantics=("arbitrary",), vmem_limit_bytes=VMEM_LIMIT),
        cost_estimate=pl.CostEstimate(flops=4 * 4 * B * B * 16 * B * 2, bytes_accessed=11 << 20, transcendentals=0),
        name="alpha",
    )(place, links, counts, pairs, integrals, signs, *[column] * 8)


HALF = 2 * B


def local(vector, one_electron, links, counts, pairs, signs):
    yl, x, c, z, yh = (lax.axis_index(a) for a in AXES)
    row_index = (yl * 4 + x) * 2 + c
    column = lax.all_gather(vector, ROW, axis=0, tiled=True).reshape(64, B, 4 * B)

    up, down = [vector], [vector]
    for _ in range(2):
        up.append(shift(up[-1], "z", 1))
        down.append(shift(down[-1], "z", -1))
    near = [vector, down[1], down[2], up[2], up[1]]
    chunks = []
    for n in range(2):
        rows = slice(n * HALF, (n + 1) * HALF)
        up3, down3 = shift(up[2][rows], "z", 1), shift(down[2][rows], "z", -1)
        far = [down3, shift(up3[:HALF // 2], "z", 1), shift(down3[HALF // 2:], "z", -1), up3]
        chunks.append(far)

    def near_spots(start, rows):
        return [(slot, start, 0, rows) for slot in (0, 1, 2, 6, 7)]

    def far_spots(to):
        return [(3, 0, to, HALF), (4, 0, to, HALF // 2), (4, 0, to + HALF // 2, HALF // 2), (5, 0, to, HALF)]

    is_source = (yl == z >> 2) & (x == z & 3)
    packed = pack(jnp.stack([row_index, is_source.astype(jnp.int32), yh]), links, counts, pairs, one_electron, signs)
    first, second = packed[:FEW], packed[FEW:]
    o, p, q, r = (0, 0), (0, 1), (0, 2), (0, 3)
    yo, yp, yq, yr = (1, 0), (1, 1), (1, 2), (1, 3)
    first += spread(first, [(o, yo)])
    first += spread(first, [(o, p), (yo, yp)])
    first += spread(first, [(o, r), (yo, yr), (p, q), (yp, yq)])
    second += spread(second, [(o, p)])
    second += spread(second, [(o, r), (p, q)])
    second += spread(second, [(o, yo), (p, yp), (q, yq), (r, yr)])
    phases, sizes = prepare_beta(first, second, shift(first, "c", 1), shift(second, "c", 1))

    theirs, ours = (jnp.stack([z, yh, which, (which ^ c)]).astype(jnp.int32) for which in (1 - yh, yh))
    tables = (links, counts, phases, sizes)
    partial = [
        beta_part(theirs, *tables, HALF, near + chunks[n], near_spots(n * HALF, HALF) + far_spots(0)) for n in range(2)
    ]
    sent = [shift(value, "yh", 1) for value in partial]
    ours, _ = lax.optimization_barrier((ours, partial[1]))
    kept = beta_part(ours, *tables, 2 * HALF, near + chunks[0] + chunks[1], near_spots(0, 2 * HALF) + far_spots(0) + far_spots(HALF))
    place, _ = lax.optimization_barrier((row_index[None].astype(jnp.int32), partial[1]))
    alpha = alpha_part(place, links, counts, pairs, one_electron, signs, column)
    return alpha + kept + jnp.concatenate(sent, axis=0)


def solution(mesh):
    fine = Mesh(mesh.devices.reshape(SIZES), AXES)
    in_specs = (P(ROW, COL), P(), P(), P(), P(ROW, None), P(ROW, None, None, None))
    return jax.shard_map(local, mesh=fine, in_specs=in_specs, out_specs=P(ROW, COL), check_vma=False)
```

time: 483 us -> 173 us (0.36)
  the two profiles are of different devices: /device:TPU:1 before, /device:TPU:4 now
where the time goes in v2:
time: 173 us; the launch traced here: 171 us
  waiting for transfers between devices  69.3 us (40%)
  local copies, waits for them, and re-layouts  31.1 us (18%)
  starting transfers between devices  28.7 us (17%)
  Pallas kernels  25 us (14%)
  between operations  13.8 us (8%)
  other arithmetic  3.51 us (2%)
    ppermute x6, waiting for transfers between devices, spread(): return lax.ppermute(value, AXES, pairs)  52.6 us
    unnamed x83, local copies, waits for them, and re-layouts  28 us
    ppermute x16, starting transfers between devices, shift(): return lax.ppermute(value, axis, [(i, (i + by) % n) for i in range(n)])  22.7 us
    ppermute x16, waiting for transfers between devices, shift(): return lax.ppermute(value, axis, [(i, (i + by) % n) for i in range(n)])  16 us
    pallas_call x3, Pallas kernels, beta_part(): pl.pallas_call(functools.partial(beta_kernel, spots=spots), out_shape=jax...  14.3 us
    pallas_call x1, Pallas kernels, alpha_part(): pl.pallas_call(alpha_kernel, out_shape=jax.ShapeDtypeStruct((4 * B, 4 * B...  8.77 us
    ppermute x6, starting transfers between devices, spread(): return lax.ppermute(value, AXES, pairs)  5.99 us
  transfers between devices with their start and end apart: 23, of which 4 were waited for; matrix products, arithmetic and copies ran while one was open for 3% of the time, Pallas kernels for 15%

profile of v2, /device:TPU:4, one launch (start us, length us, event | category | flops | bytes accessed | tf_op | source)
XLA Modules:
  0.0 171.4 jit_solution(6941040652999669654)
XLA Ops:
  7.3 2.0 %collective-permute-start.10 = (f32[512,512]{1,0:T(8,128)}, f32[512,512]{1,0:T(8,128)S(1)}, u32[]{:S(2)}, u32[]{:S(2)}) collective-permute-start(f32[512,512]{1,0:T(8,128)} %rest_0_.5), channel_id=1, source_target_pairs={{0,2},{2,4},{4,6},{6,8},{8,10},{10,12},{12,14},{14,0},{1,3},{3,5},... | collective-permute-start | bytes 3145736 | tf_op jit(solution)/shard_map/ppermute | solution.py:35
  9.3 4.0 %collective-permute-start.8 = (f32[512,512]{1,0:T(8,128)}, f32[512,512]{1,0:T(8,128)S(1)}, u32[]{:S(2)}, u32[]{:S(2)}) collective-permute-start(f32[512,512]{1,0:T(8,128)} %rest_0_.5), channel_id=1, source_target_pairs={{0,14},{2,0},{4,2},{6,4},{8,6},{10,8},{12,10},{14,12},{1,15},{3,1}... | collective-permute-start | bytes 3145736 | tf_op jit(solution)/shard_map/ppermute | solution.py:35
  13.3 0.8 copy.8.links
  14.1 1.6 copy-done.13
  17.8 1.3 pack.1
  20.6 16.0 %collective-permute-done.10.rest_4_ = f32[512,512]{1,0:T(8,128)S(1)} collective-permute-done((f32[512,512]{1,0:T(8,128)}, f32[512,512]{1,0:T(8,128)S(1)}, u32[]{:S(2)}, u32[]{:S(2)}) %collective-permute-start.10) | collective-permute-done | bytes 1048608 | tf_op jit(solution)/shard_map/ppermute | solution.py:35
  36.6 3.2 %collective-permute-start.9 = (f32[512,512]{1,0:T(8,128)S(1)}, f32[512,512]{1,0:T(8,128)S(1)}, u32[]{:S(2)}, u32[]{:S(2)}) collective-permute-start(f32[512,512]{1,0:T(8,128)S(1)} %collective-permute-done.8.rest_1_), channel_id=1, source_target_pairs={{0,14},{2,0},{4,2},{6,4},{8,6},{10,8},{12,10},{14,12},{1,15},{3,1}... | collective-permute-start | bytes 3145736 | tf_op jit(solution)/shard_map/ppermute | solution.py:35
  40.0 1.3 collective-permute-start.4
  42.0 30.6 %collective-permute-done.4 = f32[8,128,128]{2,1,0:T(8,128)S(1)} collective-permute-done((f32[8,128,128]{2,1,0:T(8,128)S(1)}, f32[8,128,128]{2,1,0:T(8,128)S(1)}, u32[]{:S(2)}, u32[]{:S(2)}) %collective-permute-start.4) | collective-permute-done | bytes 524320 | tf_op jit(solution)/shard_map/ppermute | solution.py:30
  72.6 1.3 collective-permute-start.5
  74.1 1.3 collective-permute-start.2
  75.6 0.7 copy-done.1
  76.4 2.6 %collective-permute-start.16 = (f32[256,512]{1,0:T(8,128)S(1)}, f32[256,512]{1,0:T(8,128)S(1)}, u32[]{:S(2)}, u32[]{:S(2)}) collective-permute-start(f32[256,512]{1,0:T(8,128)S(1)} %get-tuple-element.15), channel_id=1, source_target_pairs={{0,14},{2,0},{4,2},{6,4},{8,6},{10,8},{12,10},{14,12},{1,15},{3,1}... | collective-permute-start | bytes 1572872 | tf_op jit(solution)/shard_map/ppermute | solution.py:35
  78.9 4.4 %collective-permute-done.5 = f32[8,128,128]{2,1,0:T(8,128)S(1)} collective-permute-done((f32[8,128,128]{2,1,0:T(8,128)S(1)}, f32[8,128,128]{2,1,0:T(8,128)S(1)}, u32[]{:S(2)}, u32[]{:S(2)}) %collective-permute-start.5) | collective-permute-done | bytes 524320 | tf_op jit(solution)/shard_map/ppermute | solution.py:30
  83.4 17.6 %collective-permute-done.2 = f32[8,128,128]{2,1,0:T(8,128)S(1)} collective-permute-done((f32[8,128,128]{2,1,0:T(8,128)S(1)}, f32[8,128,128]{2,1,0:T(8,128)S(1)}, u32[]{:S(2)}, u32[]{:S(2)}) %collective-permute-start.2) | collective-permute-done | bytes 524320 | tf_op jit(solution)/shard_map/ppermute | solution.py:30
  101.7 0.7 slice.48
  102.5 0.8 copy-done.16
  103.3 0.7 slice.49
  104.0 0.8 copy-done.19
  104.8 3.2 %collective-permute-start.19 = (f32[128,512]{1,0:T(8,128)}, f32[128,512]{1,0:T(8,128)}, u32[]{:S(2)}, u32[]{:S(2)}) collective-permute-start(f32[128,512]{1,0:T(8,128)} %slice.49), channel_id=1, source_target_pairs={{0,14},{2,0},{4,2},{6,4},{8,6},{10,8},{12,10},{14,12},{1,15},{3,1}... | collective-permute-start | bytes 786440 | tf_op jit(solution)/shard_map/ppermute | solution.py:35
  108.7 0.8 copy-done.22
  109.5 0.7 slice.45
  110.2 0.8 copy-done.25
  111.1 0.8 copy-done.33
  111.8 3.2 %collective-permute-start.15 = (f32[128,512]{1,0:T(8,128)}, f32[128,512]{1,0:T(8,128)}, u32[]{:S(2)}, u32[]{:S(2)}) collective-permute-start(f32[128,512]{1,0:T(8,128)} %slice.45), channel_id=1, source_target_pairs={{0,14},{2,0},{4,2},{6,4},{8,6},{10,8},{12,10},{14,12},{1,15},{3,1}... | collective-permute-start | bytes 786440 | tf_op jit(solution)/shard_map/ppermute | solution.py:35
  115.2 0.8 copy-done.35
  116.0 1.0 copy-done.29
  117.0 1.1 copy-done.31
  118.1 1.0 copy-done.34
  119.1 1.0 copy-done.36
  120.9 1.2 copy-done.2
  122.1 1.3 copy-done.8
  123.4 1.2 copy-done.11
  124.6 4.4 %beta.5 = f32[256,512]{1,0:T(8,128)} custom-call(s32[4]{0:T(128)S(1)} %pad_add_fusion.place, s32[64,8]{1,0:T(8,128)S(1)} %copy.8.links, s32[64]{0:T(128)S(1)} %copy-done.39, bf16[2,16,256,128]{3,2,1,0:T(8,128)(2,1)S(1)} %get-tuple-element.9.phases, f32[2,16,128]{2,1,0:T(8,128)S(1)} %get-tuple-element.10.sizes, f32[512,512]{1,0:T(8,128)S(1)} %copy-done, ...), custom_call_target="tpu_custom_call" | custom-call | flops 268435456 | bytes 5767168 | tf_op jit(solution)/shard_map/beta/pallas_call | solution.py:153
  129.1 3.1 %collective-permute-start.20 = (f32[256,512]{1,0:T(8,128)}, f32[256,512]{1,0:T(8,128)}, u32[]{:S(2)}, u32[]{:S(2)}) collective-permute-start(f32[256,512]{1,0:T(8,128)} %beta.5), channel_id=1, source_target_pairs={{0,1},{1,0},{2,3},{3,2},{4,5},{5,4},{6,7},{7,6},{8,9},{9,8},{10,11... | collective-permute-start | bytes 1572872 | tf_op jit(solution)/shard_map/ppermute | solution.py:35
  132.1 4.5 %beta.3 = f32[256,512]{1,0:T(8,128)} custom-call(s32[4]{0:T(128)S(1)} %pad_add_fusion.place, s32[64,8]{1,0:T(8,128)S(1)} %copy.8.links, s32[64]{0:T(128)S(1)} %copy-done.39, bf16[2,16,256,128]{3,2,1,0:T(8,128)(2,1)S(1)} %get-tuple-element.9.phases, f32[2,16,128]{2,1,0:T(8,128)S(1)} %get-tuple-element.10.sizes, f32[512,512]{1,0:T(8,128)S(1)} %copy-done, ...), custom_call_target="tpu_custom_call" | custom-call | flops 268435456 | bytes 5767168 | tf_op jit(solution)/shard_map/beta/pallas_call | solution.py:153
  137.4 1.2 copy-done.3
  138.6 1.2 copy-done.6
  139.9 1.2 copy-done.9
  141.1 1.2 copy-done.12
  142.3 1.0 copy-done.18
  143.4 1.0 copy-done.21
  144.4 1.0 copy-done.24
  145.4 1.0 copy-done.27
  146.5 5.4 %beta.4 = f32[512,512]{1,0:T(8,128)S(1)} custom-call(s32[4]{0:T(128)S(1)} %pad_add_fusion.3.place, s32[64,8]{1,0:T(8,128)S(1)} %copy.8.links, s32[64]{0:T(128)S(1)} %copy-done.39, bf16[2,16,256,128]{3,2,1,0:T(8,128)(2,1)S(1)} %get-tuple-element.9.phases, f32[2,16,128]{2,1,0:T(8,128)S(1)} %get-tuple-element.10.sizes, f32[512,512]{1,0:T(8,128)S(1)} %copy-done, ...), custom_call_target="tpu_custom_call" | custom-call | flops 536870912 | bytes 10485760 | tf_op jit(solution)/shard_map/beta/pallas_call | solution.py:153
  151.9 1.0 copy-done.14
  152.9 8.8 %alpha.1 = f32[512,512]{1,0:T(8,128)} custom-call(s32[1]{0:T(128)} %bitcast.place, s32[64,8]{1,0:T(8,128)} %copy-done.32, s32[64]{0:T(128)} %counts.9, s32[4,8]{1,0:T(4,128)} %pairs.3, f32[16,16]{1,0:T(8,128)} %integrals.3, s32[4,8,128,128]{3,2,1,0:T(8,128)} %signs.3, f32[64,128,512]{2,1,0:T(8,128)} %bitcast.8, f32[64,128,512]{2,1,0:T(8,128)} %bitcast.9, ...), custom_call_target="tpu_custom_call" | custom-call | flops 1073741824 | bytes 11534336 | tf_op jit(solution)/shard_map/alpha/pallas_call | solution.py:195
  161.7 2.9 %maximum_add_fusion = f32[512,512]{1,0:T(8,128)} fusion(f32[256,512]{1,0:T(8,128)} %collective-permute-done.21, f32[256,512]{1,0:T(8,128)} %collective-permute-done.20, f32[512,512]{1,0:T(8,128)} %alpha.1, f32[512,512]{1,0:T(8,128)S(1)} %copy-done.15), kind=kLoop, calls=%fused_computation | loop fusion | flops 786432 | bytes 4194304 | tf_op jit(solution)/shard_map/add | solution.py:264
  (104 shorter events, 8.5 us)
Async XLA Ops:
  6.5 146.4 %all-gather.2.cloned.1.call-start = ((), (), s32[]{:S(2)}) async-start(), calls=%async_computation | async-start | bytes 17825792 | tf_op jit(solution)/shard_map/all_gather | solution.py:221
  7.3 29.3 %collective-permute-start.10 = (f32[512,512]{1,0:T(8,128)}, f32[512,512]{1,0:T(8,128)S(1)}, u32[]{:S(2)}, u32[]{:S(2)}) collective-permute-start(f32[512,512]{1,0:T(8,128)} %rest_0_.5), channel_id=1, source_target_pairs={{0,2},{2,4},{4,6},{6,8},{8,10},{10,12},{12,14},{14,0},{1,3},{3,5},... | collective-permute-start | bytes 3145736 | tf_op jit(solution)/shard_map/ppermute | solution.py:35
  9.3 27.3 %collective-permute-start.8 = (f32[512,512]{1,0:T(8,128)}, f32[512,512]{1,0:T(8,128)S(1)}, u32[]{:S(2)}, u32[]{:S(2)}) collective-permute-start(f32[512,512]{1,0:T(8,128)} %rest_0_.5), channel_id=1, source_target_pairs={{0,14},{2,0},{4,2},{6,4},{8,6},{10,8},{12,10},{14,12},{1,15},{3,1}... | collective-permute-start | bytes 3145736 | tf_op jit(solution)/shard_map/ppermute | solution.py:35
  14.1 123.4 %copy-start.32 = (s32[64,8]{1,0:T(8,128)}, s32[64,8]{1,0:T(8,128)S(1)}, u32[]{:S(2)}) copy-start(s32[64,8]{1,0:T(8,128)S(1)} %copy.8.links) | copy-start | bytes 6148
  14.1 1.6 copy-start.13
  19.2 20.6 %collective-permute-start = (f32[8,128,128]{2,1,0:T(8,128)S(1)}, f32[8,128,128]{2,1,0:T(8,128)S(1)}, u32[]{:S(2)}, u32[]{:S(2)}) collective-permute-start(f32[8,128,128]{2,1,0:T(8,128)S(1)} %get-tuple-element.20), channel_id=1, source_target_pairs={{0,128},{16,144},{1,129},{17,145},{34,162},{50,178},{35,163},{51,1... | collective-permute-start | bytes 1572872 | tf_op jit(solution)/shard_map/ppermute | solution.py:30
  19.9 19.9 %collective-permute-start.3 = (f32[8,128,128]{2,1,0:T(8,128)S(1)}, f32[8,128,128]{2,1,0:T(8,128)S(1)}, u32[]{:S(2)}, u32[]{:S(2)}) collective-permute-start(f32[8,128,128]{2,1,0:T(8,128)S(1)} %get-tuple-element.19), channel_id=1, source_target_pairs={{0,32},{16,48},{1,33},{17,49},{34,66},{50,82},{35,67},{51,83},{68,... | collective-permute-start | bytes 1572872 | tf_op jit(solution)/shard_map/ppermute | solution.py:30
  36.6 36.0 %copy-start.7 = (f32[512,512]{1,0:T(8,128)}, f32[512,512]{1,0:T(8,128)S(1)}, u32[]{:S(2)}) copy-start(f32[512,512]{1,0:T(8,128)S(1)} %collective-permute-done.10.rest_4_) | copy-start | bytes 3145732
  36.6 38.8 %collective-permute-start.11 = (f32[512,512]{1,0:T(8,128)S(1)}, f32[512,512]{1,0:T(8,128)S(1)}, u32[]{:S(2)}, u32[]{:S(2)}) collective-permute-start(f32[512,512]{1,0:T(8,128)S(1)} %collective-permute-done.10.rest_4_), channel_id=1, source_target_pairs={{0,2},{2,4},{4,6},{6,8},{8,10},{10,12},{12,14},{14,0},{1,3},{3,5},... | collective-permute-start | bytes 3145736 | tf_op jit(solution)/shard_map/ppermute | solution.py:35
  36.6 36.0 %copy-start.10 = (f32[512,512]{1,0:T(8,128)}, f32[512,512]{1,0:T(8,128)S(1)}, u32[]{:S(2)}) copy-start(f32[512,512]{1,0:T(8,128)S(1)} %collective-permute-done.8.rest_1_) | copy-start | bytes 3145732
  36.6 39.0 %collective-permute-start.9 = (f32[512,512]{1,0:T(8,128)S(1)}, f32[512,512]{1,0:T(8,128)S(1)}, u32[]{:S(2)}, u32[]{:S(2)}) collective-permute-start(f32[512,512]{1,0:T(8,128)S(1)} %collective-permute-done.8.rest_1_), channel_id=1, source_target_pairs={{0,14},{2,0},{4,2},{6,4},{8,6},{10,8},{12,10},{14,12},{1,15},{3,1}... | collective-permute-start | bytes 3145736 | tf_op jit(solution)/shard_map/ppermute | solution.py:35
  40.0 32.6 %collective-permute-start.4 = (f32[8,128,128]{2,1,0:T(8,128)S(1)}, f32[8,128,128]{2,1,0:T(8,128)S(1)}, u32[]{:S(2)}, u32[]{:S(2)}) collective-permute-start(f32[8,128,128]{2,1,0:T(8,128)S(1)} %get-tuple-element.17), channel_id=1, source_target_pairs={{0,96},{32,64},{16,112},{48,80},{1,97},{33,65},{17,113},{49,81},{3... | collective-permute-start | bytes 1572872 | tf_op jit(solution)/shard_map/ppermute | solution.py:30
  41.3 32.7 %collective-permute-start.1 = (f32[8,128,128]{2,1,0:T(8,128)S(1)}, f32[8,128,128]{2,1,0:T(8,128)S(1)}, u32[]{:S(2)}, u32[]{:S(2)}) collective-permute-start(f32[8,128,128]{2,1,0:T(8,128)S(1)} %get-tuple-element.18), channel_id=1, source_target_pairs={{0,32},{128,160},{16,48},{144,176},{1,33},{129,161},{17,49},{145,1... | collective-permute-start | bytes 1572872 | tf_op jit(solution)/shard_map/ppermute | solution.py:30
  72.6 10.7 %collective-permute-start.5 = (f32[8,128,128]{2,1,0:T(8,128)S(1)}, f32[8,128,128]{2,1,0:T(8,128)S(1)}, u32[]{:S(2)}, u32[]{:S(2)}) collective-permute-start(f32[8,128,128]{2,1,0:T(8,128)S(1)} %add.36), channel_id=1, source_target_pairs={{0,128},{32,160},{64,192},{96,224},{16,144},{48,176},{80,208},{112... | collective-permute-start | bytes 1572872 | tf_op jit(solution)/shard_map/ppermute | solution.py:30
  74.1 26.9 %collective-permute-start.2 = (f32[8,128,128]{2,1,0:T(8,128)S(1)}, f32[8,128,128]{2,1,0:T(8,128)S(1)}, u32[]{:S(2)}, u32[]{:S(2)}) collective-permute-start(f32[8,128,128]{2,1,0:T(8,128)S(1)} %add.33), channel_id=1, source_target_pairs={{0,96},{128,224},{32,64},{160,192},{16,112},{144,240},{48,80},{176... | collective-permute-start | bytes 1572872 | tf_op jit(solution)/shard_map/ppermute | solution.py:30
  75.5 25.7 %collective-permute-start.17 = (f32[256,512]{1,0:T(8,128)S(1)}, f32[256,512]{1,0:T(8,128)S(1)}, u32[]{:S(2)}, u32[]{:S(2)}) collective-permute-start(f32[256,512]{1,0:T(8,128)S(1)} %get-tuple-element.13), channel_id=1, source_target_pairs={{0,2},{2,4},{4,6},{6,8},{8,10},{10,12},{12,14},{14,0},{1,3},{3,5},... | collective-permute-start | bytes 1572872 | tf_op jit(solution)/shard_map/ppermute | solution.py:35
  75.6 25.5 %copy-start.4 = (f32[512,512]{1,0:T(8,128)}, f32[512,512]{1,0:T(8,128)S(1)}, u32[]{:S(2)}) copy-start(f32[512,512]{1,0:T(8,128)S(1)} %collective-permute-done.9.rest_2_) | copy-start | bytes 3145732
  76.4 26.9 %collective-permute-start.16 = (f32[256,512]{1,0:T(8,128)S(1)}, f32[256,512]{1,0:T(8,128)S(1)}, u32[]{:S(2)}, u32[]{:S(2)}) collective-permute-start(f32[256,512]{1,0:T(8,128)S(1)} %get-tuple-element.15), channel_id=1, source_target_pairs={{0,14},{2,0},{4,2},{6,4},{8,6},{10,8},{12,10},{14,12},{1,15},{3,1}... | collective-permute-start | bytes 1572872 | tf_op jit(solution)/shard_map/ppermute | solution.py:35
  78.9 25.8 %collective-permute-start.13 = (f32[256,512]{1,0:T(8,128)S(1)}, f32[256,512]{1,0:T(8,128)S(1)}, u32[]{:S(2)}, u32[]{:S(2)}) collective-permute-start(f32[256,512]{1,0:T(8,128)S(1)} %get-tuple-element.14), channel_id=1, source_target_pairs={{0,2},{2,4},{4,6},{6,8},{8,10},{10,12},{12,14},{14,0},{1,3},{3,5},... | collective-permute-start | bytes 1572872 | tf_op jit(solution)/shard_map/ppermute | solution.py:35
  83.4 26.2 %collective-permute-start.12 = (f32[256,512]{1,0:T(8,128)S(1)}, f32[256,512]{1,0:T(8,128)S(1)}, u32[]{:S(2)}, u32[]{:S(2)}) collective-permute-start(f32[256,512]{1,0:T(8,128)S(1)} %get-tuple-element.16), channel_id=1, source_target_pairs={{0,14},{2,0},{4,2},{6,4},{8,6},{10,8},{12,10},{14,12},{1,15},{3,1}... | collective-permute-start | bytes 1572872 | tf_op jit(solution)/shard_map/ppermute | solution.py:35
  83.4 26.8 %copy-start.28 = (f32[8,128,128]{2,1,0:T(8,128)}, f32[8,128,128]{2,1,0:T(8,128)S(1)}, u32[]{:S(2)}) copy-start(f32[8,128,128]{2,1,0:T(8,128)S(1)} %add.37.refs_1_) | copy-start | bytes 1572868
  101.0 10.1 %collective-permute-start.7 = (f32[8,128,128]{2,1,0:T(8,128)S(1)}, f32[8,128,128]{2,1,0:T(8,128)S(1)}, u32[]{:S(2)}, u32[]{:S(2)}) collective-permute-start(f32[8,128,128]{2,1,0:T(8,128)S(1)} %add.37.refs_1_), channel_id=1, source_target_pairs={{0,16},{16,0},{1,17},{17,1},{2,18},{18,2},{3,19},{19,3},{4,20},{20... | collective-permute-start | bytes 1572872 | tf_op jit(solution)/shard_map/ppermute | solution.py:35
  101.1 14.1 %copy-start.30 = (f32[8,128,128]{2,1,0:T(8,128)}, f32[8,128,128]{2,1,0:T(8,128)S(1)}, u32[]{:S(2)}) copy-start(f32[8,128,128]{2,1,0:T(8,128)S(1)} %add.34.refs_0_) | copy-start | bytes 1572868
  101.1 19.7 %copy-start = (f32[512,512]{1,0:T(8,128)S(1)}, f32[512,512]{1,0:T(8,128)}, u32[]{:S(2)}) copy-start(f32[512,512]{1,0:T(8,128)} %rest_0_.5) | copy-start | bytes 3145732
  101.1 19.7 %copy-start.39 = (s32[64]{0:T(128)S(1)}, s32[64]{0:T(128)}, u32[]{:S(2)}) copy-start(s32[64]{0:T(128)} %counts.9) | copy-start | bytes 772
  101.1 14.0 %collective-permute-start.6 = (f32[8,128,128]{2,1,0:T(8,128)S(1)}, f32[8,128,128]{2,1,0:T(8,128)S(1)}, u32[]{:S(2)}, u32[]{:S(2)}) collective-permute-start(f32[8,128,128]{2,1,0:T(8,128)S(1)} %add.34.refs_0_), channel_id=1, source_target_pairs={{0,16},{16,0},{1,17},{17,1},{2,18},{18,2},{3,19},{19,3},{4,20},{20... | collective-permute-start | bytes 1572872 | tf_op jit(solution)/shard_map/ppermute | solution.py:35
  103.3 17.5 %collective-permute-start.18 = (f32[128,512]{1,0:T(8,128)}, f32[128,512]{1,0:T(8,128)S(1)}, u32[]{:S(2)}, u32[]{:S(2)}) collective-permute-start(f32[128,512]{1,0:T(8,128)} %slice.48), channel_id=1, source_target_pairs={{0,2},{2,4},{4,6},{6,8},{8,10},{10,12},{12,14},{14,0},{1,3},{3,5},... | collective-permute-start | bytes 786440 | tf_op jit(solution)/shard_map/ppermute | solution.py:35
  104.8 16.0 %collective-permute-start.19 = (f32[128,512]{1,0:T(8,128)}, f32[128,512]{1,0:T(8,128)}, u32[]{:S(2)}, u32[]{:S(2)}) collective-permute-start(f32[128,512]{1,0:T(8,128)} %slice.49), channel_id=1, source_target_pairs={{0,14},{2,0},{4,2},{6,4},{8,6},{10,8},{12,10},{14,12},{1,15},{3,1}... | collective-permute-start | bytes 786440 | tf_op jit(solution)/shard_map/ppermute | solution.py:35
  109.5 22.6 %collective-permute-start.14 = (f32[128,512]{1,0:T(8,128)}, f32[128,512]{1,0:T(8,128)}, u32[]{:S(2)}, u32[]{:S(2)}) collective-permute-start(f32[128,512]{1,0:T(8,128)} %slice.44), channel_id=1, source_target_pairs={{0,2},{2,4},{4,6},{6,8},{8,10},{10,12},{12,14},{14,0},{1,3},{3,5},... | collective-permute-start | bytes 786440 | tf_op jit(solution)/shard_map/ppermute | solution.py:35
  111.8 20.3 %collective-permute-start.15 = (f32[128,512]{1,0:T(8,128)}, f32[128,512]{1,0:T(8,128)}, u32[]{:S(2)}, u32[]{:S(2)}) collective-permute-start(f32[128,512]{1,0:T(8,128)} %slice.45), channel_id=1, source_target_pairs={{0,14},{2,0},{4,2},{6,4},{8,6},{10,8},{12,10},{14,12},{1,15},{3,1}... | collective-permute-start | bytes 786440 | tf_op jit(solution)/shard_map/ppermute | solution.py:35
  115.1 5.8 %copy-start.5 = (f32[512,512]{1,0:T(8,128)S(1)}, f32[512,512]{1,0:T(8,128)}, u32[]{:S(2)}) copy-start(f32[512,512]{1,0:T(8,128)} %copy-done.4) | copy-start | bytes 3145732
  115.1 5.8 %copy-start.17 = (f32[256,512]{1,0:T(8,128)S(1)}, f32[256,512]{1,0:T(8,128)}, u32[]{:S(2)}) copy-start(f32[256,512]{1,0:T(8,128)} %copy-done.16) | copy-start | bytes 1572868
  115.1 5.8 %copy-start.20 = (f32[256,512]{1,0:T(8,128)S(1)}, f32[256,512]{1,0:T(8,128)}, u32[]{:S(2)}) copy-start(f32[256,512]{1,0:T(8,128)} %copy-done.19) | copy-start | bytes 1572868
  116.0 1.0 copy-start.29
  117.0 1.1 copy-start.31
  118.1 1.0 copy-start.34
  120.9 1.2 copy-start.2
  122.1 1.3 copy-start.8
  123.4 1.2 copy-start.11
  124.6 7.5 %copy-start.23 = (f32[256,512]{1,0:T(8,128)S(1)}, f32[256,512]{1,0:T(8,128)}, u32[]{:S(2)}) copy-start(f32[256,512]{1,0:T(8,128)} %copy-done.22) | copy-start | bytes 1572868
  124.6 7.5 %copy-start.26 = (f32[256,512]{1,0:T(8,128)S(1)}, f32[256,512]{1,0:T(8,128)}, u32[]{:S(2)}) copy-start(f32[256,512]{1,0:T(8,128)} %copy-done.25) | copy-start | bytes 1572868
  129.1 32.6 %collective-permute-start.20 = (f32[256,512]{1,0:T(8,128)}, f32[256,512]{1,0:T(8,128)}, u32[]{:S(2)}, u32[]{:S(2)}) collective-permute-start(f32[256,512]{1,0:T(8,128)} %beta.5), channel_id=1, source_target_pairs={{0,1},{1,0},{2,3},{3,2},{4,5},{5,4},{6,7},{7,6},{8,9},{9,8},{10,11... | collective-permute-start | bytes 1572872 | tf_op jit(solution)/shard_map/ppermute | solution.py:35
  136.7 25.0 %collective-permute-start.21 = (f32[256,512]{1,0:T(8,128)}, f32[256,512]{1,0:T(8,128)}, u32[]{:S(2)}, u32[]{:S(2)}) collective-permute-start(f32[256,512]{1,0:T(8,128)} %beta.3), channel_id=1, source_target_pairs={{0,1},{1,0},{2,3},{3,2},{4,5},{5,4},{6,7},{7,6},{8,9},{9,8},{10,11... | collective-permute-start | bytes 1572872 | tf_op jit(solution)/shard_map/ppermute | solution.py:35
  137.4 1.2 copy-start.3
  138.6 1.2 copy-start.6
  139.9 1.2 copy-start.9
  141.1 1.2 copy-start.12
  152.9 8.8 %copy-start.15 = (f32[512,512]{1,0:T(8,128)S(1)}, f32[512,512]{1,0:T(8,128)}, u32[]{:S(2)}) copy-start(f32[512,512]{1,0:T(8,128)} %copy-done.14) | copy-start | bytes 3145732
  (16 other events, 14.1 us)
Sparse Core Ops, SparseCore 0:
  9.2 122.3 all-gather.1

commit v3 on v2

--- a/solution.py
+++ b/solution.py
@@ -12,7 +12,7 @@
 ROW = ("yl", "x", "c")
 COL = ("z", "yh")
 B = 128
-VMEM_LIMIT = 56 * 1024 * 1024
+VMEM_LIMIT = 60 * 1024 * 1024
 
 
 def flat(yl, x, c, z, yh):
@@ -114,7 +114,64 @@
 
 def beta_kernel(place, links, counts, phases, sizes, *rest, spots):
     count = len(spots)
-    pieces, (out, held, names, left, sems) = rest[:count], rest[count:]
+    pieces, (out, held, names, sems) = rest[:count], rest[count:]
+    rows = out.shape[0]
+    copies = [
+        pltpu.make_async_copy(piece.at[pl.ds(start, size), :], held.at[slot, pl.ds(to, size), :], sems.at[i])
+        for i, (piece, (slot, start, to, size)) in enumerate(zip(pieces, spots))
+    ]
+    for copy in copies:
+        copy.start()
+    z, yh, which = place[0], place[1], place[2]
+    first = (z * 2 + which) * 4
+    rank = jnp.int32(0)
+    for i in range(4):
+        for l in range(8):
+            source = links[first + i, l]
+            names[jnp.minimum(rank, 2 * FEW)] = source * 4 + i
+            rank = rank + ((l < counts[first + i]) & (((source >> 2) & 1) == yh)).astype(jnp.int32)
+
+    for r in range(1, 2 * FEW):
+        names[r] = jnp.where(r < rank, names[r], 0)
+    out[...] = jnp.zeros_like(out)
+
+    @pl.when(is_source)
+    def _():
+        rank = jnp.int32(0)
+        for i in range(4):
+            for l in range(8):
+                used = (l < counts[first + i]) & (((links[first + i, l] >> 2) & 1) == yh)
+
+                @pl.when(used)
+                def _(i=i, l=l, rank=rank):
+                    pair = pairs[i, l]
+                    out[jnp.minimum(rank, 2 * FEW - 1)] = signs[i, l].astype(jnp.float32) * integrals[pair >> 4, pair & 15]
+
+                rank = rank + used.astype(jnp.int32)
+
+        def clear(i, carry):
+            out[i] = jnp.zeros((B, B), jnp.float32)
+            return carry
+
+        lax.fori_loop(rank, 2 * FEW, clear, 0)
+
+
+def pack(place, links, counts, pairs, integrals, signs):
+    scalar = pl.BlockSpec(memory_space=pltpu.SMEM)
+    return pl.pallas_call(
+        pack_kernel,
+        out_shape=jax.ShapeDtypeStruct((2 * FEW, B, B), jnp.float32),
+        in_specs=[scalar] * 5 + [pl.BlockSpec(memory_space=pltpu.VMEM)],
+        out_specs=pl.BlockSpec(memory_space=pltpu.VMEM),
+        compiler_params=pltpu.CompilerParams(vmem_limit_bytes=16 << 20),
+        cost_estimate=pl.CostEstimate(flops=32 * B * B, bytes_accessed=48 * B * B * 4, transcendentals=0),
+        name="pack",
+    )(place, links, counts, pairs, integrals, signs)
+
+
+def beta_kernel(place, links, counts, phases, sizes, *rest, spots):
+    count = len(spots)
+    pieces, (out, held, names, sems) = rest[:count], rest[count:]
     rows = out.shape[0]
     copies = [
         pltpu.make_async_copy(piece.at[pl.ds(start, size), :], held.at[slot, pl.ds(to, size), :], sems.at[i])
@@ -145,8 +202,10 @@
         slot = ((name >> 5) - z) & 7
         lanes = pl.ds(pl.multiple_of(((name >> 2) & 3) * B, B), B)
         target = pl.ds(pl.multiple_of((name & 3) * B, B), B)
-        left[r % 2, :, :B], left[r % 2, :, B:] = halves(held[slot, :, lanes] * sizes[0, r:r + 1, :])
-        out[:, target] += jnp.dot(left[r % 2], phases[0, r], preferred_element_type=jnp.float32)
+        for start in range(0, rows, B):
+            tile = slice(start, start + B)
+            both = jnp.concatenate(halves(held[slot, tile, lanes] * sizes[0, r:r + 1, :]), axis=1)
+            out[tile, target] += jnp.dot(both, phases[0, r], preferred_element_type=jnp.float32)
 
 
 def beta_part(place, links, counts, phases, sizes, rows, pieces, spots):
@@ -163,32 +222,35 @@
             out_specs=pl.BlockSpec((rows, 4 * B), lambda i, *_: (0, 0), pipeline_mode=pl.Buffered(1)),
             scratch_shapes=[
                 pltpu.VMEM((8, rows, 4 * B), jnp.float32),
-                pltpu.SMEM((2 * FEW,), jnp.int32),
-                pltpu.VMEM((2, rows, 2 * B), jnp.bfloat16),
+                pltpu.SMEM((2 * FEW + 1,), jnp.int32),
                 pltpu.SemaphoreType.DMA((len(spots),)),
             ],
         ),
-        compiler_params=pltpu.CompilerParams(dimension_semantics=("arbitrary",), vmem_limit_bytes=24 << 20),
+        compiler_params=pltpu.CompilerParams(dimension_semantics=("arbitrary",), vmem_limit_bytes=VMEM_LIMIT),
         cost_estimate=pl.CostEstimate(flops=16 * rows * B * 2 * B * 2, bytes_accessed=rows * 512 * 36 + (1 << 20), transcendentals=0),
         name="beta",
     )(place, links, counts, phases, sizes, *pieces)
 
 
 def alpha_kernel(place, links, counts, pairs, integrals, signs, *rest):
-    tiles, (out, left, high, low) = rest[:8], rest[8:]
+    tiles, (kept, out) = rest[:8], rest[8:]
     step = pl.program_id(0)
     block = place[0] * 4 + step
+    coefs = []
     for l in range(8):
         pair = pairs[step, l]
-        coef = jnp.where(l < counts[block], integrals[pair >> 4, pair & 15], 0.0)
-        left[:, l * B:(l + 1) * B] = signs[0, l].astype(jnp.float32).astype(jnp.bfloat16)
-        high[l * B:(l + 1) * B, :], low[l * B:(l + 1) * B, :] = halves(tiles[l][0] * coef)
-    out[...] = jnp.dot(left[...], high[...], preferred_element_type=jnp.float32) + jnp.dot(
-        left[...], low[...], preferred_element_type=jnp.float32
-    )
-
-
-def alpha_part(place, links, counts, pairs, integrals, signs, column):
+        coefs.append(jnp.where(l < counts[block], integrals[pair >> 4, pair & 15], 0.0))
+    phase = jnp.concatenate([signs[0, k].astype(jnp.float32).astype(jnp.bfloat16) for k in range(8)], axis=1)
+    for half in range(2):
+        lanes = slice(half * 2 * B, (half + 1) * 2 * B)
+        parts = [halves(tiles[k][0, :, lanes] * coefs[k]) for k in range(8)]
+        right = jnp.concatenate([pair[0] for pair in parts], axis=0)
+        total = kept[:, lanes] + jnp.dot(phase, right, preferred_element_type=jnp.float32)
+        right = jnp.concatenate([pair[1] for pair in parts], axis=0)
+        out[:, lanes] = total + jnp.dot(phase, right, preferred_element_type=jnp.float32)
+
+
+def alpha_part(place, links, counts, pairs, integrals, signs, column, kept):
     def tile(l):
         return pl.BlockSpec((1, B, 4 * B), lambda i, place, links, *_: (links[place[0] * 4 + i, l], 0, 0))
 
@@ -198,18 +260,15 @@
         grid_spec=pltpu.PrefetchScalarGridSpec(
             num_scalar_prefetch=5,
             grid=(4,),
-            in_specs=[pl.BlockSpec((1, 8, B, B), lambda i, *_: (i, 0, 0, 0))] + [tile(l) for l in range(8)],
+            in_specs=[pl.BlockSpec((1, 8, B, B), lambda i, *_: (i, 0, 0, 0))] + [tile(l) for l in range(8)] + [
+                pl.BlockSpec((B, 4 * B), lambda i, *_: (i, 0)),
+            ],
             out_specs=pl.BlockSpec((B, 4 * B), lambda i, *_: (i, 0)),
-            scratch_shapes=[
-                pltpu.VMEM((B, 8 * B), jnp.bfloat16),
-                pltpu.VMEM((8 * B, 4 * B), jnp.bfloat16),
-                pltpu.VMEM((8 * B, 4 * B), jnp.bfloat16),
-            ],
         ),
         compiler_params=pltpu.CompilerParams(dimension_semantics=("arbitrary",), vmem_limit_bytes=VMEM_LIMIT),
-        cost_estimate=pl.CostEstimate(flops=4 * 4 * B * B * 16 * B * 2, bytes_accessed=11 << 20, transcendentals=0),
+        cost_estimate=pl.CostEstimate(flops=4 * 4 * B * B * 16 * B * 2, bytes_accessed=14 << 20, transcendentals=0),
         name="alpha",
-    )(place, links, counts, pairs, integrals, signs, *[column] * 8)
+    )(place, links, counts, pairs, integrals, signs, *[column] * 8, kept)
 
 
 HALF = 2 * B
@@ -259,9 +318,8 @@
     sent = [shift(value, "yh", 1) for value in partial]
     ours, _ = lax.optimization_barrier((ours, partial[1]))
     kept = beta_part(ours, *tables, 2 * HALF, near + chunks[0] + chunks[1], near_spots(0, 2 * HALF) + far_spots(0) + far_spots(HALF))
-    place, _ = lax.optimization_barrier((row_index[None].astype(jnp.int32), partial[1]))
-    alpha = alpha_part(place, links, counts, pairs, one_electron, signs, column)
-    return alpha + kept + jnp.concatenate(sent, axis=0)
+    place = row_index[None].astype(jnp.int32)
+    return alpha_part(place, links, counts, pairs, one_electron, signs, column, kept) + jnp.concatenate(sent, axis=0)
 
 
 def solution(mesh):

time: 173 us -> 160 us (0.925)
  the two profiles are of different devices: /device:TPU:4 before, /device:TPU:1 now
where the time goes in v3:
time: 160 us; the launch traced here: 157 us
  waiting for transfers between devices  51.4 us (32%)
  starting transfers between devices  45 us (28%)
  Pallas kernels  32.1 us (20%)
  between operations  13.7 us (9%)
  local copies, waits for them, and re-layouts  10.9 us (7%)
  other arithmetic  4.06 us (3%)
    ppermute x16, starting transfers between devices, shift(): return lax.ppermute(value, axis, [(i, (i + by) % n) for i in range(n)])  32.7 us
    ppermute x6, waiting for transfers between devices, spread(): return lax.ppermute(value, AXES, pairs)  30.1 us
    pallas_call x3, Pallas kernels, beta_part(): pl.pallas_call(functools.partial(beta_kernel, spots=spots), out_shape=jax...  21.3 us
    ppermute x16, waiting for transfers between devices, shift(): return lax.ppermute(value, axis, [(i, (i + by) % n) for i in range(n)])  20.6 us
    ppermute x6, starting transfers between devices, spread(): return lax.ppermute(value, AXES, pairs)  12.4 us
    pallas_call x1, Pallas kernels, alpha_part(): pl.pallas_call(alpha_kernel, out_shape=jax.ShapeDtypeStruct((4 * B, 4 * B...  8.52 us
    unnamed x31, local copies, waits for them, and re-layouts  7.77 us
  transfers between devices with their start and end apart: 23, of which 8 were waited for; matrix products, arithmetic and copies ran while one was open for 4% of the time, Pallas kernels for 20%

profile of v3, /device:TPU:1, one launch (start us, length us, event | category | flops | bytes accessed | tf_op | source)
XLA Modules:
  0.0 157.2 jit_solution(8313065798572936409)
XLA Ops:
  6.5 0.7 all-gather.2.cloned.1.call-update
  7.3 2.5 %collective-permute-start.10 = (f32[512,512]{1,0:T(8,128)}, f32[512,512]{1,0:T(8,128)S(1)}, u32[]{:S(2)}, u32[]{:S(2)}) collective-permute-start(f32[512,512]{1,0:T(8,128)} %rest_0_.5), channel_id=1, source_target_pairs={{0,2},{2,4},{4,6},{6,8},{8,10},{10,12},{12,14},{14,0},{1,3},{3,5},... | collective-permute-start | bytes 3145736 | tf_op jit(solution)/shard_map/ppermute | solution.py:35
  9.8 4.0 %collective-permute-start.8 = (f32[512,512]{1,0:T(8,128)}, f32[512,512]{1,0:T(8,128)}, u32[]{:S(2)}, u32[]{:S(2)}) collective-permute-start(f32[512,512]{1,0:T(8,128)} %rest_0_.5), channel_id=1, source_target_pairs={{0,14},{2,0},{4,2},{6,4},{8,6},{10,8},{12,10},{14,12},{1,15},{3,1}... | collective-permute-start | bytes 3145736 | tf_op jit(solution)/shard_map/ppermute | solution.py:35
  13.8 0.8 copy.10.links
  14.7 1.6 %copy-done.1 = s32[4,8,128,128]{3,2,1,0:T(8,128)S(1)} copy-done((s32[4,8,128,128]{3,2,1,0:T(8,128)S(1)}, s32[4,8,128,128]{3,2,1,0:T(8,128)}, u32[]{:S(2)}) %copy-start.1) | copy-done | bytes 2097176
  16.3 0.7 copy-done.4
  17.0 0.7 copy-done.5
  17.6 0.7 copy-done.6
  18.3 1.7 %pack.1 = f32[16,128,128]{2,1,0:T(8,128)S(1)} custom-call(s32[3]{0:T(128)S(1)} %pad_add_fusion.3.place, s32[64,8]{1,0:T(8,128)S(1)} %copy.10.links, s32[64]{0:T(128)S(1)} %copy-done.5, s32[4,8]{1,0:T(4,128)S(1)} %copy-done.6, f32[16,16]{1,0:T(8,128)S(1)} %copy-done.4, s32[4,8,128,128]{3,2,1,0:T(8,128)S(1)} %copy-done.1), custom_call_target="tpu_custom_call" | custom-call | flops 524288 | bytes 3145728 | tf_op jit(solution)/shard_map/pack/pallas_call | solution.py:161
  20.2 2.8 %collective-permute-start = (f32[8,128,128]{2,1,0:T(8,128)S(1)}, f32[8,128,128]{2,1,0:T(8,128)S(1)}, u32[]{:S(2)}, u32[]{:S(2)}) collective-permute-start(f32[8,128,128]{2,1,0:T(8,128)S(1)} %get-tuple-element.18), channel_id=1, source_target_pairs={{0,128},{16,144},{1,129},{17,145},{34,162},{50,178},{35,163},{51,1... | collective-permute-start | bytes 1572872 | tf_op jit(solution)/shard_map/ppermute | solution.py:30
  23.0 1.3 collective-permute-start.3
  24.3 12.5 %collective-permute-done.10.rest_4_ = f32[512,512]{1,0:T(8,128)S(1)} collective-permute-done((f32[512,512]{1,0:T(8,128)}, f32[512,512]{1,0:T(8,128)S(1)}, u32[]{:S(2)}, u32[]{:S(2)}) %collective-permute-start.10) | collective-permute-done | bytes 1048608 | tf_op jit(solution)/shard_map/ppermute | solution.py:35
  36.8 2.7 %collective-permute-start.9 = (f32[512,512]{1,0:T(8,128)}, f32[512,512]{1,0:T(8,128)S(1)}, u32[]{:S(2)}, u32[]{:S(2)}) collective-permute-start(f32[512,512]{1,0:T(8,128)} %collective-permute-done.8.rest_1_), channel_id=1, source_target_pairs={{0,14},{2,0},{4,2},{6,4},{8,6},{10,8},{12,10},{14,12},{1,15},{3,1}... | collective-permute-start | bytes 3145736 | tf_op jit(solution)/shard_map/ppermute | solution.py:35
  39.5 2.2 %collective-permute-done = f32[8,128,128]{2,1,0:T(8,128)S(1)} collective-permute-done((f32[8,128,128]{2,1,0:T(8,128)S(1)}, f32[8,128,128]{2,1,0:T(8,128)S(1)}, u32[]{:S(2)}, u32[]{:S(2)}) %collective-permute-start) | collective-permute-done | bytes 524320 | tf_op jit(solution)/shard_map/ppermute | solution.py:30
  41.7 4.8 %collective-permute-done.3 = f32[8,128,128]{2,1,0:T(8,128)S(1)} collective-permute-done((f32[8,128,128]{2,1,0:T(8,128)S(1)}, f32[8,128,128]{2,1,0:T(8,128)S(1)}, u32[]{:S(2)}, u32[]{:S(2)}) %collective-permute-start.3) | collective-permute-done | bytes 524320 | tf_op jit(solution)/shard_map/ppermute | solution.py:30
  46.6 1.3 collective-permute-start.4
  47.9 4.2 %collective-permute-start.1 = (f32[8,128,128]{2,1,0:T(8,128)S(1)}, f32[8,128,128]{2,1,0:T(8,128)S(1)}, u32[]{:S(2)}, u32[]{:S(2)}) collective-permute-start(f32[8,128,128]{2,1,0:T(8,128)S(1)} %get-tuple-element.16), channel_id=1, source_target_pairs={{0,32},{128,160},{16,48},{144,176},{1,33},{129,161},{17,49},{145,1... | collective-permute-start | bytes 1572872 | tf_op jit(solution)/shard_map/ppermute | solution.py:30
  52.2 5.5 %collective-permute-done.4 = f32[8,128,128]{2,1,0:T(8,128)S(1)} collective-permute-done((f32[8,128,128]{2,1,0:T(8,128)S(1)}, f32[8,128,128]{2,1,0:T(8,128)S(1)}, u32[]{:S(2)}, u32[]{:S(2)}) %collective-permute-start.4) | collective-permute-done | bytes 524320 | tf_op jit(solution)/shard_map/ppermute | solution.py:30
  57.8 1.3 collective-permute-start.5
  59.1 15.3 %collective-permute-done.1 = f32[8,128,128]{2,1,0:T(8,128)S(1)} collective-permute-done((f32[8,128,128]{2,1,0:T(8,128)S(1)}, f32[8,128,128]{2,1,0:T(8,128)S(1)}, u32[]{:S(2)}, u32[]{:S(2)}) %collective-permute-start.1) | collective-permute-done | bytes 524320 | tf_op jit(solution)/shard_map/ppermute | solution.py:30
  74.5 1.3 collective-permute-start.2
  76.1 0.7 copy-done.7
  76.8 2.0 %collective-permute-start.16 = (f32[256,512]{1,0:T(8,128)S(1)}, f32[256,512]{1,0:T(8,128)S(1)}, u32[]{:S(2)}, u32[]{:S(2)}) collective-permute-start(f32[256,512]{1,0:T(8,128)S(1)} %get-tuple-element.13), channel_id=1, source_target_pairs={{0,14},{2,0},{4,2},{6,4},{8,6},{10,8},{12,10},{14,12},{1,15},{3,1}... | collective-permute-start | bytes 1572872 | tf_op jit(solution)/shard_map/ppermute | solution.py:35
  78.8 2.3 %collective-permute-done.5 = f32[8,128,128]{2,1,0:T(8,128)S(1)} collective-permute-done((f32[8,128,128]{2,1,0:T(8,128)S(1)}, f32[8,128,128]{2,1,0:T(8,128)S(1)}, u32[]{:S(2)}, u32[]{:S(2)}) %collective-permute-start.5) | collective-permute-done | bytes 524320 | tf_op jit(solution)/shard_map/ppermute | solution.py:30
  81.2 9.2 %collective-permute-start.12 = (f32[256,512]{1,0:T(8,128)S(1)}, f32[256,512]{1,0:T(8,128)S(1)}, u32[]{:S(2)}, u32[]{:S(2)}) collective-permute-start(f32[256,512]{1,0:T(8,128)S(1)} %get-tuple-element.14), channel_id=1, source_target_pairs={{0,14},{2,0},{4,2},{6,4},{8,6},{10,8},{12,10},{14,12},{1,15},{3,1}... | collective-permute-start | bytes 1572872 | tf_op jit(solution)/shard_map/ppermute | solution.py:35
  90.4 3.7 %collective-permute-start.7 = (f32[8,128,128]{2,1,0:T(8,128)S(1)}, f32[8,128,128]{2,1,0:T(8,128)S(1)}, u32[]{:S(2)}, u32[]{:S(2)}) collective-permute-start(f32[8,128,128]{2,1,0:T(8,128)S(1)} %add.34.refs_1_), channel_id=1, source_target_pairs={{0,16},{16,0},{1,17},{17,1},{2,18},{18,2},{3,19},{19,3},{4,20},{20... | collective-permute-start | bytes 1572872 | tf_op jit(solution)/shard_map/ppermute | solution.py:35
  94.5 0.7 slice.48
  95.2 2.1 %collective-permute-start.18 = (f32[128,512]{1,0:T(8,128)}, f32[128,512]{1,0:T(8,128)S(1)}, u32[]{:S(2)}, u32[]{:S(2)}) collective-permute-start(f32[128,512]{1,0:T(8,128)} %slice.48), channel_id=1, source_target_pairs={{0,2},{2,4},{4,6},{6,8},{8,10},{10,12},{12,14},{14,0},{1,3},{3,5},... | collective-permute-start | bytes 786440 | tf_op jit(solution)/shard_map/ppermute | solution.py:35
  97.3 0.7 slice.49
  98.0 1.4 collective-permute-done.13.rest_8_.rest_12_
  99.4 0.8 slice.44
  100.2 1.4 collective-permute-start.14
  101.6 0.7 slice.45
  102.4 1.5 collective-permute-start.15
  103.9 0.6 pad_add_fusion.2.place
  104.5 0.6 prepare_beta.1
  105.1 1.3 copy-done
  106.4 0.6 copy-done.3
  107.0 0.7 copy-done.14
  107.7 6.5 %beta.5 = f32[256,512]{1,0:T(8,128)} custom-call(s32[4]{0:T(128)} %pad_add_fusion.2.place, s32[64,8]{1,0:T(8,128)} %copy-done.2, s32[64]{0:T(128)} %counts.9, bf16[2,16,256,128]{3,2,1,0:T(8,128)(2,1)} %copy-done, f32[2,16,128]{2,1,0:T(8,128)} %copy-done.3, f32[512,512]{1,0:T(8,128)} %rest_0_.5, f32[512,512]{1,0:T(8,128)} %collective-permute-done.8.rest_1_, ...), custom_call_target="tpu_custom_call" | custom-call | flops 268435456 | bytes 5767168 | tf_op jit(solution)/shard_map/beta/pallas_call | solution.py:212
  114.2 1.9 %collective-permute-start.20 = (f32[256,512]{1,0:T(8,128)}, f32[256,512]{1,0:T(8,128)S(1)}, u32[]{:S(2)}, u32[]{:S(2)}) collective-permute-start(f32[256,512]{1,0:T(8,128)} %beta.5), channel_id=1, source_target_pairs={{0,1},{1,0},{2,3},{3,2},{4,5},{5,4},{6,7},{7,6},{8,9},{9,8},{10,11... | collective-permute-start | bytes 1572872 | tf_op jit(solution)/shard_map/ppermute | solution.py:35
  116.1 6.4 %beta.3 = f32[256,512]{1,0:T(8,128)} custom-call(s32[4]{0:T(128)} %pad_add_fusion.2.place, s32[64,8]{1,0:T(8,128)} %copy-done.2, s32[64]{0:T(128)} %counts.9, bf16[2,16,256,128]{3,2,1,0:T(8,128)(2,1)} %copy-done, f32[2,16,128]{2,1,0:T(8,128)} %copy-done.3, f32[512,512]{1,0:T(8,128)} %rest_0_.5, f32[512,512]{1,0:T(8,128)} %collective-permute-done.8.rest_1_, ...), custom_call_target="tpu_custom_call" | custom-call | flops 268435456 | bytes 5767168 | tf_op jit(solution)/shard_map/beta/pallas_call | solution.py:212
  122.5 1.2 collective-permute-start.21
  123.8 0.6 pad_add_fusion.place
  124.4 8.4 %beta.4.rest_8_ = f32[512,512]{1,0:T(8,128)} custom-call(s32[4]{0:T(128)} %pad_add_fusion.place, s32[64,8]{1,0:T(8,128)} %copy-done.2, s32[64]{0:T(128)} %counts.9, bf16[2,16,256,128]{3,2,1,0:T(8,128)(2,1)} %copy-done, f32[2,16,128]{2,1,0:T(8,128)} %copy-done.3, f32[512,512]{1,0:T(8,128)} %rest_0_.5, f32[512,512]{1,0:T(8,128)} %collective-permute-done.8.rest_1_, ...), custom_call_target="tpu_custom_call" | custom-call | flops 536870912 | bytes 10485760 | tf_op jit(solution)/shard_map/beta/pallas_call | solution.py:212
  132.8 8.5 %alpha.1 = f32[512,512]{1,0:T(8,128)} custom-call(s32[1]{0:T(128)} %bitcast.place, s32[64,8]{1,0:T(8,128)} %copy-done.2, s32[64]{0:T(128)} %counts.9, s32[4,8]{1,0:T(4,128)} %pairs.3, f32[16,16]{1,0:T(8,128)} %integrals.3, s32[4,8,128,128]{3,2,1,0:T(8,128)} %signs.3, f32[64,128,512]{2,1,0:T(8,128)} %bitcast.8, f32[64,128,512]{2,1,0:T(8,128)} %bitcast.9, ...), custom_call_target="tpu_custom_call" | custom-call | flops 1073741824 | bytes 14680064 | tf_op jit(solution)/shard_map/alpha/pallas_call | solution.py:257
  141.3 6.7 %collective-permute-done.21 = f32[256,512]{1,0:T(8,128)S(1)} collective-permute-done((f32[256,512]{1,0:T(8,128)}, f32[256,512]{1,0:T(8,128)S(1)}, u32[]{:S(2)}, u32[]{:S(2)}) %collective-permute-start.21) | collective-permute-done | bytes 524320 | tf_op jit(solution)/shard_map/ppermute | solution.py:35
  148.0 2.4 %maximum_add_fusion = f32[512,512]{1,0:T(8,128)} fusion(f32[512,512]{1,0:T(8,128)} %alpha.1, f32[256,512]{1,0:T(8,128)S(1)} %collective-permute-done.21, f32[256,512]{1,0:T(8,128)S(1)} %collective-permute-done.20), kind=kLoop, calls=%fused_computation | loop fusion | flops 524288 | bytes 3145728 | tf_op jit(solution)/shard_map/add | solution.py:322
  (52 shorter events, 1.2 us)
Async XLA Ops:
  6.5 126.3 %all-gather.2.cloned.1.call-start = ((), (), s32[]{:S(2)}) async-start(), calls=%async_computation | async-start | bytes 17825792 | tf_op jit(solution)/shard_map/all_gather | solution.py:280
  7.3 29.6 %collective-permute-start.10 = (f32[512,512]{1,0:T(8,128)}, f32[512,512]{1,0:T(8,128)S(1)}, u32[]{:S(2)}, u32[]{:S(2)}) collective-permute-start(f32[512,512]{1,0:T(8,128)} %rest_0_.5), channel_id=1, source_target_pairs={{0,2},{2,4},{4,6},{6,8},{8,10},{10,12},{12,14},{14,0},{1,3},{3,5},... | collective-permute-start | bytes 3145736 | tf_op jit(solution)/shard_map/ppermute | solution.py:35
  9.8 27.0 %collective-permute-start.8 = (f32[512,512]{1,0:T(8,128)}, f32[512,512]{1,0:T(8,128)}, u32[]{:S(2)}, u32[]{:S(2)}) collective-permute-start(f32[512,512]{1,0:T(8,128)} %rest_0_.5), channel_id=1, source_target_pairs={{0,14},{2,0},{4,2},{6,4},{8,6},{10,8},{12,10},{14,12},{1,15},{3,1}... | collective-permute-start | bytes 3145736 | tf_op jit(solution)/shard_map/ppermute | solution.py:35
  14.6 5.6 %copy-start.2 = (s32[64,8]{1,0:T(8,128)}, s32[64,8]{1,0:T(8,128)S(1)}, u32[]{:S(2)}) copy-start(s32[64,8]{1,0:T(8,128)S(1)} %copy.10.links) | copy-start | bytes 6148
  14.7 1.6 %copy-start.1 = (s32[4,8,128,128]{3,2,1,0:T(8,128)S(1)}, s32[4,8,128,128]{3,2,1,0:T(8,128)}, u32[]{:S(2)}) copy-start(s32[4,8,128,128]{3,2,1,0:T(8,128)} %signs.3) | copy-start | bytes 6291460
  16.3 0.7 copy-start.4
  17.0 0.7 copy-start.5
  17.6 0.7 copy-start.6
  20.2 21.5 %collective-permute-start = (f32[8,128,128]{2,1,0:T(8,128)S(1)}, f32[8,128,128]{2,1,0:T(8,128)S(1)}, u32[]{:S(2)}, u32[]{:S(2)}) collective-permute-start(f32[8,128,128]{2,1,0:T(8,128)S(1)} %get-tuple-element.18), channel_id=1, source_target_pairs={{0,128},{16,144},{1,129},{17,145},{34,162},{50,178},{35,163},{51,1... | collective-permute-start | bytes 1572872 | tf_op jit(solution)/shard_map/ppermute | solution.py:30
  23.0 23.5 %collective-permute-start.3 = (f32[8,128,128]{2,1,0:T(8,128)S(1)}, f32[8,128,128]{2,1,0:T(8,128)S(1)}, u32[]{:S(2)}, u32[]{:S(2)}) collective-permute-start(f32[8,128,128]{2,1,0:T(8,128)S(1)} %get-tuple-element.17), channel_id=1, source_target_pairs={{0,32},{16,48},{1,33},{17,49},{34,66},{50,82},{35,67},{51,83},{68,... | collective-permute-start | bytes 1572872 | tf_op jit(solution)/shard_map/ppermute | solution.py:30
  36.8 20.9 %copy-start.9 = (f32[512,512]{1,0:T(8,128)}, f32[512,512]{1,0:T(8,128)S(1)}, u32[]{:S(2)}) copy-start(f32[512,512]{1,0:T(8,128)S(1)} %collective-permute-done.10.rest_4_) | copy-start | bytes 3145732
  36.8 39.0 %collective-permute-start.11 = (f32[512,512]{1,0:T(8,128)S(1)}, f32[512,512]{1,0:T(8,128)S(1)}, u32[]{:S(2)}, u32[]{:S(2)}) collective-permute-start(f32[512,512]{1,0:T(8,128)S(1)} %collective-permute-done.10.rest_4_), channel_id=1, source_target_pairs={{0,2},{2,4},{4,6},{6,8},{8,10},{10,12},{12,14},{14,0},{1,3},{3,5},... | collective-permute-start | bytes 3145736 | tf_op jit(solution)/shard_map/ppermute | solution.py:35
  36.8 39.2 %collective-permute-start.9 = (f32[512,512]{1,0:T(8,128)}, f32[512,512]{1,0:T(8,128)S(1)}, u32[]{:S(2)}, u32[]{:S(2)}) collective-permute-start(f32[512,512]{1,0:T(8,128)} %collective-permute-done.8.rest_1_), channel_id=1, source_target_pairs={{0,14},{2,0},{4,2},{6,4},{8,6},{10,8},{12,10},{14,12},{1,15},{3,1}... | collective-permute-start | bytes 3145736 | tf_op jit(solution)/shard_map/ppermute | solution.py:35
  46.6 11.1 %collective-permute-start.4 = (f32[8,128,128]{2,1,0:T(8,128)S(1)}, f32[8,128,128]{2,1,0:T(8,128)S(1)}, u32[]{:S(2)}, u32[]{:S(2)}) collective-permute-start(f32[8,128,128]{2,1,0:T(8,128)S(1)} %get-tuple-element.15), channel_id=1, source_target_pairs={{0,96},{32,64},{16,112},{48,80},{1,97},{33,65},{17,113},{49,81},{3... | collective-permute-start | bytes 1572872 | tf_op jit(solution)/shard_map/ppermute | solution.py:30
  47.9 26.5 %collective-permute-start.1 = (f32[8,128,128]{2,1,0:T(8,128)S(1)}, f32[8,128,128]{2,1,0:T(8,128)S(1)}, u32[]{:S(2)}, u32[]{:S(2)}) collective-permute-start(f32[8,128,128]{2,1,0:T(8,128)S(1)} %get-tuple-element.16), channel_id=1, source_target_pairs={{0,32},{128,160},{16,48},{144,176},{1,33},{129,161},{17,49},{145,1... | collective-permute-start | bytes 1572872 | tf_op jit(solution)/shard_map/ppermute | solution.py:30
  57.8 23.4 %collective-permute-start.5 = (f32[8,128,128]{2,1,0:T(8,128)S(1)}, f32[8,128,128]{2,1,0:T(8,128)S(1)}, u32[]{:S(2)}, u32[]{:S(2)}) collective-permute-start(f32[8,128,128]{2,1,0:T(8,128)S(1)} %add.33), channel_id=1, source_target_pairs={{0,128},{32,160},{64,192},{96,224},{16,144},{48,176},{80,208},{112... | collective-permute-start | bytes 1572872 | tf_op jit(solution)/shard_map/ppermute | solution.py:30
  74.5 15.9 %collective-permute-start.2 = (f32[8,128,128]{2,1,0:T(8,128)S(1)}, f32[8,128,128]{2,1,0:T(8,128)S(1)}, u32[]{:S(2)}, u32[]{:S(2)}) collective-permute-start(f32[8,128,128]{2,1,0:T(8,128)S(1)} %add.30), channel_id=1, source_target_pairs={{0,96},{128,224},{32,64},{160,192},{16,112},{144,240},{48,80},{176... | collective-permute-start | bytes 1572872 | tf_op jit(solution)/shard_map/ppermute | solution.py:30
  75.8 1.0 copy-start.7
  75.9 18.3 %collective-permute-start.17 = (f32[256,512]{1,0:T(8,128)S(1)}, f32[256,512]{1,0:T(8,128)S(1)}, u32[]{:S(2)}, u32[]{:S(2)}) collective-permute-start(f32[256,512]{1,0:T(8,128)S(1)} %get-tuple-element.11), channel_id=1, source_target_pairs={{0,2},{2,4},{4,6},{6,8},{8,10},{10,12},{12,14},{14,0},{1,3},{3,5},... | collective-permute-start | bytes 1572872 | tf_op jit(solution)/shard_map/ppermute | solution.py:35
  76.0 18.1 %copy-start.8 = (f32[512,512]{1,0:T(8,128)}, f32[512,512]{1,0:T(8,128)S(1)}, u32[]{:S(2)}) copy-start(f32[512,512]{1,0:T(8,128)S(1)} %collective-permute-done.9.rest_2_) | copy-start | bytes 3145732
  76.8 18.4 %collective-permute-start.16 = (f32[256,512]{1,0:T(8,128)S(1)}, f32[256,512]{1,0:T(8,128)S(1)}, u32[]{:S(2)}, u32[]{:S(2)}) collective-permute-start(f32[256,512]{1,0:T(8,128)S(1)} %get-tuple-element.13), channel_id=1, source_target_pairs={{0,14},{2,0},{4,2},{6,4},{8,6},{10,8},{12,10},{14,12},{1,15},{3,1}... | collective-permute-start | bytes 1572872 | tf_op jit(solution)/shard_map/ppermute | solution.py:35
  78.8 20.6 %collective-permute-start.13 = (f32[256,512]{1,0:T(8,128)S(1)}, f32[256,512]{1,0:T(8,128)S(1)}, u32[]{:S(2)}, u32[]{:S(2)}) collective-permute-start(f32[256,512]{1,0:T(8,128)S(1)} %get-tuple-element.12), channel_id=1, source_target_pairs={{0,2},{2,4},{4,6},{6,8},{8,10},{10,12},{12,14},{14,0},{1,3},{3,5},... | collective-permute-start | bytes 1572872 | tf_op jit(solution)/shard_map/ppermute | solution.py:35
  81.2 19.1 %collective-permute-start.12 = (f32[256,512]{1,0:T(8,128)S(1)}, f32[256,512]{1,0:T(8,128)S(1)}, u32[]{:S(2)}, u32[]{:S(2)}) collective-permute-start(f32[256,512]{1,0:T(8,128)S(1)} %get-tuple-element.14), channel_id=1, source_target_pairs={{0,14},{2,0},{4,2},{6,4},{8,6},{10,8},{12,10},{14,12},{1,15},{3,1}... | collective-permute-start | bytes 1572872 | tf_op jit(solution)/shard_map/ppermute | solution.py:35
  90.4 11.9 %collective-permute-start.7 = (f32[8,128,128]{2,1,0:T(8,128)S(1)}, f32[8,128,128]{2,1,0:T(8,128)S(1)}, u32[]{:S(2)}, u32[]{:S(2)}) collective-permute-start(f32[8,128,128]{2,1,0:T(8,128)S(1)} %add.34.refs_1_), channel_id=1, source_target_pairs={{0,16},{16,0},{1,17},{17,1},{2,18},{18,2},{3,19},{19,3},{4,20},{20... | collective-permute-start | bytes 1572872 | tf_op jit(solution)/shard_map/ppermute | solution.py:35
  94.2 8.2 %copy-start.10 = (f32[256,512]{1,0:T(8,128)}, f32[256,512]{1,0:T(8,128)S(1)}, u32[]{:S(2)}) copy-start(f32[256,512]{1,0:T(8,128)S(1)} %collective-permute-done.17.rest_8_) | copy-start | bytes 1572868
  94.2 10.3 %collective-permute-start.6 = (f32[8,128,128]{2,1,0:T(8,128)S(1)}, f32[8,128,128]{2,1,0:T(8,128)S(1)}, u32[]{:S(2)}, u32[]{:S(2)}) collective-permute-start(f32[8,128,128]{2,1,0:T(8,128)S(1)} %add.31.refs_0_), channel_id=1, source_target_pairs={{0,16},{16,0},{1,17},{17,1},{2,18},{18,2},{3,19},{19,3},{4,20},{20... | collective-permute-start | bytes 1572872 | tf_op jit(solution)/shard_map/ppermute | solution.py:35
  95.2 11.8 %copy-start.11 = (f32[256,512]{1,0:T(8,128)}, f32[256,512]{1,0:T(8,128)S(1)}, u32[]{:S(2)}) copy-start(f32[256,512]{1,0:T(8,128)S(1)} %collective-permute-done.16.rest_5_) | copy-start | bytes 1572868
  95.2 11.8 %collective-permute-start.18 = (f32[128,512]{1,0:T(8,128)}, f32[128,512]{1,0:T(8,128)S(1)}, u32[]{:S(2)}, u32[]{:S(2)}) collective-permute-start(f32[128,512]{1,0:T(8,128)} %slice.48), channel_id=1, source_target_pairs={{0,2},{2,4},{4,6},{6,8},{8,10},{10,12},{12,14},{14,0},{1,3},{3,5},... | collective-permute-start | bytes 786440 | tf_op jit(solution)/shard_map/ppermute | solution.py:35
  99.4 14.8 %copy-start.12 = (f32[256,512]{1,0:T(8,128)}, f32[256,512]{1,0:T(8,128)S(1)}, u32[]{:S(2)}) copy-start(f32[256,512]{1,0:T(8,128)S(1)} %collective-permute-done.13.rest_8_.rest_12_) | copy-start | bytes 1572868
  99.4 7.6 %collective-permute-start.19 = (f32[128,512]{1,0:T(8,128)}, f32[128,512]{1,0:T(8,128)}, u32[]{:S(2)}, u32[]{:S(2)}) collective-permute-start(f32[128,512]{1,0:T(8,128)} %slice.49), channel_id=1, source_target_pairs={{0,14},{2,0},{4,2},{6,4},{8,6},{10,8},{12,10},{14,12},{1,15},{3,1}... | collective-permute-start | bytes 786440 | tf_op jit(solution)/shard_map/ppermute | solution.py:35
  100.2 2.1 %copy-start.13 = (f32[256,512]{1,0:T(8,128)}, f32[256,512]{1,0:T(8,128)S(1)}, u32[]{:S(2)}) copy-start(f32[256,512]{1,0:T(8,128)S(1)} %collective-permute-done.12.rest_5_.rest_9_) | copy-start | bytes 1572868
  100.2 15.9 %collective-permute-start.14 = (f32[128,512]{1,0:T(8,128)}, f32[128,512]{1,0:T(8,128)}, u32[]{:S(2)}, u32[]{:S(2)}) collective-permute-start(f32[128,512]{1,0:T(8,128)} %slice.44), channel_id=1, source_target_pairs={{0,2},{2,4},{4,6},{6,8},{8,10},{10,12},{12,14},{14,0},{1,3},{3,5},... | collective-permute-start | bytes 786440 | tf_op jit(solution)/shard_map/ppermute | solution.py:35
  102.4 13.7 %collective-permute-start.15 = (f32[128,512]{1,0:T(8,128)}, f32[128,512]{1,0:T(8,128)}, u32[]{:S(2)}, u32[]{:S(2)}) collective-permute-start(f32[128,512]{1,0:T(8,128)} %slice.45), channel_id=1, source_target_pairs={{0,14},{2,0},{4,2},{6,4},{8,6},{10,8},{12,10},{14,12},{1,15},{3,1}... | collective-permute-start | bytes 786440 | tf_op jit(solution)/shard_map/ppermute | solution.py:35
  105.1 1.4 copy-start
  106.4 0.6 copy-start.3
  107.0 0.7 copy-start.14
  114.2 27.1 %collective-permute-start.20 = (f32[256,512]{1,0:T(8,128)}, f32[256,512]{1,0:T(8,128)S(1)}, u32[]{:S(2)}, u32[]{:S(2)}) collective-permute-start(f32[256,512]{1,0:T(8,128)} %beta.5), channel_id=1, source_target_pairs={{0,1},{1,0},{2,3},{3,2},{4,5},{5,4},{6,7},{7,6},{8,9},{9,8},{10,11... | collective-permute-start | bytes 1572872 | tf_op jit(solution)/shard_map/ppermute | solution.py:35
  122.5 25.5 %collective-permute-start.21 = (f32[256,512]{1,0:T(8,128)}, f32[256,512]{1,0:T(8,128)S(1)}, u32[]{:S(2)}, u32[]{:S(2)}) collective-permute-start(f32[256,512]{1,0:T(8,128)} %beta.3), channel_id=1, source_target_pairs={{0,1},{1,0},{2,3},{3,2},{4,5},{5,4},{6,7},{7,6},{8,9},{9,8},{10,11... | collective-permute-start | bytes 1572872 | tf_op jit(solution)/shard_map/ppermute | solution.py:35
Sparse Core Ops, SparseCore 0:
  9.2 120.3 all-gather.1

commit v4 on v2

--- a/solution.py
+++ b/solution.py
@@ -12,7 +12,7 @@
 ROW = ("yl", "x", "c")
 COL = ("z", "yh")
 B = 128
-VMEM_LIMIT = 56 * 1024 * 1024
+VMEM_LIMIT = 60 * 1024 * 1024
 
 
 def flat(yl, x, c, z, yh):
@@ -35,6 +35,14 @@
     return lax.ppermute(value, axis, [(i, (i + by) % n) for i in range(n)])
 
 
+def pair_values(pair_ids, used, integrals):
+    flat_table = integrals.reshape(-1)
+    onehot = pair_ids[:, :, None] == jnp.arange(flat_table.shape[0], dtype=jnp.int32)[None, None, :]
+    values = jnp.sum(jnp.where(onehot, flat_table[None, None, :], 0.0), axis=2)
+    in_use = jnp.arange(pair_ids.shape[1], dtype=jnp.int32)[None, :] < used[:, None]
+    return jnp.where(in_use, values, 0.0)
+
+
 def halves(value):
     high = value.astype(jnp.bfloat16)
     low = (value - high.astype(jnp.float32)).astype(jnp.bfloat16)
@@ -112,9 +120,9 @@
     )(place, links, counts, pairs, integrals, signs)
 
 
-def beta_kernel(place, links, counts, phases, sizes, *rest, spots):
+def beta_kernel(names, phases, sizes, *rest, spots):
     count = len(spots)
-    pieces, (out, held, names, left, sems) = rest[:count], rest[count:]
+    pieces, (out, held, sems) = rest[:count], rest[count:]
     rows = out.shape[0]
     copies = [
         pltpu.make_async_copy(piece.at[pl.ds(start, size), :], held.at[slot, pl.ds(to, size), :], sems.at[i])
@@ -122,94 +130,89 @@
     ]
     for copy in copies:
         copy.start()
-    z, yh, which = place[0], place[1], place[2]
-    first = (z * 2 + which) * 4
-    rank = jnp.int32(0)
-    for r in range(2 * FEW):
-        names[r] = 0
-    for i in range(4):
-        for l in range(8):
-            source = links[first + i, l]
-            used = (l < counts[first + i]) & (((source >> 2) & 1) == yh)
-
-            @pl.when(used)
-            def _(i=i, source=source, rank=rank):
-                names[jnp.minimum(rank, 2 * FEW - 1)] = source * 4 + i
-
-            rank = rank + used.astype(jnp.int32)
     out[...] = jnp.zeros_like(out)
     for copy in copies:
         copy.wait()
     for r in range(2 * FEW):
         name = names[r]
-        slot = ((name >> 5) - z) & 7
         lanes = pl.ds(pl.multiple_of(((name >> 2) & 3) * B, B), B)
         target = pl.ds(pl.multiple_of((name & 3) * B, B), B)
-        left[r % 2, :, :B], left[r % 2, :, B:] = halves(held[slot, :, lanes] * sizes[0, r:r + 1, :])
-        out[:, target] += jnp.dot(left[r % 2], phases[0, r], preferred_element_type=jnp.float32)
-
-
-def beta_part(place, links, counts, phases, sizes, rows, pieces, spots):
+        for start in range(0, rows, B):
+            tile = slice(start, start + B)
+            both = jnp.concatenate(halves(held[name >> 4, tile, lanes] * sizes[0, r:r + 1, :]), axis=1)
+            out[tile, target] += jnp.dot(both, phases[0, r], preferred_element_type=jnp.float32)
+
+
+def beta_names(links, counts, z, yh, which, c):
+    first = (z * 2 + which) * 4
+    source = lax.dynamic_slice_in_dim(links, first, 4).reshape(32)
+    block = jnp.arange(32, dtype=jnp.int32) // 8
+    link = jnp.arange(32, dtype=jnp.int32) % 8
+    limit = jnp.broadcast_to(lax.dynamic_slice_in_dim(counts, first, 4)[:, None], (4, 8)).reshape(32)
+    used = (link < limit) & (((source >> 2) & 1) == yh)
+    before = jnp.arange(32)[None, :] < jnp.arange(32)[:, None]
+    rank = jnp.sum(jnp.where(before & used[None, :], 1, 0), axis=1)
+    name = (((source >> 3) - z) & 7) * 16 + (source & 3) * 4 + block
+    at = used[None, :] & (rank[None, :] == jnp.arange(2 * FEW)[:, None])
+    names = jnp.sum(jnp.where(at, name[None, :], 0), axis=1)
+    return jnp.concatenate([names, (which ^ c)[None]]).astype(jnp.int32)
+
+
+def beta_part(names, phases, sizes, rows, pieces, spots):
     return pl.pallas_call(
         functools.partial(beta_kernel, spots=spots),
         out_shape=jax.ShapeDtypeStruct((rows, 4 * B), jnp.float32),
         grid_spec=pltpu.PrefetchScalarGridSpec(
-            num_scalar_prefetch=3,
+            num_scalar_prefetch=1,
             grid=(1,),
             in_specs=[
-                pl.BlockSpec((1, 2 * FEW, 2 * B, B), lambda i, place, *_: (place[3], 0, 0, 0), pipeline_mode=pl.Buffered(1)),
-                pl.BlockSpec((1, 2 * FEW, B), lambda i, place, *_: (place[3], 0, 0), pipeline_mode=pl.Buffered(1)),
+                pl.BlockSpec((1, 2 * FEW, 2 * B, B), lambda i, names: (names[2 * FEW], 0, 0, 0), pipeline_mode=pl.Buffered(1)),
+                pl.BlockSpec((1, 2 * FEW, B), lambda i, names: (names[2 * FEW], 0, 0), pipeline_mode=pl.Buffered(1)),
             ] + [pl.BlockSpec(memory_space=pl.ANY)] * len(spots),
             out_specs=pl.BlockSpec((rows, 4 * B), lambda i, *_: (0, 0), pipeline_mode=pl.Buffered(1)),
             scratch_shapes=[
                 pltpu.VMEM((8, rows, 4 * B), jnp.float32),
-                pltpu.SMEM((2 * FEW,), jnp.int32),
-                pltpu.VMEM((2, rows, 2 * B), jnp.bfloat16),
                 pltpu.SemaphoreType.DMA((len(spots),)),
             ],
         ),
-        compiler_params=pltpu.CompilerParams(dimension_semantics=("arbitrary",), vmem_limit_bytes=24 << 20),
+        compiler_params=pltpu.CompilerParams(dimension_semantics=("arbitrary",), vmem_limit_bytes=VMEM_LIMIT),
         cost_estimate=pl.CostEstimate(flops=16 * rows * B * 2 * B * 2, bytes_accessed=rows * 512 * 36 + (1 << 20), transcendentals=0),
         name="beta",
-    )(place, links, counts, phases, sizes, *pieces)
-
-
-def alpha_kernel(place, links, counts, pairs, integrals, signs, *rest):
-    tiles, (out, left, high, low) = rest[:8], rest[8:]
-    step = pl.program_id(0)
-    block = place[0] * 4 + step
-    for l in range(8):
-        pair = pairs[step, l]
-        coef = jnp.where(l < counts[block], integrals[pair >> 4, pair & 15], 0.0)
-        left[:, l * B:(l + 1) * B] = signs[0, l].astype(jnp.float32).astype(jnp.bfloat16)
-        high[l * B:(l + 1) * B, :], low[l * B:(l + 1) * B, :] = halves(tiles[l][0] * coef)
-    out[...] = jnp.dot(left[...], high[...], preferred_element_type=jnp.float32) + jnp.dot(
-        left[...], low[...], preferred_element_type=jnp.float32
-    )
-
-
-def alpha_part(place, links, counts, pairs, integrals, signs, column):
+    )(names, phases, sizes, *pieces)
+
+
+def alpha_kernel(blocks, coefs, signs, *rest):
+    tiles, (kept, out) = rest[:8], rest[8:]
+    coefs = [coefs[pl.program_id(0) * 8 + l] for l in range(8)]
+    phase = jnp.concatenate([signs[0, k].astype(jnp.float32).astype(jnp.bfloat16) for k in range(8)], axis=1)
+    for half in range(2):
+        lanes = slice(half * 2 * B, (half + 1) * 2 * B)
+        parts = [halves(tiles[k][0, :, lanes] * coefs[k]) for k in range(8)]
+        right = jnp.concatenate([pair[0] for pair in parts], axis=0)
+        total = kept[:, lanes] + jnp.dot(phase, right, preferred_element_type=jnp.float32)
+        right = jnp.concatenate([pair[1] for pair in parts], axis=0)
+        out[:, lanes] = total + jnp.dot(phase, right, preferred_element_type=jnp.float32)
+
+
+def alpha_part(blocks, coefs, signs, column, kept):
     def tile(l):
-        return pl.BlockSpec((1, B, 4 * B), lambda i, place, links, *_: (links[place[0] * 4 + i, l], 0, 0))
+        return pl.BlockSpec((1, B, 4 * B), lambda i, blocks, _: (blocks[i * 8 + l], 0, 0))
 
     return pl.pallas_call(
         alpha_kernel,
         out_shape=jax.ShapeDtypeStruct((4 * B, 4 * B), jnp.float32),
         grid_spec=pltpu.PrefetchScalarGridSpec(
-            num_scalar_prefetch=5,
+            num_scalar_prefetch=2,
             grid=(4,),
-            in_specs=[pl.BlockSpec((1, 8, B, B), lambda i, *_: (i, 0, 0, 0))] + [tile(l) for l in range(8)],
+            in_specs=[pl.BlockSpec((1, 8, B, B), lambda i, *_: (i, 0, 0, 0))] + [tile(l) for l in range(8)] + [
+                pl.BlockSpec((B, 4 * B), lambda i, *_: (i, 0)),
+            ],
             out_specs=pl.BlockSpec((B, 4 * B), lambda i, *_: (i, 0)),
-            scratch_shapes=[
-                pltpu.VMEM((B, 8 * B), jnp.bfloat16),
-                pltpu.VMEM((8 * B, 4 * B), jnp.bfloat16),
-                pltpu.VMEM((8 * B, 4 * B), jnp.bfloat16),
-            ],
         ),
         compiler_params=pltpu.CompilerParams(dimension_semantics=("arbitrary",), vmem_limit_bytes=VMEM_LIMIT),
-        cost_estimate=pl.CostEstimate(flops=4 * 4 * B * B * 16 * B * 2, bytes_accessed=11 << 20, transcendentals=0),
+        cost_estimate=pl.CostEstimate(flops=4 * 4 * B * B * 16 * B * 2, bytes_accessed=14 << 20, transcendentals=0),
         name="alpha",
-    )(place, links, counts, pairs, integrals, signs, *[column] * 8)
+    )(blocks, coefs, signs, *[column] * 8, kept)
 
 
 HALF = 2 * B
@@ -221,9 +224,15 @@
     column = lax.all_gather(vector, ROW, axis=0, tiled=True).reshape(64, B, 4 * B)
 
     up, down = [vector], [vector]
-    for _ in range(2):
-        up.append(shift(up[-1], "z", 1))
-        down.append(shift(down[-1], "z", -1))
+    theirs, ours = (beta_names(links, counts, z, yh, which, c) for which in (1 - yh, yh))
+    local_counts = lax.dynamic_slice_in_dim(counts, row_index * 4, 4)
+    coefs = pair_values(pairs, local_counts, one_electron).reshape(32)
+    blocks = lax.dynamic_slice_in_dim(links, row_index * 4, 4).reshape(32)
+    up.append(shift(vector, "z", 1))
+    down.append(shift(vector, "z", -1))
+    (theirs, ours, coefs, blocks), up[1] = lax.optimization_barrier(((theirs, ours, coefs, blocks), up[1]))
+    up.append(shift(up[-1], "z", 1))
+    down.append(shift(down[-1], "z", -1))
     near = [vector, down[1], down[2], up[2], up[1]]
     chunks = []
     for n in range(2):
@@ -251,17 +260,14 @@
     second += spread(second, [(o, yo), (p, yp), (q, yq), (r, yr)])
     phases, sizes = prepare_beta(first, second, shift(first, "c", 1), shift(second, "c", 1))
 
-    theirs, ours = (jnp.stack([z, yh, which, (which ^ c)]).astype(jnp.int32) for which in (1 - yh, yh))
-    tables = (links, counts, phases, sizes)
+    tables = (phases, sizes)
     partial = [
         beta_part(theirs, *tables, HALF, near + chunks[n], near_spots(n * HALF, HALF) + far_spots(0)) for n in range(2)
     ]
     sent = [shift(value, "yh", 1) for value in partial]
     ours, _ = lax.optimization_barrier((ours, partial[1]))
     kept = beta_part(ours, *tables, 2 * HALF, near + chunks[0] + chunks[1], near_spots(0, 2 * HALF) + far_spots(0) + far_spots(HALF))
-    place, _ = lax.optimization_barrier((row_index[None].astype(jnp.int32), partial[1]))
-    alpha = alpha_part(place, links, counts, pairs, one_electron, signs, column)
-    return alpha + kept + jnp.concatenate(sent, axis=0)
+    return alpha_part(blocks, coefs, signs, column, kept) + jnp.concatenate(sent, axis=0)
 
 
 def solution(mesh):

time: 173 us -> 158 us (0.913)
  the two profiles are of different devices: /device:TPU:4 before, /device:TPU:1 now
where the time goes in v4:
time: 158 us; the launch traced here: 157 us
  waiting for transfers between devices  51.9 us (33%)
  starting transfers between devices  45.1 us (29%)
  Pallas kernels  29.3 us (19%)
  between operations  13.8 us (9%)
  local copies, waits for them, and re-layouts  12.1 us (8%)
  other arithmetic  5.05 us (3%)
    ppermute x16, starting transfers between devices, shift(): return lax.ppermute(value, axis, [(i, (i + by) % n) for i in range(n)])  32.8 us
    ppermute x6, waiting for transfers between devices, spread(): return lax.ppermute(value, AXES, pairs)  30 us
    pallas_call x3, Pallas kernels, beta_part(): pl.pallas_call(functools.partial(beta_kernel, spots=spots), out_shape=jax...  19.2 us
    ppermute x16, waiting for transfers between devices, shift(): return lax.ppermute(value, axis, [(i, (i + by) % n) for i in range(n)])  19.2 us
    ppermute x6, starting transfers between devices, spread(): return lax.ppermute(value, AXES, pairs)  12.3 us
    unnamed x41, local copies, waits for them, and re-layouts  9.29 us
    pallas_call x1, Pallas kernels, alpha_part(): pl.pallas_call(alpha_kernel, out_shape=jax.ShapeDtypeStruct((4 * B, 4 * B...  7.8 us
  transfers between devices with their start and end apart: 23, of which 9 were waited for; matrix products, arithmetic and copies ran while one was open for 4% of the time, Pallas kernels for 19%

profile of v4, /device:TPU:1, one launch (start us, length us, event | category | flops | bytes accessed | tf_op | source)
XLA Modules:
  0.0 157.2 jit_solution(5667183126692287085)
XLA Ops:
  6.5 0.7 all-gather.2.cloned.1.call-update
  7.3 2.5 %collective-permute-start = (f32[512,512]{1,0:T(8,128)}, f32[512,512]{1,0:T(8,128)}, u32[]{:S(2)}, u32[]{:S(2)}) collective-permute-start(f32[512,512]{1,0:T(8,128)} %rest_0_.5), channel_id=1, source_target_pairs={{0,2},{2,4},{4,6},{6,8},{8,10},{10,12},{12,14},{14,0},{1,3},{3,5},... | collective-permute-start | bytes 3145736 | tf_op jit(solution)/shard_map/ppermute | solution.py:35
  9.8 4.0 %collective-permute-start.9 = (f32[512,512]{1,0:T(8,128)}, f32[512,512]{1,0:T(8,128)}, u32[]{:S(2)}, u32[]{:S(2)}) collective-permute-start(f32[512,512]{1,0:T(8,128)} %rest_0_.5), channel_id=1, source_target_pairs={{0,14},{2,0},{4,2},{6,4},{8,6},{10,8},{12,10},{14,12},{1,15},{3,1}... | collective-permute-start | bytes 3145736 | tf_op jit(solution)/shard_map/ppermute | solution.py:35
  13.8 0.8 copy.18.links
  14.7 1.6 %copy-done.1 = s32[4,8,128,128]{3,2,1,0:T(8,128)S(1)} copy-done((s32[4,8,128,128]{3,2,1,0:T(8,128)S(1)}, s32[4,8,128,128]{3,2,1,0:T(8,128)}, u32[]{:S(2)}) %copy-start.1) | copy-done | bytes 2097176
  16.3 0.7 copy-done.3
  17.0 0.7 copy-done.5
  17.7 0.7 copy-done.7
  18.3 1.7 %pack.1 = f32[16,128,128]{2,1,0:T(8,128)S(1)} custom-call(s32[3]{0:T(128)S(1)} %pad_add_fusion.2.place, s32[64,8]{1,0:T(8,128)S(1)} %copy.18.links, s32[64]{0:T(128)S(1)} %copy-done.7, s32[4,8]{1,0:T(4,128)S(1)} %copy-done.5, f32[16,16]{1,0:T(8,128)S(1)} %copy-done.3, s32[4,8,128,128]{3,2,1,0:T(8,128)S(1)} %copy-done.1), custom_call_target="tpu_custom_call" | custom-call | flops 524288 | bytes 3145728 | tf_op jit(solution)/shard_map/pack/pallas_call | solution.py:112
  20.1 2.8 %collective-permute-start.1 = (f32[8,128,128]{2,1,0:T(8,128)S(1)}, f32[8,128,128]{2,1,0:T(8,128)S(1)}, u32[]{:S(2)}, u32[]{:S(2)}) collective-permute-start(f32[8,128,128]{2,1,0:T(8,128)S(1)} %get-tuple-element.28), channel_id=1, source_target_pairs={{0,128},{16,144},{1,129},{17,145},{34,162},{50,178},{35,163},{51,1... | collective-permute-start | bytes 1572872 | tf_op jit(solution)/shard_map/ppermute | solution.py:30
  23.0 1.3 collective-permute-start.4
  26.1 0.6 reshape.148.blocks
  26.8 0.6 select_n.82.coefs
  27.6 0.6 pad_add_fusion.1.names
  28.4 0.7 pad_add_fusion.names
  29.0 7.9 %collective-permute-done.rest_4_ = f32[512,512]{1,0:T(8,128)} collective-permute-done((f32[512,512]{1,0:T(8,128)}, f32[512,512]{1,0:T(8,128)}, u32[]{:S(2)}, u32[]{:S(2)}) %collective-permute-start) | collective-permute-done | bytes 1048608 | tf_op jit(solution)/shard_map/ppermute | solution.py:35
  36.9 2.7 %collective-permute-start.10 = (f32[512,512]{1,0:T(8,128)}, f32[512,512]{1,0:T(8,128)S(1)}, u32[]{:S(2)}, u32[]{:S(2)}) collective-permute-start(f32[512,512]{1,0:T(8,128)} %collective-permute-done.9.rest_1_), channel_id=1, source_target_pairs={{0,14},{2,0},{4,2},{6,4},{8,6},{10,8},{12,10},{14,12},{1,15},{3,1}... | collective-permute-start | bytes 3145736 | tf_op jit(solution)/shard_map/ppermute | solution.py:35
  39.6 2.0 %collective-permute-done.1 = f32[8,128,128]{2,1,0:T(8,128)S(1)} collective-permute-done((f32[8,128,128]{2,1,0:T(8,128)S(1)}, f32[8,128,128]{2,1,0:T(8,128)S(1)}, u32[]{:S(2)}, u32[]{:S(2)}) %collective-permute-start.1) | collective-permute-done | bytes 524320 | tf_op jit(solution)/shard_map/ppermute | solution.py:30
  41.6 4.9 %collective-permute-done.4 = f32[8,128,128]{2,1,0:T(8,128)S(1)} collective-permute-done((f32[8,128,128]{2,1,0:T(8,128)S(1)}, f32[8,128,128]{2,1,0:T(8,128)S(1)}, u32[]{:S(2)}, u32[]{:S(2)}) %collective-permute-start.4) | collective-permute-done | bytes 524320 | tf_op jit(solution)/shard_map/ppermute | solution.py:30
  46.6 1.3 collective-permute-start.5
  47.9 4.2 %collective-permute-start.2 = (f32[8,128,128]{2,1,0:T(8,128)S(1)}, f32[8,128,128]{2,1,0:T(8,128)S(1)}, u32[]{:S(2)}, u32[]{:S(2)}) collective-permute-start(f32[8,128,128]{2,1,0:T(8,128)S(1)} %get-tuple-element.26), channel_id=1, source_target_pairs={{0,32},{128,160},{16,48},{144,176},{1,33},{129,161},{17,49},{145,1... | collective-permute-start | bytes 1572872 | tf_op jit(solution)/shard_map/ppermute | solution.py:30
  52.2 5.5 %collective-permute-done.5 = f32[8,128,128]{2,1,0:T(8,128)S(1)} collective-permute-done((f32[8,128,128]{2,1,0:T(8,128)S(1)}, f32[8,128,128]{2,1,0:T(8,128)S(1)}, u32[]{:S(2)}, u32[]{:S(2)}) %collective-permute-start.5) | collective-permute-done | bytes 524320 | tf_op jit(solution)/shard_map/ppermute | solution.py:30
  57.8 1.3 collective-permute-start.6
  59.1 15.3 %collective-permute-done.2 = f32[8,128,128]{2,1,0:T(8,128)S(1)} collective-permute-done((f32[8,128,128]{2,1,0:T(8,128)S(1)}, f32[8,128,128]{2,1,0:T(8,128)S(1)}, u32[]{:S(2)}, u32[]{:S(2)}) %collective-permute-start.2) | collective-permute-done | bytes 524320 | tf_op jit(solution)/shard_map/ppermute | solution.py:30
  74.5 1.3 collective-permute-start.3
  76.1 0.7 copy-done.9
  76.8 2.0 %collective-permute-start.16 = (f32[256,512]{1,0:T(8,128)S(1)}, f32[256,512]{1,0:T(8,128)S(1)}, u32[]{:S(2)}, u32[]{:S(2)}) collective-permute-start(f32[256,512]{1,0:T(8,128)S(1)} %get-tuple-element.23), channel_id=1, source_target_pairs={{0,14},{2,0},{4,2},{6,4},{8,6},{10,8},{12,10},{14,12},{1,15},{3,1}... | collective-permute-start | bytes 1572872 | tf_op jit(solution)/shard_map/ppermute | solution.py:35
  78.8 2.4 %collective-permute-done.6 = f32[8,128,128]{2,1,0:T(8,128)S(1)} collective-permute-done((f32[8,128,128]{2,1,0:T(8,128)S(1)}, f32[8,128,128]{2,1,0:T(8,128)S(1)}, u32[]{:S(2)}, u32[]{:S(2)}) %collective-permute-start.6) | collective-permute-done | bytes 524320 | tf_op jit(solution)/shard_map/ppermute | solution.py:30
  81.2 9.2 %collective-permute-start.12 = (f32[256,512]{1,0:T(8,128)S(1)}, f32[256,512]{1,0:T(8,128)S(1)}, u32[]{:S(2)}, u32[]{:S(2)}) collective-permute-start(f32[256,512]{1,0:T(8,128)S(1)} %get-tuple-element.24), channel_id=1, source_target_pairs={{0,14},{2,0},{4,2},{6,4},{8,6},{10,8},{12,10},{14,12},{1,15},{3,1}... | collective-permute-start | bytes 1572872 | tf_op jit(solution)/shard_map/ppermute | solution.py:35
  90.5 3.7 %collective-permute-start.8 = (f32[8,128,128]{2,1,0:T(8,128)S(1)}, f32[8,128,128]{2,1,0:T(8,128)S(1)}, u32[]{:S(2)}, u32[]{:S(2)}) collective-permute-start(f32[8,128,128]{2,1,0:T(8,128)S(1)} %add.115.refs_1_), channel_id=1, source_target_pairs={{0,16},{16,0},{1,17},{17,1},{2,18},{18,2},{3,19},{19,3},{4,20},{20... | collective-permute-start | bytes 1572872 | tf_op jit(solution)/shard_map/ppermute | solution.py:35
  94.5 2.2 %collective-permute-start.18 = (f32[128,512]{1,0:T(8,128)S(1)}, f32[128,512]{1,0:T(8,128)S(1)}, u32[]{:S(2)}, u32[]{:S(2)}) collective-permute-start(f32[128,512]{1,0:T(8,128)S(1)} %slice.48), channel_id=1, source_target_pairs={{0,2},{2,4},{4,6},{6,8},{8,10},{10,12},{12,14},{14,0},{1,3},{3,5},... | collective-permute-start | bytes 786440 | tf_op jit(solution)/shard_map/ppermute | solution.py:35
  96.7 2.8 %collective-permute-done.13.rest_8_.rest_12_ = f32[256,512]{1,0:T(8,128)S(1)} collective-permute-done((f32[256,512]{1,0:T(8,128)S(1)}, f32[256,512]{1,0:T(8,128)S(1)}, u32[]{:S(2)}, u32[]{:S(2)}) %collective-permute-start.13) | collective-permute-done | bytes 524320 | tf_op jit(solution)/shard_map/ppermute | solution.py:35
  99.5 1.7 %collective-permute-start.14 = (f32[128,512]{1,0:T(8,128)S(1)}, f32[128,512]{1,0:T(8,128)S(1)}, u32[]{:S(2)}, u32[]{:S(2)}) collective-permute-start(f32[128,512]{1,0:T(8,128)S(1)} %slice.44), channel_id=1, source_target_pairs={{0,2},{2,4},{4,6},{6,8},{8,10},{10,12},{12,14},{14,0},{1,3},{3,5},... | collective-permute-start | bytes 786440 | tf_op jit(solution)/shard_map/ppermute | solution.py:35
  101.2 1.3 collective-permute-start.15
  103.1 1.3 copy-done
  104.5 0.6 copy-done.2
  105.1 0.7 copy-done.15
  105.9 5.7 %beta.5 = f32[256,512]{1,0:T(8,128)} custom-call(s32[17]{0:T(128)} %pad_add_fusion.names, bf16[2,16,256,128]{3,2,1,0:T(8,128)(2,1)} %copy-done, f32[2,16,128]{2,1,0:T(8,128)} %copy-done.2, f32[512,512]{1,0:T(8,128)} %rest_0_.5, f32[512,512]{1,0:T(8,128)} %collective-permute-done.9.rest_1_, f32[512,512]{1,0:T(8,128)} %copy-done.10, f32[512,512]{1,0:T(8,128)} %copy-done.9, ...), custom_call_target="tpu_custom_call" | custom-call | flops 268435456 | bytes 5767168 | tf_op jit(solution)/shard_map/beta/pallas_call | solution.py:162
  111.6 2.3 %collective-permute-start.20 = (f32[256,512]{1,0:T(8,128)}, f32[256,512]{1,0:T(8,128)S(1)}, u32[]{:S(2)}, u32[]{:S(2)}) collective-permute-start(f32[256,512]{1,0:T(8,128)} %beta.5), channel_id=1, source_target_pairs={{0,1},{1,0},{2,3},{3,2},{4,5},{5,4},{6,7},{7,6},{8,9},{9,8},{10,11... | collective-permute-start | bytes 1572872 | tf_op jit(solution)/shard_map/ppermute | solution.py:35
  114.0 0.7 copy-done.17
  114.7 0.7 copy-done.18
  115.4 5.7 %beta.3 = f32[256,512]{1,0:T(8,128)} custom-call(s32[17]{0:T(128)} %pad_add_fusion.names, bf16[2,16,256,128]{3,2,1,0:T(8,128)(2,1)} %copy-done, f32[2,16,128]{2,1,0:T(8,128)} %copy-done.2, f32[512,512]{1,0:T(8,128)} %rest_0_.5, f32[512,512]{1,0:T(8,128)} %collective-permute-done.9.rest_1_, f32[512,512]{1,0:T(8,128)} %copy-done.10, f32[512,512]{1,0:T(8,128)} %copy-done.9, ...), custom_call_target="tpu_custom_call" | custom-call | flops 268435456 | bytes 5767168 | tf_op jit(solution)/shard_map/beta/pallas_call | solution.py:162
  121.1 0.8 collective-permute-start.21
  121.9 7.7 %beta.4.rest_8_ = f32[512,512]{1,0:T(8,128)} custom-call(s32[17]{0:T(128)} %pad_add_fusion.1.names, bf16[2,16,256,128]{3,2,1,0:T(8,128)(2,1)} %copy-done, f32[2,16,128]{2,1,0:T(8,128)} %copy-done.2, f32[512,512]{1,0:T(8,128)} %rest_0_.5, f32[512,512]{1,0:T(8,128)} %collective-permute-done.9.rest_1_, f32[512,512]{1,0:T(8,128)} %copy-done.10, ...), custom_call_target="tpu_custom_call" | custom-call | flops 536870912 | bytes 10485760 | tf_op jit(solution)/shard_map/beta/pallas_call | solution.py:162
  129.7 1.9 %all-gather.2.cloned.1.call-done = f32[8192,512]{1,0:T(8,128)} async-done(((f32[512,512]{1,0:T(8,128)}), f32[8192,512]{1,0:T(8,128)}) %all-gather.2.cloned.1.call-update) | async-done | bytes 16777232 | tf_op jit(solution)/shard_map/all_gather | solution.py:224
  131.6 7.8 %alpha.1 = f32[512,512]{1,0:T(8,128)} custom-call(s32[32]{0:T(128)} %reshape.148.blocks, f32[32]{0:T(128)} %select_n.82.coefs, s32[4,8,128,128]{3,2,1,0:T(8,128)} %signs.3, f32[64,128,512]{2,1,0:T(8,128)} %bitcast.6, f32[64,128,512]{2,1,0:T(8,128)} %bitcast.7, f32[64,128,512]{2,1,0:T(8,128)} %bitcast.8, f32[64,128,512]{2,1,0:T(8,128)} %bitcast.9, ...), custom_call_target="tpu_custom_call" | custom-call | flops 1073741824 | bytes 14680064 | tf_op jit(solution)/shard_map/alpha/pallas_call | solution.py:201
  139.4 8.5 %collective-permute-done.21 = f32[256,512]{1,0:T(8,128)S(1)} collective-permute-done((f32[256,512]{1,0:T(8,128)}, f32[256,512]{1,0:T(8,128)S(1)}, u32[]{:S(2)}, u32[]{:S(2)}) %collective-permute-start.21) | collective-permute-done | bytes 524320 | tf_op jit(solution)/shard_map/ppermute | solution.py:35
  147.9 2.4 %maximum_add_fusion = f32[512,512]{1,0:T(8,128)} fusion(f32[512,512]{1,0:T(8,128)} %alpha.1, f32[256,512]{1,0:T(8,128)S(1)} %collective-permute-done.21, f32[256,512]{1,0:T(8,128)S(1)} %collective-permute-done.20), kind=kLoop, calls=%fused_computation | loop fusion | flops 524288 | bytes 3145728 | tf_op jit(solution)/shard_map/add | solution.py:270
  (89 shorter events, 3.9 us)
Async XLA Ops:
  6.5 125.1 %all-gather.2.cloned.1.call-start = ((), (), s32[]{:S(2)}) async-start(), calls=%async_computation | async-start | bytes 17825792 | tf_op jit(solution)/shard_map/all_gather | solution.py:224
  7.3 29.7 %collective-permute-start = (f32[512,512]{1,0:T(8,128)}, f32[512,512]{1,0:T(8,128)}, u32[]{:S(2)}, u32[]{:S(2)}) collective-permute-start(f32[512,512]{1,0:T(8,128)} %rest_0_.5), channel_id=1, source_target_pairs={{0,2},{2,4},{4,6},{6,8},{8,10},{10,12},{12,14},{14,0},{1,3},{3,5},... | collective-permute-start | bytes 3145736 | tf_op jit(solution)/shard_map/ppermute | solution.py:35
  9.8 27.1 %collective-permute-start.9 = (f32[512,512]{1,0:T(8,128)}, f32[512,512]{1,0:T(8,128)}, u32[]{:S(2)}, u32[]{:S(2)}) collective-permute-start(f32[512,512]{1,0:T(8,128)} %rest_0_.5), channel_id=1, source_target_pairs={{0,14},{2,0},{4,2},{6,4},{8,6},{10,8},{12,10},{14,12},{1,15},{3,1}... | collective-permute-start | bytes 3145736 | tf_op jit(solution)/shard_map/ppermute | solution.py:35
  14.7 1.6 %copy-start.1 = (s32[4,8,128,128]{3,2,1,0:T(8,128)S(1)}, s32[4,8,128,128]{3,2,1,0:T(8,128)}, u32[]{:S(2)}) copy-start(s32[4,8,128,128]{3,2,1,0:T(8,128)} %signs.3) | copy-start | bytes 6291460
  16.3 0.7 copy-start.3
  17.0 0.7 copy-start.5
  17.6 0.7 copy-start.7
  18.3 6.0 %copy-start.4 = (f32[16,16]{1,0:T(8,128)S(1)}, f32[16,16]{1,0:T(8,128)}, u32[]{:S(2)}) copy-start(f32[16,16]{1,0:T(8,128)} %integrals.1) | copy-start | bytes 3076
  18.3 6.1 %copy-start.8 = (s32[64]{0:T(128)S(1)}, s32[64]{0:T(128)}, u32[]{:S(2)}) copy-start(s32[64]{0:T(128)} %counts.1) | copy-start | bytes 772
  18.3 6.5 %copy-start.19 = (s32[64,8]{0,1:T(8,128)S(1)}, s32[64,8]{0,1:T(8,128)}, u32[]{:S(2)}) copy-start(s32[64,8]{0,1:T(8,128)} %param.8) | copy-start | bytes 6148
  18.3 6.9 %copy-start.6 = (s32[4,8]{1,0:T(4,128)S(1)}, s32[4,8]{1,0:T(4,128)}, u32[]{:S(2)}) copy-start(s32[4,8]{1,0:T(4,128)} %pairs.1) | copy-start | bytes 388
  20.1 21.4 %collective-permute-start.1 = (f32[8,128,128]{2,1,0:T(8,128)S(1)}, f32[8,128,128]{2,1,0:T(8,128)S(1)}, u32[]{:S(2)}, u32[]{:S(2)}) collective-permute-start(f32[8,128,128]{2,1,0:T(8,128)S(1)} %get-tuple-element.28), channel_id=1, source_target_pairs={{0,128},{16,144},{1,129},{17,145},{34,162},{50,178},{35,163},{51,1... | collective-permute-start | bytes 1572872 | tf_op jit(solution)/shard_map/ppermute | solution.py:30
  23.0 23.5 %collective-permute-start.4 = (f32[8,128,128]{2,1,0:T(8,128)S(1)}, f32[8,128,128]{2,1,0:T(8,128)S(1)}, u32[]{:S(2)}, u32[]{:S(2)}) collective-permute-start(f32[8,128,128]{2,1,0:T(8,128)S(1)} %get-tuple-element.27), channel_id=1, source_target_pairs={{0,32},{16,48},{1,33},{17,49},{34,66},{50,82},{35,67},{51,83},{68,... | collective-permute-start | bytes 1572872 | tf_op jit(solution)/shard_map/ppermute | solution.py:30
  36.9 38.9 %collective-permute-start.11 = (f32[512,512]{1,0:T(8,128)}, f32[512,512]{1,0:T(8,128)S(1)}, u32[]{:S(2)}, u32[]{:S(2)}) collective-permute-start(f32[512,512]{1,0:T(8,128)} %collective-permute-done.rest_4_), channel_id=1, source_target_pairs={{0,2},{2,4},{4,6},{6,8},{8,10},{10,12},{12,14},{14,0},{1,3},{3,5},... | collective-permute-start | bytes 3145736 | tf_op jit(solution)/shard_map/ppermute | solution.py:35
  36.9 39.0 %collective-permute-start.10 = (f32[512,512]{1,0:T(8,128)}, f32[512,512]{1,0:T(8,128)S(1)}, u32[]{:S(2)}, u32[]{:S(2)}) collective-permute-start(f32[512,512]{1,0:T(8,128)} %collective-permute-done.9.rest_1_), channel_id=1, source_target_pairs={{0,14},{2,0},{4,2},{6,4},{8,6},{10,8},{12,10},{14,12},{1,15},{3,1}... | collective-permute-start | bytes 3145736 | tf_op jit(solution)/shard_map/ppermute | solution.py:35
  46.6 11.1 %collective-permute-start.5 = (f32[8,128,128]{2,1,0:T(8,128)S(1)}, f32[8,128,128]{2,1,0:T(8,128)S(1)}, u32[]{:S(2)}, u32[]{:S(2)}) collective-permute-start(f32[8,128,128]{2,1,0:T(8,128)S(1)} %get-tuple-element.25), channel_id=1, source_target_pairs={{0,96},{32,64},{16,112},{48,80},{1,97},{33,65},{17,113},{49,81},{3... | collective-permute-start | bytes 1572872 | tf_op jit(solution)/shard_map/ppermute | solution.py:30
  47.9 26.5 %collective-permute-start.2 = (f32[8,128,128]{2,1,0:T(8,128)S(1)}, f32[8,128,128]{2,1,0:T(8,128)S(1)}, u32[]{:S(2)}, u32[]{:S(2)}) collective-permute-start(f32[8,128,128]{2,1,0:T(8,128)S(1)} %get-tuple-element.26), channel_id=1, source_target_pairs={{0,32},{128,160},{16,48},{144,176},{1,33},{129,161},{17,49},{145,1... | collective-permute-start | bytes 1572872 | tf_op jit(solution)/shard_map/ppermute | solution.py:30
  57.8 23.4 %collective-permute-start.6 = (f32[8,128,128]{2,1,0:T(8,128)S(1)}, f32[8,128,128]{2,1,0:T(8,128)S(1)}, u32[]{:S(2)}, u32[]{:S(2)}) collective-permute-start(f32[8,128,128]{2,1,0:T(8,128)S(1)} %add.114), channel_id=1, source_target_pairs={{0,128},{32,160},{64,192},{96,224},{16,144},{48,176},{80,208},{112... | collective-permute-start | bytes 1572872 | tf_op jit(solution)/shard_map/ppermute | solution.py:30
  74.5 16.0 %collective-permute-start.3 = (f32[8,128,128]{2,1,0:T(8,128)S(1)}, f32[8,128,128]{2,1,0:T(8,128)S(1)}, u32[]{:S(2)}, u32[]{:S(2)}) collective-permute-start(f32[8,128,128]{2,1,0:T(8,128)S(1)} %add.111), channel_id=1, source_target_pairs={{0,96},{128,224},{32,64},{160,192},{16,112},{144,240},{48,80},{176... | collective-permute-start | bytes 1572872 | tf_op jit(solution)/shard_map/ppermute | solution.py:30
  75.8 1.0 copy-start.9
  75.9 18.4 %collective-permute-start.17 = (f32[256,512]{1,0:T(8,128)S(1)}, f32[256,512]{1,0:T(8,128)S(1)}, u32[]{:S(2)}, u32[]{:S(2)}) collective-permute-start(f32[256,512]{1,0:T(8,128)S(1)} %get-tuple-element.21), channel_id=1, source_target_pairs={{0,2},{2,4},{4,6},{6,8},{8,10},{10,12},{12,14},{14,0},{1,3},{3,5},... | collective-permute-start | bytes 1572872 | tf_op jit(solution)/shard_map/ppermute | solution.py:35
  76.0 18.3 %copy-start.10 = (f32[512,512]{1,0:T(8,128)}, f32[512,512]{1,0:T(8,128)S(1)}, u32[]{:S(2)}) copy-start(f32[512,512]{1,0:T(8,128)S(1)} %collective-permute-done.10.rest_2_) | copy-start | bytes 3145732
  76.8 17.6 %collective-permute-start.16 = (f32[256,512]{1,0:T(8,128)S(1)}, f32[256,512]{1,0:T(8,128)S(1)}, u32[]{:S(2)}, u32[]{:S(2)}) collective-permute-start(f32[256,512]{1,0:T(8,128)S(1)} %get-tuple-element.23), channel_id=1, source_target_pairs={{0,14},{2,0},{4,2},{6,4},{8,6},{10,8},{12,10},{14,12},{1,15},{3,1}... | collective-permute-start | bytes 1572872 | tf_op jit(solution)/shard_map/ppermute | solution.py:35
  78.8 20.6 %collective-permute-start.13 = (f32[256,512]{1,0:T(8,128)S(1)}, f32[256,512]{1,0:T(8,128)S(1)}, u32[]{:S(2)}, u32[]{:S(2)}) collective-permute-start(f32[256,512]{1,0:T(8,128)S(1)} %get-tuple-element.22), channel_id=1, source_target_pairs={{0,2},{2,4},{4,6},{6,8},{8,10},{10,12},{12,14},{14,0},{1,3},{3,5},... | collective-permute-start | bytes 1572872 | tf_op jit(solution)/shard_map/ppermute | solution.py:35
  81.2 18.3 %collective-permute-start.12 = (f32[256,512]{1,0:T(8,128)S(1)}, f32[256,512]{1,0:T(8,128)S(1)}, u32[]{:S(2)}, u32[]{:S(2)}) collective-permute-start(f32[256,512]{1,0:T(8,128)S(1)} %get-tuple-element.24), channel_id=1, source_target_pairs={{0,14},{2,0},{4,2},{6,4},{8,6},{10,8},{12,10},{14,12},{1,15},{3,1}... | collective-permute-start | bytes 1572872 | tf_op jit(solution)/shard_map/ppermute | solution.py:35
  90.5 10.7 %collective-permute-start.8 = (f32[8,128,128]{2,1,0:T(8,128)S(1)}, f32[8,128,128]{2,1,0:T(8,128)S(1)}, u32[]{:S(2)}, u32[]{:S(2)}) collective-permute-start(f32[8,128,128]{2,1,0:T(8,128)S(1)} %add.115.refs_1_), channel_id=1, source_target_pairs={{0,16},{16,0},{1,17},{17,1},{2,18},{18,2},{3,19},{19,3},{4,20},{20... | collective-permute-start | bytes 1572872 | tf_op jit(solution)/shard_map/ppermute | solution.py:35
  94.3 8.9 %copy-start.11 = (f32[256,512]{1,0:T(8,128)}, f32[256,512]{1,0:T(8,128)S(1)}, u32[]{:S(2)}) copy-start(f32[256,512]{1,0:T(8,128)S(1)} %collective-permute-done.17.rest_8_) | copy-start | bytes 1572868
  94.3 8.3 %collective-permute-start.7 = (f32[8,128,128]{2,1,0:T(8,128)S(1)}, f32[8,128,128]{2,1,0:T(8,128)S(1)}, u32[]{:S(2)}, u32[]{:S(2)}) collective-permute-start(f32[8,128,128]{2,1,0:T(8,128)S(1)} %add.112.refs_0_), channel_id=1, source_target_pairs={{0,16},{16,0},{1,17},{17,1},{2,18},{18,2},{3,19},{19,3},{4,20},{20... | collective-permute-start | bytes 1572872 | tf_op jit(solution)/shard_map/ppermute | solution.py:35
  94.5 10.6 %copy-start.12 = (f32[256,512]{1,0:T(8,128)}, f32[256,512]{1,0:T(8,128)S(1)}, u32[]{:S(2)}) copy-start(f32[256,512]{1,0:T(8,128)S(1)} %collective-permute-done.16.rest_5_) | copy-start | bytes 1572868
  94.5 10.6 %collective-permute-start.18 = (f32[128,512]{1,0:T(8,128)S(1)}, f32[128,512]{1,0:T(8,128)S(1)}, u32[]{:S(2)}, u32[]{:S(2)}) collective-permute-start(f32[128,512]{1,0:T(8,128)S(1)} %slice.48), channel_id=1, source_target_pairs={{0,2},{2,4},{4,6},{6,8},{8,10},{10,12},{12,14},{14,0},{1,3},{3,5},... | collective-permute-start | bytes 786440 | tf_op jit(solution)/shard_map/ppermute | solution.py:35
  99.4 12.2 %copy-start.13 = (f32[256,512]{1,0:T(8,128)}, f32[256,512]{1,0:T(8,128)S(1)}, u32[]{:S(2)}) copy-start(f32[256,512]{1,0:T(8,128)S(1)} %collective-permute-done.13.rest_8_.rest_12_) | copy-start | bytes 1572868
  99.5 5.6 %collective-permute-start.19 = (f32[128,512]{1,0:T(8,128)S(1)}, f32[128,512]{1,0:T(8,128)S(1)}, u32[]{:S(2)}, u32[]{:S(2)}) collective-permute-start(f32[128,512]{1,0:T(8,128)S(1)} %slice.49), channel_id=1, source_target_pairs={{0,14},{2,0},{4,2},{6,4},{8,6},{10,8},{12,10},{14,12},{1,15},{3,1}... | collective-permute-start | bytes 786440 | tf_op jit(solution)/shard_map/ppermute | solution.py:35
  99.5 12.1 %copy-start.14 = (f32[256,512]{1,0:T(8,128)}, f32[256,512]{1,0:T(8,128)S(1)}, u32[]{:S(2)}) copy-start(f32[256,512]{1,0:T(8,128)S(1)} %collective-permute-done.12.rest_5_.rest_9_) | copy-start | bytes 1572868
  99.5 14.5 %collective-permute-start.14 = (f32[128,512]{1,0:T(8,128)S(1)}, f32[128,512]{1,0:T(8,128)S(1)}, u32[]{:S(2)}, u32[]{:S(2)}) collective-permute-start(f32[128,512]{1,0:T(8,128)S(1)} %slice.44), channel_id=1, source_target_pairs={{0,2},{2,4},{4,6},{6,8},{8,10},{10,12},{12,14},{14,0},{1,3},{3,5},... | collective-permute-start | bytes 786440 | tf_op jit(solution)/shard_map/ppermute | solution.py:35
  101.2 12.7 %collective-permute-start.15 = (f32[128,512]{1,0:T(8,128)S(1)}, f32[128,512]{1,0:T(8,128)S(1)}, u32[]{:S(2)}, u32[]{:S(2)}) collective-permute-start(f32[128,512]{1,0:T(8,128)S(1)} %slice.45), channel_id=1, source_target_pairs={{0,14},{2,0},{4,2},{6,4},{8,6},{10,8},{12,10},{14,12},{1,15},{3,1}... | collective-permute-start | bytes 786440 | tf_op jit(solution)/shard_map/ppermute | solution.py:35
  103.1 1.4 copy-start
  104.5 0.6 copy-start.2
  105.1 0.7 copy-start.15
  105.1 0.8 copy-start.16
  111.6 27.8 %collective-permute-start.20 = (f32[256,512]{1,0:T(8,128)}, f32[256,512]{1,0:T(8,128)S(1)}, u32[]{:S(2)}, u32[]{:S(2)}) collective-permute-start(f32[256,512]{1,0:T(8,128)} %beta.5), channel_id=1, source_target_pairs={{0,1},{1,0},{2,3},{3,2},{4,5},{5,4},{6,7},{7,6},{8,9},{9,8},{10,11... | collective-permute-start | bytes 1572872 | tf_op jit(solution)/shard_map/ppermute | solution.py:35
  114.0 0.7 copy-start.17
  114.7 0.7 copy-start.18
  121.1 26.8 %collective-permute-start.21 = (f32[256,512]{1,0:T(8,128)}, f32[256,512]{1,0:T(8,128)S(1)}, u32[]{:S(2)}, u32[]{:S(2)}) collective-permute-start(f32[256,512]{1,0:T(8,128)} %beta.3), channel_id=1, source_target_pairs={{0,1},{1,0},{2,3},{3,2},{4,5},{5,4},{6,7},{7,6},{8,9},{9,8},{10,11... | collective-permute-start | bytes 1572872 | tf_op jit(solution)/shard_map/ppermute | solution.py:35
Sparse Core Ops, SparseCore 0:
  9.2 122.3 all-gather.1

commit v5 on v4

--- a/solution.py
+++ b/solution.py
@@ -79,12 +79,13 @@
 FEW = 8
 
 
-def pack_kernel(place, links, counts, pairs, integrals, signs, out):
+def pack_kernel(place, links, counts, pairs, integrals, signs, *outs):
     first, is_source, yh = place[0] * 4, place[1] == 1, place[2]
 
     @pl.when(jnp.logical_not(is_source))
     def _():
-        out[...] = jnp.zeros_like(out)
+        for out in outs:
+            out[...] = jnp.zeros_like(out)
 
     @pl.when(is_source)
     def _():
@@ -93,27 +94,31 @@
             for l in range(8):
                 used = (l < counts[first + i]) & (((links[first + i, l] >> 2) & 1) == yh)
 
-                @pl.when(used)
-                def _(i=i, l=l, rank=rank):
-                    pair = pairs[i, l]
-                    out[jnp.minimum(rank, 2 * FEW - 1)] = signs[i, l].astype(jnp.float32) * integrals[pair >> 4, pair & 15]
+                for half, out in enumerate(outs):
+
+                    @pl.when(used & (rank // FEW == half))
+                    def _(i=i, l=l, rank=rank, half=half, out=out):
+                        pair = pairs[i, l]
+                        out[rank - half * FEW] = signs[i, l].astype(jnp.float32) * integrals[pair >> 4, pair & 15]
 
                 rank = rank + used.astype(jnp.int32)
 
-        def clear(i, carry):
-            out[i] = jnp.zeros((B, B), jnp.float32)
-            return carry
-
-        lax.fori_loop(rank, 2 * FEW, clear, 0)
+        for half, out in enumerate(outs):
+
+            def clear(i, carry, out=out):
+                out[i] = jnp.zeros((B, B), jnp.float32)
+                return carry
+
+            lax.fori_loop(jnp.clip(rank - half * FEW, 0, FEW), FEW, clear, 0)
 
 
 def pack(place, links, counts, pairs, integrals, signs):
     scalar = pl.BlockSpec(memory_space=pltpu.SMEM)
     return pl.pallas_call(
         pack_kernel,
-        out_shape=jax.ShapeDtypeStruct((2 * FEW, B, B), jnp.float32),
+        out_shape=[jax.ShapeDtypeStruct((FEW, B, B), jnp.float32)] * 2,
         in_specs=[scalar] * 5 + [pl.BlockSpec(memory_space=pltpu.VMEM)],
-        out_specs=pl.BlockSpec(memory_space=pltpu.VMEM),
+        out_specs=[pl.BlockSpec(memory_space=pltpu.VMEM)] * 2,
         compiler_params=pltpu.CompilerParams(vmem_limit_bytes=16 << 20),
         cost_estimate=pl.CostEstimate(flops=32 * B * B, bytes_accessed=48 * B * B * 4, transcendentals=0),
         name="pack",
@@ -248,8 +253,7 @@
         return [(3, 0, to, HALF), (4, 0, to, HALF // 2), (4, 0, to + HALF // 2, HALF // 2), (5, 0, to, HALF)]
 
     is_source = (yl == z >> 2) & (x == z & 3)
-    packed = pack(jnp.stack([row_index, is_source.astype(jnp.int32), yh]), links, counts, pairs, one_electron, signs)
-    first, second = packed[:FEW], packed[FEW:]
+    first, second = pack(jnp.stack([row_index, is_source.astype(jnp.int32), yh]), links, counts, pairs, one_electron, signs)
     o, p, q, r = (0, 0), (0, 1), (0, 2), (0, 3)
     yo, yp, yq, yr = (1, 0), (1, 1), (1, 2), (1, 3)
     first += spread(first, [(o, yo)])

time: 158 us -> 159 us (level)
  waiting for transfers between devices: 51.9 us -> 44.1 us
  starting transfers between devices: 45.1 us -> 52 us
  other arithmetic: 5.05 us -> 7.16 us
    ppermute x16, starting transfers between devices: 32.8 us -> 39.7 us  [shift(): return lax.ppermute(value, axis, [(i, (i + by) % n) for i in range(n)])]
    ppermute x6, waiting for transfers between devices: 30 us -> 24.4 us  [spread(): return lax.ppermute(value, AXES, pairs)]
    ppermute x16, waiting for transfers between devices: 19.2 us -> 17.2 us  [shift(): return lax.ppermute(value, axis, [(i, (i + by) % n) for i in range(n)])]
  transfers between devices with their start and end apart: 23 -> 23, of which waited for: 9 -> 10; matrix products, arithmetic and copies ran while one was open for 4% -> 5% of each run, Pallas kernels for 19% -> 19%
where the time goes in v5:
time: 159 us; the launch traced here: 158 us
  starting transfers between devices  52 us (33%)
  waiting for transfers between devices  44.1 us (28%)
  Pallas kernels  29.5 us (19%)
  between operations  13.7 us (9%)
  local copies, waits for them, and re-layouts  11.9 us (7%)
  other arithmetic  7.16 us (5%)
    ppermute x16, starting transfers between devices, shift(): return lax.ppermute(value, axis, [(i, (i + by) % n) for i in range(n)])  39.7 us
    ppermute x6, waiting for transfers between devices, spread(): return lax.ppermute(value, AXES, pairs)  24.4 us
    pallas_call x3, Pallas kernels, beta_part(): pl.pallas_call(functools.partial(beta_kernel, spots=spots), out_shape=jax...  19.2 us
    ppermute x16, waiting for transfers between devices, shift(): return lax.ppermute(value, axis, [(i, (i + by) % n) for i in range(n)])  17.2 us
    ppermute x6, starting transfers between devices, spread(): return lax.ppermute(value, AXES, pairs)  12.2 us
    unnamed x41, local copies, waits for them, and re-layouts  9.22 us
    pallas_call x1, Pallas kernels, alpha_part(): pl.pallas_call(alpha_kernel, out_shape=jax.ShapeDtypeStruct((4 * B, 4 * B...  7.77 us
  transfers between devices with their start and end apart: 23, of which 10 were waited for; matrix products, arithmetic and copies ran while one was open for 5% of the time, Pallas kernels for 19%

profile of v5, /device:TPU:1, one launch (start us, length us, event | category | flops | bytes accessed | tf_op | source)
XLA Modules:
  0.0 158.5 jit_solution(7019984324080004865)
XLA Ops:
  6.6 0.7 all-gather.2.cloned.1.call-update
  7.3 2.5 %collective-permute-start = (f32[512,512]{1,0:T(8,128)}, f32[512,512]{1,0:T(8,128)}, u32[]{:S(2)}, u32[]{:S(2)}) collective-permute-start(f32[512,512]{1,0:T(8,128)} %rest_0_.5), channel_id=1, source_target_pairs={{0,2},{2,4},{4,6},{6,8},{8,10},{10,12},{12,14},{14,0},{1,3},{3,5},... | collective-permute-start | bytes 3145736 | tf_op jit(solution)/shard_map/ppermute | solution.py:35
  9.8 4.0 %collective-permute-start.9 = (f32[512,512]{1,0:T(8,128)}, f32[512,512]{1,0:T(8,128)}, u32[]{:S(2)}, u32[]{:S(2)}) collective-permute-start(f32[512,512]{1,0:T(8,128)} %rest_0_.5), channel_id=1, source_target_pairs={{0,14},{2,0},{4,2},{6,4},{8,6},{10,8},{12,10},{14,12},{1,15},{3,1}... | collective-permute-start | bytes 3145736 | tf_op jit(solution)/shard_map/ppermute | solution.py:35
  13.8 0.8 copy.18.links
  14.7 1.6 %copy-done.1 = s32[4,8,128,128]{3,2,1,0:T(8,128)S(1)} copy-done((s32[4,8,128,128]{3,2,1,0:T(8,128)S(1)}, s32[4,8,128,128]{3,2,1,0:T(8,128)}, u32[]{:S(2)}) %copy-start.1) | copy-done | bytes 2097176
  16.3 0.7 copy-done.3
  17.0 0.7 copy-done.5
  17.7 0.7 copy-done.7
  18.3 2.0 %pack.1 = (f32[8,128,128]{2,1,0:T(8,128)S(1)}, f32[8,128,128]{2,1,0:T(8,128)S(1)}) custom-call(s32[3]{0:T(128)S(1)} %pad_add_fusion.2.place, s32[64,8]{1,0:T(8,128)S(1)} %copy.18.links, s32[64]{0:T(128)S(1)} %copy-done.7, s32[4,8]{1,0:T(4,128)S(1)} %copy-done.5, f32[16,16]{1,0:T(8,128)S(1)} %copy-done.3, s32[4,8,128,128]{3,2,1,0:T(8,128)S(1)} %copy-done.1), custom_call_target="tpu_custom_call" | custom-call | flops 524288 | bytes 3145728 | tf_op jit(solution)/shard_map/pack/pallas_call | solution.py:117
  20.3 3.3 %collective-permute-start.4 = (f32[8,128,128]{2,1,0:T(8,128)S(1)}, f32[8,128,128]{2,1,0:T(8,128)}, u32[]{:S(2)}, u32[]{:S(2)}) collective-permute-start(f32[8,128,128]{2,1,0:T(8,128)S(1)} %get-tuple-element.20), channel_id=1, source_target_pairs={{0,32},{16,48},{1,33},{17,49},{34,66},{50,82},{35,67},{51,83},{68,... | collective-permute-start | bytes 1572872 | tf_op jit(solution)/shard_map/ppermute | solution.py:30
  23.6 2.1 %collective-permute-start.1 = (f32[8,128,128]{2,1,0:T(8,128)S(1)}, f32[8,128,128]{2,1,0:T(8,128)}, u32[]{:S(2)}, u32[]{:S(2)}) collective-permute-start(f32[8,128,128]{2,1,0:T(8,128)S(1)} %get-tuple-element.19), channel_id=1, source_target_pairs={{0,128},{16,144},{1,129},{17,145},{34,162},{50,178},{35,163},{51,1... | collective-permute-start | bytes 1572872 | tf_op jit(solution)/shard_map/ppermute | solution.py:30
  27.3 0.6 pad_add_fusion.1.names
  28.1 0.6 pad_add_fusion.names
  29.0 0.6 reshape.148.blocks
  29.7 0.6 select_n.82.coefs
  30.3 6.7 %collective-permute-done.rest_4_ = f32[512,512]{1,0:T(8,128)} collective-permute-done((f32[512,512]{1,0:T(8,128)}, f32[512,512]{1,0:T(8,128)}, u32[]{:S(2)}, u32[]{:S(2)}) %collective-permute-start) | collective-permute-done | bytes 1048608 | tf_op jit(solution)/shard_map/ppermute | solution.py:35
  37.0 2.7 %collective-permute-start.10 = (f32[512,512]{1,0:T(8,128)}, f32[512,512]{1,0:T(8,128)S(1)}, u32[]{:S(2)}, u32[]{:S(2)}) collective-permute-start(f32[512,512]{1,0:T(8,128)} %collective-permute-done.9.rest_1_), channel_id=1, source_target_pairs={{0,14},{2,0},{4,2},{6,4},{8,6},{10,8},{12,10},{14,12},{1,15},{3,1}... | collective-permute-start | bytes 3145736 | tf_op jit(solution)/shard_map/ppermute | solution.py:35
  39.6 1.5 collective-permute-done.4
  41.1 1.2 add.113
  42.3 2.9 %collective-permute-start.5 = (f32[8,128,128]{2,1,0:T(8,128)S(1)}, f32[8,128,128]{2,1,0:T(8,128)S(1)}, u32[]{:S(2)}, u32[]{:S(2)}) collective-permute-start(f32[8,128,128]{2,1,0:T(8,128)S(1)} %add.113), channel_id=1, source_target_pairs={{0,96},{32,64},{16,112},{48,80},{1,97},{33,65},{17,113},{49,81},{3... | collective-permute-start | bytes 1572872 | tf_op jit(solution)/shard_map/ppermute | solution.py:30
  45.2 1.9 %collective-permute-done.1 = f32[8,128,128]{2,1,0:T(8,128)} collective-permute-done((f32[8,128,128]{2,1,0:T(8,128)S(1)}, f32[8,128,128]{2,1,0:T(8,128)}, u32[]{:S(2)}, u32[]{:S(2)}) %collective-permute-start.1) | collective-permute-done | bytes 524320 | tf_op jit(solution)/shard_map/ppermute | solution.py:30
  47.1 1.1 add.110
  48.2 1.3 collective-permute-start.2
  49.5 3.9 %collective-permute-done.5 = f32[8,128,128]{2,1,0:T(8,128)S(1)} collective-permute-done((f32[8,128,128]{2,1,0:T(8,128)S(1)}, f32[8,128,128]{2,1,0:T(8,128)S(1)}, u32[]{:S(2)}, u32[]{:S(2)}) %collective-permute-start.5) | collective-permute-done | bytes 524320 | tf_op jit(solution)/shard_map/ppermute | solution.py:30
  53.5 1.3 collective-permute-start.6
  54.9 16.0 %collective-permute-done.2 = f32[8,128,128]{2,1,0:T(8,128)S(1)} collective-permute-done((f32[8,128,128]{2,1,0:T(8,128)S(1)}, f32[8,128,128]{2,1,0:T(8,128)S(1)}, u32[]{:S(2)}, u32[]{:S(2)}) %collective-permute-start.2) | collective-permute-done | bytes 524320 | tf_op jit(solution)/shard_map/ppermute | solution.py:30
  71.0 1.3 collective-permute-start.3
  72.6 0.7 copy-done.9
  73.3 2.0 %collective-permute-start.16 = (f32[256,512]{1,0:T(8,128)S(1)}, f32[256,512]{1,0:T(8,128)S(1)}, u32[]{:S(2)}, u32[]{:S(2)}) collective-permute-start(f32[256,512]{1,0:T(8,128)S(1)} %get-tuple-element.27), channel_id=1, source_target_pairs={{0,14},{2,0},{4,2},{6,4},{8,6},{10,8},{12,10},{14,12},{1,15},{3,1}... | collective-permute-start | bytes 1572872 | tf_op jit(solution)/shard_map/ppermute | solution.py:35
  75.3 1.1 collective-permute-done.6
  76.4 15.0 %collective-permute-start.12 = (f32[256,512]{1,0:T(8,128)S(1)}, f32[256,512]{1,0:T(8,128)S(1)}, u32[]{:S(2)}, u32[]{:S(2)}) collective-permute-start(f32[256,512]{1,0:T(8,128)S(1)} %get-tuple-element.28), channel_id=1, source_target_pairs={{0,14},{2,0},{4,2},{6,4},{8,6},{10,8},{12,10},{14,12},{1,15},{3,1}... | collective-permute-start | bytes 1572872 | tf_op jit(solution)/shard_map/ppermute | solution.py:35
  91.5 3.7 %collective-permute-start.8 = (f32[8,128,128]{2,1,0:T(8,128)S(1)}, f32[8,128,128]{2,1,0:T(8,128)S(1)}, u32[]{:S(2)}, u32[]{:S(2)}) collective-permute-start(f32[8,128,128]{2,1,0:T(8,128)S(1)} %add.115.refs_1_), channel_id=1, source_target_pairs={{0,16},{16,0},{1,17},{17,1},{2,18},{18,2},{3,19},{19,3},{4,20},{20... | collective-permute-start | bytes 1572872 | tf_op jit(solution)/shard_map/ppermute | solution.py:35
  95.4 2.3 %collective-permute-start.18 = (f32[128,512]{1,0:T(8,128)S(1)}, f32[128,512]{1,0:T(8,128)S(1)}, u32[]{:S(2)}, u32[]{:S(2)}) collective-permute-start(f32[128,512]{1,0:T(8,128)S(1)} %slice.38), channel_id=1, source_target_pairs={{0,2},{2,4},{4,6},{6,8},{8,10},{10,12},{12,14},{14,0},{1,3},{3,5},... | collective-permute-start | bytes 786440 | tf_op jit(solution)/shard_map/ppermute | solution.py:35
  98.3 1.0 collective-permute-done.12.rest_5_.rest_9_
  99.6 3.2 %collective-permute-start.15 = (f32[128,512]{1,0:T(8,128)S(1)}, f32[128,512]{1,0:T(8,128)S(1)}, u32[]{:S(2)}, u32[]{:S(2)}) collective-permute-start(f32[128,512]{1,0:T(8,128)S(1)} %slice.35), channel_id=1, source_target_pairs={{0,14},{2,0},{4,2},{6,4},{8,6},{10,8},{12,10},{14,12},{1,15},{3,1}... | collective-permute-start | bytes 786440 | tf_op jit(solution)/shard_map/ppermute | solution.py:35
  102.9 0.6 prepare_beta.1
  103.5 1.4 copy-done
  104.8 0.6 copy-done.2
  106.3 5.7 %beta.5 = f32[256,512]{1,0:T(8,128)} custom-call(s32[17]{0:T(128)} %pad_add_fusion.names, bf16[2,16,256,128]{3,2,1,0:T(8,128)(2,1)} %copy-done, f32[2,16,128]{2,1,0:T(8,128)} %copy-done.2, f32[512,512]{1,0:T(8,128)} %rest_0_.5, f32[512,512]{1,0:T(8,128)} %collective-permute-done.9.rest_1_, f32[512,512]{1,0:T(8,128)} %copy-done.10, f32[512,512]{1,0:T(8,128)} %copy-done.9, ...), custom_call_target="tpu_custom_call" | custom-call | flops 268435456 | bytes 5767168 | tf_op jit(solution)/shard_map/beta/pallas_call | solution.py:167
  112.0 3.2 %collective-permute-start.20 = (f32[256,512]{1,0:T(8,128)}, f32[256,512]{1,0:T(8,128)S(1)}, u32[]{:S(2)}, u32[]{:S(2)}) collective-permute-start(f32[256,512]{1,0:T(8,128)} %beta.5), channel_id=1, source_target_pairs={{0,1},{1,0},{2,3},{3,2},{4,5},{5,4},{6,7},{7,6},{8,9},{9,8},{10,11... | collective-permute-start | bytes 1572872 | tf_op jit(solution)/shard_map/ppermute | solution.py:35
  115.2 0.7 copy-done.17
  115.9 0.7 copy-done.18
  116.6 5.7 %beta.3 = f32[256,512]{1,0:T(8,128)} custom-call(s32[17]{0:T(128)} %pad_add_fusion.names, bf16[2,16,256,128]{3,2,1,0:T(8,128)(2,1)} %copy-done, f32[2,16,128]{2,1,0:T(8,128)} %copy-done.2, f32[512,512]{1,0:T(8,128)} %rest_0_.5, f32[512,512]{1,0:T(8,128)} %collective-permute-done.9.rest_1_, f32[512,512]{1,0:T(8,128)} %copy-done.10, f32[512,512]{1,0:T(8,128)} %copy-done.9, ...), custom_call_target="tpu_custom_call" | custom-call | flops 268435456 | bytes 5767168 | tf_op jit(solution)/shard_map/beta/pallas_call | solution.py:167
  122.5 7.8 %beta.4.rest_8_ = f32[512,512]{1,0:T(8,128)} custom-call(s32[17]{0:T(128)} %pad_add_fusion.1.names, bf16[2,16,256,128]{3,2,1,0:T(8,128)(2,1)} %copy-done, f32[2,16,128]{2,1,0:T(8,128)} %copy-done.2, f32[512,512]{1,0:T(8,128)} %rest_0_.5, f32[512,512]{1,0:T(8,128)} %collective-permute-done.9.rest_1_, f32[512,512]{1,0:T(8,128)} %copy-done.10, ...), custom_call_target="tpu_custom_call" | custom-call | flops 536870912 | bytes 10485760 | tf_op jit(solution)/shard_map/beta/pallas_call | solution.py:167
  130.2 1.9 %all-gather.2.cloned.1.call-done = f32[8192,512]{1,0:T(8,128)} async-done(((f32[512,512]{1,0:T(8,128)}), f32[8192,512]{1,0:T(8,128)}) %all-gather.2.cloned.1.call-update) | async-done | bytes 16777232 | tf_op jit(solution)/shard_map/all_gather | solution.py:229
  132.1 7.8 %alpha.1 = f32[512,512]{1,0:T(8,128)} custom-call(s32[32]{0:T(128)} %reshape.148.blocks, f32[32]{0:T(128)} %select_n.82.coefs, s32[4,8,128,128]{3,2,1,0:T(8,128)} %signs.3, f32[64,128,512]{2,1,0:T(8,128)} %bitcast.6, f32[64,128,512]{2,1,0:T(8,128)} %bitcast.7, f32[64,128,512]{2,1,0:T(8,128)} %bitcast.8, f32[64,128,512]{2,1,0:T(8,128)} %bitcast.9, ...), custom_call_target="tpu_custom_call" | custom-call | flops 1073741824 | bytes 14680064 | tf_op jit(solution)/shard_map/alpha/pallas_call | solution.py:206
  139.9 9.3 %collective-permute-done.21 = f32[256,512]{1,0:T(8,128)S(1)} collective-permute-done((f32[256,512]{1,0:T(8,128)}, f32[256,512]{1,0:T(8,128)S(1)}, u32[]{:S(2)}, u32[]{:S(2)}) %collective-permute-start.21) | collective-permute-done | bytes 524320 | tf_op jit(solution)/shard_map/ppermute | solution.py:35
  149.2 2.4 %maximum_add_fusion = f32[512,512]{1,0:T(8,128)} fusion(f32[512,512]{1,0:T(8,128)} %alpha.1, f32[256,512]{1,0:T(8,128)S(1)} %collective-permute-done.21, f32[256,512]{1,0:T(8,128)S(1)} %collective-permute-done.20), kind=kLoop, calls=%fused_computation | loop fusion | flops 524288 | bytes 3145728 | tf_op jit(solution)/shard_map/add | solution.py:274
  (89 shorter events, 4.8 us)
Async XLA Ops:
  6.5 19.5 %copy-start.19 = (s32[64,8]{0,1:T(8,128)S(1)}, s32[64,8]{0,1:T(8,128)}, u32[]{:S(2)}) copy-start(s32[64,8]{0,1:T(8,128)} %param.8) | copy-start | bytes 6148
  6.5 22.2 %copy-start.6 = (s32[4,8]{1,0:T(4,128)S(1)}, s32[4,8]{1,0:T(4,128)}, u32[]{:S(2)}) copy-start(s32[4,8]{1,0:T(4,128)} %pairs.1) | copy-start | bytes 388
  6.5 20.4 %copy-start.4 = (f32[16,16]{1,0:T(8,128)S(1)}, f32[16,16]{1,0:T(8,128)}, u32[]{:S(2)}) copy-start(f32[16,16]{1,0:T(8,128)} %integrals.1) | copy-start | bytes 3076
  6.5 19.1 %copy-start.8 = (s32[64]{0:T(128)S(1)}, s32[64]{0:T(128)}, u32[]{:S(2)}) copy-start(s32[64]{0:T(128)} %counts.1) | copy-start | bytes 772
  6.5 125.5 %all-gather.2.cloned.1.call-start = ((), (), s32[]{:S(2)}) async-start(), calls=%async_computation | async-start | bytes 17825792 | tf_op jit(solution)/shard_map/all_gather | solution.py:229
  7.3 29.7 %collective-permute-start = (f32[512,512]{1,0:T(8,128)}, f32[512,512]{1,0:T(8,128)}, u32[]{:S(2)}, u32[]{:S(2)}) collective-permute-start(f32[512,512]{1,0:T(8,128)} %rest_0_.5), channel_id=1, source_target_pairs={{0,2},{2,4},{4,6},{6,8},{8,10},{10,12},{12,14},{14,0},{1,3},{3,5},... | collective-permute-start | bytes 3145736 | tf_op jit(solution)/shard_map/ppermute | solution.py:35
  9.8 27.1 %collective-permute-start.9 = (f32[512,512]{1,0:T(8,128)}, f32[512,512]{1,0:T(8,128)}, u32[]{:S(2)}, u32[]{:S(2)}) collective-permute-start(f32[512,512]{1,0:T(8,128)} %rest_0_.5), channel_id=1, source_target_pairs={{0,14},{2,0},{4,2},{6,4},{8,6},{10,8},{12,10},{14,12},{1,15},{3,1}... | collective-permute-start | bytes 3145736 | tf_op jit(solution)/shard_map/ppermute | solution.py:35
  14.7 1.6 %copy-start.1 = (s32[4,8,128,128]{3,2,1,0:T(8,128)S(1)}, s32[4,8,128,128]{3,2,1,0:T(8,128)}, u32[]{:S(2)}) copy-start(s32[4,8,128,128]{3,2,1,0:T(8,128)} %signs.3) | copy-start | bytes 6291460
  16.3 0.7 copy-start.3
  17.0 0.7 copy-start.5
  17.7 0.7 copy-start.7
  20.3 20.8 %collective-permute-start.4 = (f32[8,128,128]{2,1,0:T(8,128)S(1)}, f32[8,128,128]{2,1,0:T(8,128)}, u32[]{:S(2)}, u32[]{:S(2)}) collective-permute-start(f32[8,128,128]{2,1,0:T(8,128)S(1)} %get-tuple-element.20), channel_id=1, source_target_pairs={{0,32},{16,48},{1,33},{17,49},{34,66},{50,82},{35,67},{51,83},{68,... | collective-permute-start | bytes 1572872 | tf_op jit(solution)/shard_map/ppermute | solution.py:30
  23.6 23.5 %collective-permute-start.1 = (f32[8,128,128]{2,1,0:T(8,128)S(1)}, f32[8,128,128]{2,1,0:T(8,128)}, u32[]{:S(2)}, u32[]{:S(2)}) collective-permute-start(f32[8,128,128]{2,1,0:T(8,128)S(1)} %get-tuple-element.19), channel_id=1, source_target_pairs={{0,128},{16,144},{1,129},{17,145},{34,162},{50,178},{35,163},{51,1... | collective-permute-start | bytes 1572872 | tf_op jit(solution)/shard_map/ppermute | solution.py:30
  37.0 35.3 %collective-permute-start.11 = (f32[512,512]{1,0:T(8,128)}, f32[512,512]{1,0:T(8,128)S(1)}, u32[]{:S(2)}, u32[]{:S(2)}) collective-permute-start(f32[512,512]{1,0:T(8,128)} %collective-permute-done.rest_4_), channel_id=1, source_target_pairs={{0,2},{2,4},{4,6},{6,8},{8,10},{10,12},{12,14},{14,0},{1,3},{3,5},... | collective-permute-start | bytes 3145736 | tf_op jit(solution)/shard_map/ppermute | solution.py:35
  37.0 35.5 %collective-permute-start.10 = (f32[512,512]{1,0:T(8,128)}, f32[512,512]{1,0:T(8,128)S(1)}, u32[]{:S(2)}, u32[]{:S(2)}) collective-permute-start(f32[512,512]{1,0:T(8,128)} %collective-permute-done.9.rest_1_), channel_id=1, source_target_pairs={{0,14},{2,0},{4,2},{6,4},{8,6},{10,8},{12,10},{14,12},{1,15},{3,1}... | collective-permute-start | bytes 3145736 | tf_op jit(solution)/shard_map/ppermute | solution.py:35
  42.3 11.1 %collective-permute-start.5 = (f32[8,128,128]{2,1,0:T(8,128)S(1)}, f32[8,128,128]{2,1,0:T(8,128)S(1)}, u32[]{:S(2)}, u32[]{:S(2)}) collective-permute-start(f32[8,128,128]{2,1,0:T(8,128)S(1)} %add.113), channel_id=1, source_target_pairs={{0,96},{32,64},{16,112},{48,80},{1,97},{33,65},{17,113},{49,81},{3... | collective-permute-start | bytes 1572872 | tf_op jit(solution)/shard_map/ppermute | solution.py:30
  48.2 22.7 %collective-permute-start.2 = (f32[8,128,128]{2,1,0:T(8,128)S(1)}, f32[8,128,128]{2,1,0:T(8,128)S(1)}, u32[]{:S(2)}, u32[]{:S(2)}) collective-permute-start(f32[8,128,128]{2,1,0:T(8,128)S(1)} %add.110), channel_id=1, source_target_pairs={{0,32},{128,160},{16,48},{144,176},{1,33},{129,161},{17,49},{145,1... | collective-permute-start | bytes 1572872 | tf_op jit(solution)/shard_map/ppermute | solution.py:30
  53.5 22.9 %collective-permute-start.6 = (f32[8,128,128]{2,1,0:T(8,128)S(1)}, f32[8,128,128]{2,1,0:T(8,128)S(1)}, u32[]{:S(2)}, u32[]{:S(2)}) collective-permute-start(f32[8,128,128]{2,1,0:T(8,128)S(1)} %add.114), channel_id=1, source_target_pairs={{0,128},{32,160},{64,192},{96,224},{16,144},{48,176},{80,208},{112... | collective-permute-start | bytes 1572872 | tf_op jit(solution)/shard_map/ppermute | solution.py:30
  71.0 20.5 %collective-permute-start.3 = (f32[8,128,128]{2,1,0:T(8,128)S(1)}, f32[8,128,128]{2,1,0:T(8,128)S(1)}, u32[]{:S(2)}, u32[]{:S(2)}) collective-permute-start(f32[8,128,128]{2,1,0:T(8,128)S(1)} %add.111), channel_id=1, source_target_pairs={{0,96},{128,224},{32,64},{160,192},{16,112},{144,240},{48,80},{176... | collective-permute-start | bytes 1572872 | tf_op jit(solution)/shard_map/ppermute | solution.py:30
  72.3 1.0 copy-start.9
  72.4 22.9 %collective-permute-start.17 = (f32[256,512]{1,0:T(8,128)S(1)}, f32[256,512]{1,0:T(8,128)S(1)}, u32[]{:S(2)}, u32[]{:S(2)}) collective-permute-start(f32[256,512]{1,0:T(8,128)S(1)} %get-tuple-element.25), channel_id=1, source_target_pairs={{0,2},{2,4},{4,6},{6,8},{8,10},{10,12},{12,14},{14,0},{1,3},{3,5},... | collective-permute-start | bytes 1572872 | tf_op jit(solution)/shard_map/ppermute | solution.py:35
  72.5 22.8 %copy-start.10 = (f32[512,512]{1,0:T(8,128)}, f32[512,512]{1,0:T(8,128)S(1)}, u32[]{:S(2)}) copy-start(f32[512,512]{1,0:T(8,128)S(1)} %collective-permute-done.10.rest_2_) | copy-start | bytes 3145732
  73.3 22.1 %collective-permute-start.16 = (f32[256,512]{1,0:T(8,128)S(1)}, f32[256,512]{1,0:T(8,128)S(1)}, u32[]{:S(2)}, u32[]{:S(2)}) collective-permute-start(f32[256,512]{1,0:T(8,128)S(1)} %get-tuple-element.27), channel_id=1, source_target_pairs={{0,14},{2,0},{4,2},{6,4},{8,6},{10,8},{12,10},{14,12},{1,15},{3,1}... | collective-permute-start | bytes 1572872 | tf_op jit(solution)/shard_map/ppermute | solution.py:35
  75.3 22.4 %collective-permute-start.13 = (f32[256,512]{1,0:T(8,128)S(1)}, f32[256,512]{1,0:T(8,128)S(1)}, u32[]{:S(2)}, u32[]{:S(2)}) collective-permute-start(f32[256,512]{1,0:T(8,128)S(1)} %get-tuple-element.26), channel_id=1, source_target_pairs={{0,2},{2,4},{4,6},{6,8},{8,10},{10,12},{12,14},{14,0},{1,3},{3,5},... | collective-permute-start | bytes 1572872 | tf_op jit(solution)/shard_map/ppermute | solution.py:35
  76.4 22.9 %collective-permute-start.12 = (f32[256,512]{1,0:T(8,128)S(1)}, f32[256,512]{1,0:T(8,128)S(1)}, u32[]{:S(2)}, u32[]{:S(2)}) collective-permute-start(f32[256,512]{1,0:T(8,128)S(1)} %get-tuple-element.28), channel_id=1, source_target_pairs={{0,14},{2,0},{4,2},{6,4},{8,6},{10,8},{12,10},{14,12},{1,15},{3,1}... | collective-permute-start | bytes 1572872 | tf_op jit(solution)/shard_map/ppermute | solution.py:35
  91.5 8.1 %collective-permute-start.8 = (f32[8,128,128]{2,1,0:T(8,128)S(1)}, f32[8,128,128]{2,1,0:T(8,128)S(1)}, u32[]{:S(2)}, u32[]{:S(2)}) collective-permute-start(f32[8,128,128]{2,1,0:T(8,128)S(1)} %add.115.refs_1_), channel_id=1, source_target_pairs={{0,16},{16,0},{1,17},{17,1},{2,18},{18,2},{3,19},{19,3},{4,20},{20... | collective-permute-start | bytes 1572872 | tf_op jit(solution)/shard_map/ppermute | solution.py:35
  95.3 8.1 %copy-start.11 = (f32[256,512]{1,0:T(8,128)}, f32[256,512]{1,0:T(8,128)S(1)}, u32[]{:S(2)}) copy-start(f32[256,512]{1,0:T(8,128)S(1)} %collective-permute-done.17.rest_8_) | copy-start | bytes 1572868
  95.3 7.6 %collective-permute-start.7 = (f32[8,128,128]{2,1,0:T(8,128)S(1)}, f32[8,128,128]{2,1,0:T(8,128)S(1)}, u32[]{:S(2)}, u32[]{:S(2)}) collective-permute-start(f32[8,128,128]{2,1,0:T(8,128)S(1)} %add.112.refs_0_), channel_id=1, source_target_pairs={{0,16},{16,0},{1,17},{17,1},{2,18},{18,2},{3,19},{19,3},{4,20},{20... | collective-permute-start | bytes 1572872 | tf_op jit(solution)/shard_map/ppermute | solution.py:35
  95.4 10.1 %copy-start.12 = (f32[256,512]{1,0:T(8,128)}, f32[256,512]{1,0:T(8,128)S(1)}, u32[]{:S(2)}) copy-start(f32[256,512]{1,0:T(8,128)S(1)} %collective-permute-done.16.rest_5_) | copy-start | bytes 1572868
  95.4 10.0 %collective-permute-start.18 = (f32[128,512]{1,0:T(8,128)S(1)}, f32[128,512]{1,0:T(8,128)S(1)}, u32[]{:S(2)}, u32[]{:S(2)}) collective-permute-start(f32[128,512]{1,0:T(8,128)S(1)} %slice.38), channel_id=1, source_target_pairs={{0,2},{2,4},{4,6},{6,8},{8,10},{10,12},{12,14},{14,0},{1,3},{3,5},... | collective-permute-start | bytes 786440 | tf_op jit(solution)/shard_map/ppermute | solution.py:35
  97.7 14.3 %copy-start.13 = (f32[256,512]{1,0:T(8,128)}, f32[256,512]{1,0:T(8,128)S(1)}, u32[]{:S(2)}) copy-start(f32[256,512]{1,0:T(8,128)S(1)} %collective-permute-done.13.rest_8_.rest_12_) | copy-start | bytes 1572868
  97.7 7.8 %collective-permute-start.19 = (f32[128,512]{1,0:T(8,128)S(1)}, f32[128,512]{1,0:T(8,128)S(1)}, u32[]{:S(2)}, u32[]{:S(2)}) collective-permute-start(f32[128,512]{1,0:T(8,128)S(1)} %slice.39), channel_id=1, source_target_pairs={{0,14},{2,0},{4,2},{6,4},{8,6},{10,8},{12,10},{14,12},{1,15},{3,1}... | collective-permute-start | bytes 786440 | tf_op jit(solution)/shard_map/ppermute | solution.py:35
  99.3 12.7 %copy-start.14 = (f32[256,512]{1,0:T(8,128)}, f32[256,512]{1,0:T(8,128)S(1)}, u32[]{:S(2)}) copy-start(f32[256,512]{1,0:T(8,128)S(1)} %collective-permute-done.12.rest_5_.rest_9_) | copy-start | bytes 1572868
  99.3 15.9 %collective-permute-start.14 = (f32[128,512]{1,0:T(8,128)S(1)}, f32[128,512]{1,0:T(8,128)S(1)}, u32[]{:S(2)}, u32[]{:S(2)}) collective-permute-start(f32[128,512]{1,0:T(8,128)S(1)} %slice.34), channel_id=1, source_target_pairs={{0,2},{2,4},{4,6},{6,8},{8,10},{10,12},{12,14},{14,0},{1,3},{3,5},... | collective-permute-start | bytes 786440 | tf_op jit(solution)/shard_map/ppermute | solution.py:35
  99.6 15.6 %collective-permute-start.15 = (f32[128,512]{1,0:T(8,128)S(1)}, f32[128,512]{1,0:T(8,128)S(1)}, u32[]{:S(2)}, u32[]{:S(2)}) collective-permute-start(f32[128,512]{1,0:T(8,128)S(1)} %slice.35), channel_id=1, source_target_pairs={{0,14},{2,0},{4,2},{6,4},{8,6},{10,8},{12,10},{14,12},{1,15},{3,1}... | collective-permute-start | bytes 786440 | tf_op jit(solution)/shard_map/ppermute | solution.py:35
  103.4 1.4 copy-start
  104.8 0.6 copy-start.2
  105.4 0.7 copy-start.15
  105.6 0.7 copy-start.16
  112.0 27.8 %collective-permute-start.20 = (f32[256,512]{1,0:T(8,128)}, f32[256,512]{1,0:T(8,128)S(1)}, u32[]{:S(2)}, u32[]{:S(2)}) collective-permute-start(f32[256,512]{1,0:T(8,128)} %beta.5), channel_id=1, source_target_pairs={{0,1},{1,0},{2,3},{3,2},{4,5},{5,4},{6,7},{7,6},{8,9},{9,8},{10,11... | collective-permute-start | bytes 1572872 | tf_op jit(solution)/shard_map/ppermute | solution.py:35
  115.2 0.7 copy-start.17
  115.9 0.7 copy-start.18
  122.4 26.8 %collective-permute-start.21 = (f32[256,512]{1,0:T(8,128)}, f32[256,512]{1,0:T(8,128)S(1)}, u32[]{:S(2)}, u32[]{:S(2)}) collective-permute-start(f32[256,512]{1,0:T(8,128)} %beta.3), channel_id=1, source_target_pairs={{0,1},{1,0},{2,3},{3,2},{4,5},{5,4},{6,7},{7,6},{8,9},{9,8},{10,11... | collective-permute-start | bytes 1572872 | tf_op jit(solution)/shard_map/ppermute | solution.py:35
Sparse Core Ops, SparseCore 0:
  9.2 122.8 all-gather.1
